TPU v7x, 256 devices: a whole 4x4x8 slice. The times are simulated.
256 devices in a mesh: band: 32 (over x, z_hi, y), mem: 8 (over z_lo, core).
Axes of the slice: x: 4, y: 4, z: 8 (z_hi: 2, z_lo: 4; z = z_hi * 4 + z_lo), core: 2. Of those that a mesh axis runs over, the one named last changes fastest.
Arguments:
- state: float32 [32768, 8192], P('band', 'mem'), may hold values from -10 to 10
- obs_anom: bfloat16 [8192, 8192], P('band', 'mem'), may hold values from -8 to 8
- innov: float32 [8192, 8192], P('band', 'mem'), may hold values from -12 to 12
- pattern: int32 [32, 4, 8, 4], P('band'), may hold values 0 or 1
- distance: int32 [32, 4, 8, 4], P('band'), may hold values from 0 to 7
- taper: float32 [8], replicated, may hold values from 0.2 to 1
- order: int32 [32, 4], P('band'), may hold values from 0 to 3, each once within a row
Outputs:
- analysis: float32 [32768, 8192], P('band', 'mem')
Inputs may be any that keep to these rules, and one draw needn't show every extreme that they name: Each row of order lists 0 .. 3 once each.
All inputs are finite; a program needn't handle non-finite values. No bound on the sum of `pattern` on one device may be relied on, other than what follows from the above.
Results may differ from a plain program's by a relative error of at most 0.0028.
Values may be sent and summed in bfloat16 or wider, within the bound.
No kernel may reach another device: no remote copies, remote signals or barrier semaphores. Data moves between devices by JAX's collectives and lax.ppermute only.
A program may use at most 64 MiB of HBM per device.

v0:
```python
import jax
import jax.numpy as jnp
from jax import lax
from jax.sharding import PartitionSpec as P


def from_behind(value, axis, steps):
    count = lax.axis_size(axis)
    pairs = [(source, (source + steps) % count) for source in range(count)]
    return lax.ppermute(value, axis, pairs)


def spread(blocks):
    rows, cols = blocks.shape
    return jnp.broadcast_to(blocks[:, None, :, None], (rows, 128, cols, 64)).reshape(
        rows * 128, cols * 64
    )


def on_device(state, obs_anom, innov, pattern, distance, taper, order):
    members = lax.axis_size("mem") * state.shape[1]
    scale = 1.0 / (members - 1)
    num_obs = obs_anom.shape[0]
    arrivals = order.shape[1]
    gram_part = jnp.dot(obs_anom, obs_anom.T, preferred_element_type=jnp.float32)
    gram = lax.psum(gram_part, "mem")
    spd = gram * scale + jnp.eye(num_obs, dtype=jnp.float32)
    factor = jnp.linalg.cholesky(spd)
    weights_own = jax.scipy.linalg.cho_solve((factor, True), innov).astype(jnp.bfloat16)
    own_batch = jnp.stack([obs_anom, weights_own])
    batches = [own_batch]
    current = own_batch
    for offset in range(1, arrivals):
        current = from_behind(current, "band", 1)
        batches.append(current)
    stacked = jnp.stack(batches)
    onehot = (distance[0][..., None] == jnp.arange(taper.shape[0], dtype=jnp.int32)).astype(
        jnp.float32
    )
    local = pattern[0].astype(jnp.float32) * jnp.sum(onehot * taper, axis=-1)
    field = state
    for step in range(arrivals):
        offset = order[0, step]
        chosen = lax.dynamic_index_in_dim(stacked, offset, 0, keepdims=False)
        y_batch = chosen[0].astype(jnp.float32)
        w_batch = chosen[1].astype(jnp.float32)
        blocks = lax.dynamic_index_in_dim(local, offset, 0, keepdims=False)
        cross_part = jnp.dot(field, y_batch.T, precision=lax.Precision.HIGHEST)
        cross = lax.psum(cross_part, "mem")
        field = field + jnp.dot(
            cross * scale * spread(blocks), w_batch, precision=lax.Precision.HIGHEST
        )
    return field


def solution(mesh):
    return jax.shard_map(
        on_device,
        mesh=mesh,
        in_specs=(
            P("band", "mem"),
            P("band", "mem"),
            P("band", "mem"),
            P("band", None, None, None),
            P("band", None, None, None),
            P(),
            P("band", None),
        ),
        out_specs=P("band", "mem"),
        check_vma=False,
    )
```

profile of v0, /device:TPU:1, one launch (start us, length us, event | category | flops | bytes accessed | tf_op | source)
XLA Modules:
  0.0 639.9 jit_solution(768353029783687942)
XLA Ops:
  6.5 2.3 fusion.45
  9.0 72.7 %all-reduce.7.cloned.1.call-done = f32[256,256]{0,1:T(8,128)} async-done(((f32[256,256]{0,1:T(8,128)}), f32[256,256]{0,1:T(8,128)}) %all-reduce.7.cloned.1.call-update) | async-done | bytes 262160 | tf_op jit(solution)/shard_map/psum | solution.py:26
  83.8 11.7 %cholesky.50 = f32[128,128]{1,0:T(8,128)S(1)} custom-call(f32[128,128]{1,0:T(8,128)S(1)} %cholesky.118), custom_call_target="Cholesky" | custom-call | tf_op jit(solution)/shard_map/jit(cholesky)/cholesky | solution.py:28
  95.5 9.8 %custom-call.18 = f32[1,128,128]{1,2,0:T(8,128)S(1)} custom-call(f32[1,128,128]{2,1,0:T(8,128)S(1)} %get-tuple-element.28), custom_call_target="InvertDiagBlocksLowerTriangular" | custom-call | tf_op jit(solution)/shard_map/jit(cholesky)/cholesky | solution.py:28
  105.9 11.7 %cholesky.105 = f32[128,128]{1,0:T(8,128)S(1)} custom-call(f32[128,128]{1,0:T(8,128)S(1)} %convolution_subtract_fusion.2), custom_call_target="Cholesky" | custom-call | tf_op jit(solution)/shard_map/jit(cholesky)/cholesky | solution.py:28
  119.8 4.5 while.1
  124.3 19.7 %custom-call.19 = f32[2,128,128]{1,2,0:T(8,128)S(1)} custom-call(f32[2,128,128]{2,1,0:T(8,128)S(1)} %get-tuple-element.12), custom_call_target="InvertDiagBlocksLowerTriangular" | custom-call | tf_op jit(solution)/shard_map/jit(_cho_solve)/triangular_solve | solution.py:29
  149.2 53.2 %collective-permute-done = bf16[2,256,1024]{2,1,0:T(8,128)(2,1)S(1)} collective-permute-done((bf16[2,256,1024]{2,1,0:T(8,128)(2,1)S(1)}, bf16[2,256,1024]{2,1,0:T(8,128)(2,1)S(1)}, u32[]{:S(2)}, u32[]{:S(2)}) %collective-permute-start) | collective-permute-done | bytes 1048608 | tf_op jit(solution)/shard_map/ppermute | solution.py:10
  202.3 50.1 %collective-permute-done.1 = bf16[2,256,1024]{2,1,0:T(8,128)(2,1)} collective-permute-done((bf16[2,256,1024]{2,1,0:T(8,128)(2,1)S(1)}, bf16[2,256,1024]{2,1,0:T(8,128)(2,1)}, u32[]{:S(2)}, u32[]{:S(2)}) %collective-permute-start.1) | collective-permute-done | bytes 1048608 | tf_op jit(solution)/shard_map/ppermute | solution.py:10
  255.1 43.7 %collective-permute-done.2 = bf16[2,256,1024]{2,1,0:T(8,128)(2,1)} collective-permute-done((bf16[2,256,1024]{2,1,0:T(8,128)(2,1)}, bf16[2,256,1024]{2,1,0:T(8,128)(2,1)}, u32[]{:S(2)}, u32[]{:S(2)}) %collective-permute-start.2) | collective-permute-done | bytes 1048608 | tf_op jit(solution)/shard_map/ppermute | solution.py:10
  302.7 3.2 convolution_bitcast_fusion
  312.2 60.7 %all-reduce.9.cloned.1.call-done = f32[1024,256]{0,1:T(8,128)} async-done(((f32[1024,256]{0,1:T(8,128)}), f32[1024,256]{0,1:T(8,128)}) %all-reduce.9.cloned.1.call-update) | async-done | bytes 1048592 | tf_op jit(solution)/shard_map/psum | solution.py:49
  373.0 4.9 convolution_add_fusion.3
  377.9 2.0 copy-done.2
  379.9 4.3 fusion.11
  384.3 73.1 %all-reduce.11.cloned.1.call-done = f32[1024,256]{0,1:T(8,128)} async-done(((f32[1024,256]{0,1:T(8,128)}), f32[1024,256]{0,1:T(8,128)}) %all-reduce.11.cloned.1.call-update) | async-done | bytes 1048592 | tf_op jit(solution)/shard_map/psum | solution.py:49
  457.5 4.9 convolution_add_fusion.2
  462.4 2.0 copy-done.1
  464.4 4.2 fusion.10
  468.9 73.0 %all-reduce.13.cloned.1.call-done = f32[1024,256]{0,1:T(8,128)} async-done(((f32[1024,256]{0,1:T(8,128)}), f32[1024,256]{0,1:T(8,128)}) %all-reduce.13.cloned.1.call-update) | async-done | bytes 1048592 | tf_op jit(solution)/shard_map/psum | solution.py:49
  542.0 4.9 convolution_add_fusion.1
  548.9 4.3 fusion.9
  553.2 73.1 %all-reduce.15.cloned.1.call-done = f32[1024,256]{0,1:T(8,128)} async-done(((f32[1024,256]{0,1:T(8,128)}), f32[1024,256]{0,1:T(8,128)}) %all-reduce.15.cloned.1.call-update) | async-done | bytes 1048592 | tf_op jit(solution)/shard_map/psum | solution.py:49
  626.5 6.7 %convolution_add_fusion = f32[1024,1024]{1,0:T(8,128)} fusion(f32[1024,1024]{1,0:T(8,128)} %copy-done, f32[32,8,8,128]{3,2,1,0:T(8,128)S(1)} %bitcast.122, f32[1024,256]{0,1:T(8,128)} %all-reduce.15.cloned.1.call-done, bf16[4,2,256,1024]{3,2,1,0:T(8,128)(2,1)} %copy-done.3, s32[]{:T(128)S(6)} %select_n.26, s32[]{:T(128)S(6)} %add.80), kind=kOutput, calls=%fused_computation.3 | convolution fusion | flops 3222798336 | bytes 11010056 | tf_op jit(solution)/shard_map/dot_general | solution.py:50
  (70 shorter events, 20.6 us)
Async XLA Ops:
  6.5 137.4 %copy-start.6 = (f32[256,1024]{1,0:T(8,128)S(1)}, f32[256,1024]{1,0:T(8,128)}, u32[]{:S(2)}) copy-start(f32[256,1024]{1,0:T(8,128)} %param.9) | copy-start | bytes 3145732
  6.5 75.1 %all-reduce.7.cloned.1.call-start = ((), (), s32[]{:S(2)}) async-start(), calls=%async_computation | async-start | bytes 524288 | tf_op jit(solution)/shard_map/psum | solution.py:26
  8.9 364.0 %all-reduce.9.cloned.1.call-start = ((), (), s32[]{:S(2)}) async-start(), calls=%async_computation.1 | async-start | bytes 2097152 | tf_op jit(solution)/shard_map/psum | solution.py:49
  124.3 23.4 %copy-start.5 = (bf16[256,1024]{1,0:T(8,128)(2,1)S(1)}, bf16[256,1024]{1,0:T(8,128)(2,1)}, u32[]{:S(2)}) copy-start(bf16[256,1024]{1,0:T(8,128)(2,1)} %param.8) | copy-start | bytes 1572868
  145.2 107.2 %copy-start.9 = (s32[1,4]{1,0:T(1,128)S(1)}, s32[1,4]{1,0:T(1,128)}, u32[]{:S(2)}) copy-start(s32[1,4]{1,0:T(1,128)} %param.13) | copy-start | bytes 52
  147.9 54.4 %collective-permute-start = (bf16[2,256,1024]{2,1,0:T(8,128)(2,1)S(1)}, bf16[2,256,1024]{2,1,0:T(8,128)(2,1)S(1)}, u32[]{:S(2)}, u32[]{:S(2)}) collective-permute-start(bf16[2,256,1024]{2,1,0:T(8,128)(2,1)S(1)} %get-tuple-element.24), channel_id=1, source_target_pairs={{0,8},{8,16},{16,24},{24,32},{32,40},{40,48},{48,56},{56,64},{64,7... | collective-permute-start | bytes 3145736 | tf_op jit(solution)/shard_map/ppermute | solution.py:10
  202.3 50.1 %collective-permute-start.1 = (bf16[2,256,1024]{2,1,0:T(8,128)(2,1)S(1)}, bf16[2,256,1024]{2,1,0:T(8,128)(2,1)}, u32[]{:S(2)}, u32[]{:S(2)}) collective-permute-start(bf16[2,256,1024]{2,1,0:T(8,128)(2,1)S(1)} %collective-permute-done), channel_id=1, source_target_pairs={{0,8},{8,16},{16,24},{24,32},{32,40},{40,48},{48,56},{56,64},{64,7... | collective-permute-start | bytes 3145736 | tf_op jit(solution)/shard_map/ppermute | solution.py:10
  252.4 46.4 %collective-permute-start.2 = (bf16[2,256,1024]{2,1,0:T(8,128)(2,1)}, bf16[2,256,1024]{2,1,0:T(8,128)(2,1)}, u32[]{:S(2)}, u32[]{:S(2)}) collective-permute-start(bf16[2,256,1024]{2,1,0:T(8,128)(2,1)} %collective-permute-done.1), channel_id=1, source_target_pairs={{0,8},{8,16},{16,24},{24,32},{32,40},{40,48},{48,56},{56,64},{64,7... | collective-permute-start | bytes 3145736 | tf_op jit(solution)/shard_map/ppermute | solution.py:10
  298.8 3.9 copy-start.4
  300.8 1.9 copy-start.3
  302.7 9.2 %copy-start.8 = (s32[1,4,8,4]{2,3,1,0:T(4,128)S(1)}, s32[1,4,8,4]{2,3,1,0:T(4,128)}, u32[]{:S(2)}) copy-start(s32[1,4,8,4]{2,3,1,0:T(4,128)} %param.11) | copy-start | bytes 1540
  302.7 9.2 %copy-start.10 = (f32[8]{0:T(128)S(1)}, f32[8]{0:T(128)}, u32[]{:S(2)}) copy-start(f32[8]{0:T(128)} %param.12) | copy-start | bytes 100
  302.7 9.4 %copy-start.7 = (s32[1,4,8,4]{2,3,1,0:T(4,128)S(1)}, s32[1,4,8,4]{2,3,1,0:T(4,128)}, u32[]{:S(2)}) copy-start(s32[1,4,8,4]{2,3,1,0:T(4,128)} %param.10) | copy-start | bytes 1540
  305.9 151.4 %all-reduce.11.cloned.1.call-start = ((), (), s32[]{:S(2)}) async-start(), calls=%async_computation.2 | async-start | bytes 2097152 | tf_op jit(solution)/shard_map/psum | solution.py:49
  377.9 2.0 copy-start.2
  384.2 157.7 %all-reduce.13.cloned.1.call-start = ((), (), s32[]{:S(2)}) async-start(), calls=%async_computation.3 | async-start | bytes 2097152 | tf_op jit(solution)/shard_map/psum | solution.py:49
  462.4 2.0 copy-start.1
  468.7 157.7 %all-reduce.15.cloned.1.call-start = ((), (), s32[]{:S(2)}) async-start(), calls=%async_computation.4 | async-start | bytes 2097152 | tf_op jit(solution)/shard_map/psum | solution.py:49
  546.9 2.0 copy-start
Sparse Core Ops, SparseCore 0:
  10.0 71.6 all-reduce.6
  306.0 66.8 all-reduce.8
  384.3 72.9 all-reduce.10
  468.8 73.0 all-reduce.12
  553.3 72.9 all-reduce.14
where the time goes:
time: 649 us; the launch traced here: 640 us
  waiting for transfers between devices  500 us (77%)
  other arithmetic  58 us (9%)
  matrix products  43.7 us (7%)
  between operations  22.8 us (4%)
  local copies, waits for them, and re-layouts  13.5 us (2%)
    psum x4, waiting for transfers between devices, on_device(): cross = lax.psum(cross_part, 'mem')  280 us
    ppermute x3, waiting for transfers between devices, from_behind(): return lax.ppermute(value, axis, pairs)  147 us
    psum x1, waiting for transfers between devices, on_device(): gram = lax.psum(gram_part, 'mem')  72.7 us
    another operation x6, other arithmetic, on_device(): factor = jnp.linalg.cholesky(spd)  34 us
    dot_general x4, matrix products, on_device(): jnp.dot(cross * scale * spread(blocks), w_batch, precision=lax.Precision....  21.4 us
    another operation x4, other arithmetic, on_device(): jax.scipy.linalg.cho_solve((factor, True), innov).astype(jnp.bfloat16)  19.7 us
    dot_general x4, matrix products, on_device(): cross_part = jnp.dot(field, y_batch.T, precision=lax.Precision.HIGHEST)  15.9 us
  transfers between devices with their start and end apart: 8, of which 8 were waited for; matrix products, arithmetic and copies ran while one was open for 0% of the time, Pallas kernels for 0%

commit v1 on v0

v1 whole, which is shorter than its diff:
```python
import jax
import jax.numpy as jnp
from jax import lax
from jax.experimental import pallas as pl
from jax.experimental.pallas import tpu as pltpu
from jax.sharding import PartitionSpec as P

HIGH = lax.Precision.HIGHEST
BF = jnp.bfloat16
F32 = jnp.float32
RING = 4


def mem_swap(value, bit):
    count = lax.axis_size("mem")
    return lax.ppermute(value, "mem", [(m, m ^ bit) for m in range(count)])


def band_send(value, pairs):
    return lax.ppermute(value, "band", pairs)


def fetch_batches(own):
    bands = lax.axis_size("band")
    y = lax.axis_index("band") % RING
    ahead = [
        band_send(own, [(s, s + r) for s in range(bands) if s % RING + r < RING])
        for r in range(1, RING)
    ]
    prev = band_send(own, [(s, (s + RING) % bands) for s in range(bands) if s % RING])
    wrapped = [
        band_send(prev, [(s, s + r - RING) for s in range(bands) if s % RING + r >= RING])
        for r in range(1, RING)
    ]
    return [jnp.where(y >= r, ahead[r - 1], wrapped[r - 1]) for r in range(1, RING)]


def dot(a, b, dims, precision=None):
    return lax.dot_general(a, b, (dims, ((), ())), precision=precision, preferred_element_type=F32)


def sum_scatter(part, z, core):
    keep = lax.dynamic_index_in_dim(part, core, 0, keepdims=False)
    give = lax.dynamic_index_in_dim(part, 1 - core, 0, keepdims=False)
    chip = keep + mem_swap(give.astype(BF), 1).astype(F32)
    total = lax.dynamic_index_in_dim(chip, z, 0, keepdims=False)
    chip16 = chip.astype(BF)
    for d in range(1, 4):
        block = lax.dynamic_index_in_dim(chip16, z ^ d, 0, keepdims=False)
        total = total + mem_swap(block, 2 * d).astype(F32)
    return total


def gather(block, z, core):
    line = jnp.stack([block] + [mem_swap(block, 2 * d) for d in range(1, 4)])
    half = jnp.stack([lax.dynamic_index_in_dim(line, z ^ k, 0, keepdims=False) for k in range(4)])
    other = mem_swap(half, 1)
    return jnp.where(core == 0, jnp.stack([half, other]), jnp.stack([other, half]))


def sum_all_f32(part, z, core):
    rows = part.shape[0] // 2
    halves = part.reshape(2, rows, part.shape[1])
    keep = lax.dynamic_index_in_dim(halves, core, 0, keepdims=False)
    give = lax.dynamic_index_in_dim(halves, 1 - core, 0, keepdims=False)
    half = keep + mem_swap(give, 1)
    total = half
    for d in range(1, 4):
        total = total + mem_swap(half, 2 * d)
    other = mem_swap(total, 1)
    return jnp.where(
        core == 0, jnp.concatenate([total, other]), jnp.concatenate([other, total])
    )


def weigh_kernel(scale, gram_ref, innov_ref, out_ref, x_ref, r_ref):
    n = gram_ref.shape[0]
    rows = lax.broadcasted_iota(jnp.int32, (n, n), 0)
    cols = lax.broadcasted_iota(jnp.int32, (n, n), 1)
    eye = jnp.where(rows == cols, 1.0, 0.0).astype(F32)
    a = gram_ref[...] * scale + eye
    most = jnp.max(jnp.sum(jnp.abs(a), axis=1, keepdims=True)) * 1.0001
    start = 2.0 / (1.0 + most)
    rho = (most - 1.0) / (most + 1.0)
    x_ref[...] = eye * start
    r_ref[...] = eye - a * start

    def unfinished(rho):
        return rho > 2e-3

    def improve(rho):
        square = rho * rho
        grow = 2.0 / (2.0 - square)
        x = x_ref[...]
        x = (x + jnp.dot(x, r_ref[...], precision=HIGH, preferred_element_type=F32)) * grow
        x_ref[...] = x
        r_ref[...] = eye - jnp.dot(a, x, precision=HIGH, preferred_element_type=F32)
        return square / (2.0 - square)

    lax.while_loop(unfinished, improve, rho)
    x = x_ref[...]
    x = x + jnp.dot(x, r_ref[...], precision=HIGH, preferred_element_type=F32)
    out_ref[...] = jnp.dot(
        x, innov_ref[...], precision=HIGH, preferred_element_type=F32
    ).astype(BF)


def weigh(gram, innov, scale):
    n, width = innov.shape
    return pl.pallas_call(
        lambda *refs: weigh_kernel(scale, *refs),
        out_shape=jax.ShapeDtypeStruct((n, width), BF),
        in_specs=[pl.BlockSpec(memory_space=pltpu.VMEM)] * 2,
        out_specs=pl.BlockSpec(memory_space=pltpu.VMEM),
        scratch_shapes=[pltpu.VMEM((n, n), F32)] * 2,
        name="weigh",
    )(gram, innov)


def on_device(state, obs_anom, innov, pattern, distance, taper, order):
    members = lax.axis_size("mem") * state.shape[1]
    scale = 1.0 / (members - 1)
    cells, width = state.shape
    num_obs = obs_anom.shape[0]
    arrivals = order.shape[1]
    mem = lax.axis_index("mem")
    z, core = mem // 2, mem % 2
    mine = core * 4 + z
    rows = cells // 8

    gram = sum_all_f32(dot(obs_anom, obs_anom, ((1,), (1,))), z, core)
    y_all = jnp.stack([obs_anom] + fetch_batches(obs_anom))
    weights = weigh(gram, innov, scale)
    w_all = jnp.stack([weights] + fetch_batches(weights))

    state16 = state.astype(BF)
    cross_part = jnp.concatenate(
        [dot(state16, y_all[a], ((1,), (1,))) for a in range(arrivals)], axis=1
    )
    cross = sum_scatter(cross_part.reshape(2, 4, rows, arrivals * num_obs), z, core)
    cross = cross.reshape(rows, arrivals, num_obs)

    first = [lax.dynamic_index_in_dim(w_all, order[0, t], 0, keepdims=False) for t in range(arrivals)]
    later = [lax.dynamic_index_in_dim(y_all, order[0, t], 0, keepdims=False) for t in range(arrivals)]
    pairs = [(t, s) for t in range(arrivals) for s in range(t + 1, arrivals)]
    link_part = jnp.concatenate(
        [dot(first[t], later[s], ((1,), (1,))) for t, s in pairs], axis=0
    )
    link_rows = link_part.shape[0] // 8
    link = gather(
        sum_scatter(link_part.reshape(2, 4, link_rows, num_obs), z, core).astype(BF), z, core
    ).reshape(len(pairs), num_obs, num_obs)

    onehot = (distance[0][..., None] == jnp.arange(taper.shape[0], dtype=jnp.int32)).astype(F32)
    local = pattern[0].astype(F32) * jnp.sum(onehot * taper, axis=-1)
    local = lax.dynamic_index_in_dim(local, mine, 1, keepdims=False) * scale
    span = num_obs // local.shape[1]
    coefs = []
    for s in range(arrivals):
        value = lax.dynamic_index_in_dim(cross, order[0, s], 1, keepdims=False)
        for t in range(s):
            value = value + dot(coefs[t], link[pairs.index((t, s))], ((1,), (0,)))
        factor = lax.dynamic_index_in_dim(local, order[0, s], 0, keepdims=False)
        factor = jnp.broadcast_to(factor[:, None], (factor.shape[0], span)).reshape(1, num_obs)
        coefs.append((value * factor).astype(BF))
    all_coefs = gather(jnp.concatenate(coefs, axis=1), z, core)
    w_cat = jnp.concatenate(first, axis=0)
    return state + dot(all_coefs.reshape(cells, arrivals * num_obs), w_cat, ((1,), (0,)))


def solution(mesh):
    return jax.shard_map(
        on_device,
        mesh=mesh,
        in_specs=(
            P("band", "mem"),
            P("band", "mem"),
            P("band", "mem"),
            P("band", None, None, None),
            P("band", None, None, None),
            P(),
            P("band", None),
        ),
        out_specs=P("band", "mem"),
        check_vma=False,
    )
```

time: 649 us -> 237 us (0.37); the launches traced: 640 us -> 235 us
  waiting for transfers between devices: 500 us -> 50.7 us
  starting transfers between devices: 1.84 us -> 115 us
  other arithmetic: 58 us -> 17.1 us
  matrix products: 43.7 us -> 15.1 us
  between operations: 22.8 us -> 7.85 us
  Pallas kernels: 0 us -> 9.09 us
    psum x5 -> x0, waiting for transfers between devices: 353 us -> none  [the longest x4 280 us: on_device(): cross = lax.psum(cross_part, 'mem')]
    ppermute x3 -> x35, starting transfers between devices: 1.29 us -> 115 us  [the longest x14 60.8 us: band_send(): return lax.ppermute(value, 'band', pairs)]
    ppermute x3 -> x35, waiting for transfers between devices: 147 us -> 50.7 us  [the longest x21 37 us: mem_swap(): return lax.ppermute(value, 'mem', [(m, m ^ bit) for m in range(count)])]
    another operation x12 -> x13, other arithmetic: 55.9 us -> 6.64 us  [the longest x4 3.58 us: on_device(): w_all = jnp.stack([weights] + fetch_batches(weights))]
    dot_general x9 -> x18, matrix products: 39.6 us -> 15.1 us  [dot(): lax.dot_general(a, b, (dims, ((), ())), precision=precision, preferred_el...]
    pallas_call x0 -> x1, Pallas kernels: none -> 9.09 us  [weigh(): pl.pallas_call(lambda *refs: weigh_kernel(scale, *refs), out_shape=jax.Sh...]
    dynamic_slice x0 -> x10, local copies, waits for them, and re-layouts: none -> 7.6 us  [the longest x2 4.96 us: sum_scatter(): keep = lax.dynamic_index_in_dim(part, core, 0, keepdims=False)]
  transfers between devices with their start and end apart: 8 -> 35, of which waited for: 8 -> 11; matrix products, arithmetic and copies ran while one was open for 0% -> 18% of each run, Pallas kernels for 0% -> 4%
where the time goes in v1:
time: 237 us; the launch traced here: 235 us
  starting transfers between devices  115 us (49%)
  waiting for transfers between devices  50.7 us (21%)
  local copies, waits for them, and re-layouts  19.9 us (8%)
  other arithmetic  17.1 us (7%)
  matrix products  15.1 us (6%)
  Pallas kernels  9.09 us (4%)
  between operations  7.85 us (3%)
    ppermute x14, starting transfers between devices, band_send(): return lax.ppermute(value, 'band', pairs)  60.8 us
    ppermute x21, starting transfers between devices, mem_swap(): return lax.ppermute(value, 'mem', [(m, m ^ bit) for m in range(count)])  54 us
    ppermute x21, waiting for transfers between devices, mem_swap(): return lax.ppermute(value, 'mem', [(m, m ^ bit) for m in range(count)])  37 us
    dot_general x18, matrix products, dot(): lax.dot_general(a, b, (dims, ((), ())), precision=precision, preferred_el...  15.1 us
    ppermute x14, waiting for transfers between devices, band_send(): return lax.ppermute(value, 'band', pairs)  13.7 us
    pallas_call x1, Pallas kernels, weigh(): pl.pallas_call(lambda *refs: weigh_kernel(scale, *refs), out_shape=jax.Sh...  9.09 us
    reshape x1, local copies, waits for them, and re-layouts, on_device(): cross_part.reshape(2, 4, rows, arrivals * num_obs)  5.62 us
    dynamic_slice x2, local copies, waits for them, and re-layouts, sum_scatter(): keep = lax.dynamic_index_in_dim(part, core, 0, keepdims=False)  4.96 us
  transfers between devices with their start and end apart: 35, of which 11 were waited for; matrix products, arithmetic and copies ran while one was open for 18% of the time, Pallas kernels for 4%

profile of v1, /device:TPU:1, one launch (start us, length us, event | category | flops | bytes accessed | tf_op | source)
XLA Modules:
  0.0 234.7 jit_solution(14156843415938481619)
XLA Ops:
  1.6 3.3 %collective-permute-start.11 = (f32[128,256]{1,0:T(8,128)S(1)}, f32[128,256]{1,0:T(8,128)S(1)}, u32[]{:S(2)}, u32[]{:S(2)}) collective-permute-start(f32[128,256]{1,0:T(8,128)S(1)} %dynamic-slice_bitcast_fusion.7), channel_id=1, source_target_pairs={{0,1},{1,0},{2,3},{3,2},{4,5},{5,4},{6,7},{7,6},{8,9},{9,8},{10,11... | collective-permute-start | bytes 393224 | tf_op jit(solution)/shard_map/ppermute | solution.py:16
  6.5 2.9 %collective-permute-start.13 = (f32[128,256]{1,0:T(8,128)S(1)}, f32[128,256]{1,0:T(8,128)S(1)}, u32[]{:S(2)}, u32[]{:S(2)}) collective-permute-start(f32[128,256]{1,0:T(8,128)S(1)} %bitcast_add_fusion.4), channel_id=1, source_target_pairs={{0,4},{1,5},{2,6},{3,7},{4,0},{5,1},{6,2},{7,3},{8,12},{9,13},{10,... | collective-permute-start | bytes 393224 | tf_op jit(solution)/shard_map/ppermute | solution.py:16
  10.0 8.9 %collective-permute-start = (bf16[256,1024]{1,0:T(8,128)(2,1)}, bf16[256,1024]{1,0:T(8,128)(2,1)S(1)}, u32[]{:S(2)}, u32[]{:S(2)}) collective-permute-start(bf16[256,1024]{1,0:T(8,128)(2,1)} %param.8), channel_id=1, source_target_pairs={{0,8},{8,16},{16,24},{32,40},{40,48},{48,56},{64,72},{72,80},{80,8... | collective-permute-start | bytes 1572872 | tf_op jit(solution)/shard_map/ppermute | solution.py:20
  21.4 26.1 %collective-permute-start.3 = (bf16[256,1024]{1,0:T(8,128)(2,1)S(1)}, bf16[256,1024]{1,0:T(8,128)(2,1)}, u32[]{:S(2)}, u32[]{:S(2)}) collective-permute-start(bf16[256,1024]{1,0:T(8,128)(2,1)S(1)} %copy-done), channel_id=1, source_target_pairs={{0,16},{8,24},{32,48},{40,56},{64,80},{72,88},{96,112},{104,120},{... | collective-permute-start | bytes 1572872 | tf_op jit(solution)/shard_map/ppermute | solution.py:20
  60.9 7.8 %collective-permute-start.5 = (bf16[256,1024]{1,0:T(8,128)(2,1)S(1)}, bf16[256,1024]{1,0:T(8,128)(2,1)}, u32[]{:S(2)}, u32[]{:S(2)}) collective-permute-start(bf16[256,1024]{1,0:T(8,128)(2,1)S(1)} %copy-done), channel_id=1, source_target_pairs={{0,24},{32,56},{64,88},{96,120},{128,152},{160,184},{192,216},{224... | collective-permute-start | bytes 1572872 | tf_op jit(solution)/shard_map/ppermute | solution.py:20
  69.4 9.1 %weigh.1 = bf16[256,1024]{1,0:T(8,128)(2,1)} custom-call(f32[256,256]{1,0:T(8,128)} %maximum_select_fusion.2.refs_0_, f32[256,1024]{1,0:T(8,128)} %refs_1_.1), custom_call_target="tpu_custom_call" | custom-call | tf_op jit(solution)/shard_map/weigh/pallas_call | solution.py:110
  83.0 2.8 %collective-permute-start.21 = (bf16[256,1024]{1,0:T(8,128)(2,1)}, bf16[256,1024]{1,0:T(8,128)(2,1)}, u32[]{:S(2)}, u32[]{:S(2)}) collective-permute-start(bf16[256,1024]{1,0:T(8,128)(2,1)} %weigh.1), channel_id=1, source_target_pairs={{0,24},{32,56},{64,88},{96,120},{128,152},{160,184},{192,216},{224... | collective-permute-start | bytes 1572872 | tf_op jit(solution)/shard_map/ppermute | solution.py:20
  89.8 2.6 %collective-permute-start.16 = (bf16[256,1024]{1,0:T(8,128)(2,1)}, bf16[256,1024]{1,0:T(8,128)(2,1)}, u32[]{:S(2)}, u32[]{:S(2)}) collective-permute-start(bf16[256,1024]{1,0:T(8,128)(2,1)} %weigh.1), channel_id=1, source_target_pairs={{0,8},{8,16},{16,24},{32,40},{40,48},{48,56},{64,72},{72,80},{80,8... | collective-permute-start | bytes 1572872 | tf_op jit(solution)/shard_map/ppermute | solution.py:20
  97.0 2.6 %pad_maximum_fusion = f32[1024,1024]{0,1:T(8,128)} fusion(f32[1024,256]{0,1:T(8,128)S(1)} %convolution_bitcast_fusion, f32[1024,256]{0,1:T(8,128)S(1)} %convolution_bitcast_fusion.1, f32[1024,256]{0,1:T(8,128)S(1)} %convolution_bitcast_fusion.2, f32[1024,256]{0,1:T(8,128)S(1)} %copy-done.1), kind=kLoop, calls=%fused_computation | loop fusion | flops 3145728 | bytes 8388608 | tf_op jit(solution)/shard_map/concatenate | solution.py:137
  99.6 5.6 %reshape.77 = f32[2,4,128,1024]{2,1,0,3:T(4,128)} reshape(f32[1024,1024]{0,1:T(8,128)} %pad_maximum_fusion) | data formatting | bytes 8388608 | tf_op jit(solution)/shard_map/reshape | solution.py:140
  112.7 3.0 %collective-permute-done.22 = bf16[256,1024]{1,0:T(8,128)(2,1)} collective-permute-done((bf16[256,1024]{1,0:T(8,128)(2,1)}, bf16[256,1024]{1,0:T(8,128)(2,1)}, u32[]{:S(2)}, u32[]{:S(2)}) %collective-permute-start.22) | collective-permute-done | bytes 524320 | tf_op jit(solution)/shard_map/ppermute | solution.py:20
  115.7 3.3 %collective-permute-start.7 = (bf16[4,128,1024]{2,1,0:T(8,128)(2,1)}, bf16[4,128,1024]{2,1,0:T(8,128)(2,1)}, u32[]{:S(2)}, u32[]{:S(2)}) collective-permute-start(bf16[4,128,1024]{2,1,0:T(8,128)(2,1)} %bitcast.140), channel_id=1, source_target_pairs={{0,1},{1,0},{2,3},{3,2},{4,5},{5,4},{6,7},{7,6},{8,9},{9,8},{10,11... | collective-permute-start | bytes 3145736 | tf_op jit(solution)/shard_map/ppermute | solution.py:16
  121.2 9.4 %collective-permute-done.18 = bf16[256,1024]{1,0:T(8,128)(2,1)S(1)} collective-permute-done((bf16[256,1024]{1,0:T(8,128)(2,1)}, bf16[256,1024]{1,0:T(8,128)(2,1)S(1)}, u32[]{:S(2)}, u32[]{:S(2)}) %collective-permute-start.18) | collective-permute-done | bytes 524320 | tf_op jit(solution)/shard_map/ppermute | solution.py:20
  135.2 9.6 %collective-permute-start.23 = (bf16[4,192,256]{2,1,0:T(8,128)(2,1)S(1)}, bf16[4,192,256]{2,1,0:T(8,128)(2,1)S(1)}, u32[]{:S(2)}, u32[]{:S(2)}) collective-permute-start(bf16[4,192,256]{2,1,0:T(8,128)(2,1)S(1)} %fusion.31), channel_id=1, source_target_pairs={{0,1},{1,0},{2,3},{3,2},{4,5},{5,4},{6,7},{7,6},{8,9},{9,8},{10,11... | collective-permute-start | bytes 1179656 | tf_op jit(solution)/shard_map/ppermute | solution.py:16
  147.8 5.5 %collective-permute-start.24 = (bf16[192,256]{1,0:T(8,128)(2,1)}, bf16[192,256]{1,0:T(8,128)(2,1)S(1)}, u32[]{:S(2)}, u32[]{:S(2)}) collective-permute-start(bf16[192,256]{1,0:T(8,128)(2,1)} %get-tuple-element.39), channel_id=1, source_target_pairs={{0,2},{1,3},{2,0},{3,1},{4,6},{5,7},{6,4},{7,5},{8,10},{9,11},{10,... | collective-permute-start | bytes 294920 | tf_op jit(solution)/shard_map/ppermute | solution.py:16
  155.9 3.0 %constant_dynamic-slice_fusion.19 = f32[1,4,128,1024]{2,1,0,3:T(4,128)} fusion(f32[2,4,128,1024]{2,1,0,3:T(4,128)} %reshape.77, s32[]{:T(128)S(6)} %select_n.161), kind=kLoop, calls=%fused_computation.124 | loop fusion | bytes 4194308 | tf_op jit(solution)/shard_map/jit(dynamic_index_in_dim)/dynamic_slice | solution.py:43
  175.0 8.7 %collective-permute-start.30 = (bf16[4,192,256]{2,1,0:T(8,128)(2,1)S(1)}, bf16[4,192,256]{2,1,0:T(8,128)(2,1)S(1)}, u32[]{:S(2)}, u32[]{:S(2)}) collective-permute-start(bf16[4,192,256]{2,1,0:T(8,128)(2,1)S(1)} %get-tuple-element.34), channel_id=1, source_target_pairs={{0,1},{1,0},{2,3},{3,2},{4,5},{5,4},{6,7},{7,6},{8,9},{9,8},{10,11... | collective-permute-start | bytes 1179656 | tf_op jit(solution)/shard_map/ppermute | solution.py:16
  183.7 4.4 %collective-permute-done.8 = bf16[128,1024]{1,0:T(8,128)(2,1)S(1)} collective-permute-done((bf16[128,1024]{1,0:T(8,128)(2,1)S(1)}, bf16[128,1024]{1,0:T(8,128)(2,1)S(1)}, u32[]{:S(2)}, u32[]{:S(2)}) %collective-permute-start.8) | collective-permute-done | bytes 262176 | tf_op jit(solution)/shard_map/ppermute | solution.py:16
  188.1 11.9 %collective-permute-done.9 = bf16[128,1024]{1,0:T(8,128)(2,1)S(1)} collective-permute-done((bf16[128,1024]{1,0:T(8,128)(2,1)S(1)}, bf16[128,1024]{1,0:T(8,128)(2,1)S(1)}, u32[]{:S(2)}, u32[]{:S(2)}) %collective-permute-start.9) | collective-permute-done | bytes 262176 | tf_op jit(solution)/shard_map/ppermute | solution.py:16
  202.2 2.7 %collective-permute-start.32 = (bf16[128,1024]{1,0:T(8,128)(2,1)S(1)}, bf16[128,1024]{1,0:T(8,128)(2,1)S(1)}, u32[]{:S(2)}, u32[]{:S(2)}) collective-permute-start(bf16[128,1024]{1,0:T(8,128)(2,1)S(1)} %get-tuple-element.43), channel_id=1, source_target_pairs={{0,4},{1,5},{2,6},{3,7},{4,0},{5,1},{6,2},{7,3},{8,12},{9,13},{10,... | collective-permute-start | bytes 786440 | tf_op jit(solution)/shard_map/ppermute | solution.py:16
  205.8 7.9 %collective-permute-done.31 = bf16[128,1024]{1,0:T(8,128)(2,1)S(1)} collective-permute-done((bf16[128,1024]{1,0:T(8,128)(2,1)S(1)}, bf16[128,1024]{1,0:T(8,128)(2,1)S(1)}, u32[]{:S(2)}, u32[]{:S(2)}) %collective-permute-start.31) | collective-permute-done | bytes 262176 | tf_op jit(solution)/shard_map/ppermute | solution.py:16
  213.7 7.5 %collective-permute-done.33 = bf16[128,1024]{1,0:T(8,128)(2,1)S(1)} collective-permute-done((bf16[128,1024]{1,0:T(8,128)(2,1)S(1)}, bf16[128,1024]{1,0:T(8,128)(2,1)S(1)}, u32[]{:S(2)}, u32[]{:S(2)}) %collective-permute-start.33) | collective-permute-done | bytes 262176 | tf_op jit(solution)/shard_map/ppermute | solution.py:16
  221.7 4.1 %collective-permute-start.34 = (bf16[4,128,1024]{2,1,0:T(8,128)(2,1)S(1)}, bf16[4,128,1024]{2,1,0:T(8,128)(2,1)S(1)}, u32[]{:S(2)}, u32[]{:S(2)}) collective-permute-start(bf16[4,128,1024]{2,1,0:T(8,128)(2,1)S(1)} %get-tuple-element.20), channel_id=1, source_target_pairs={{0,1},{1,0},{2,3},{3,2},{4,5},{5,4},{6,7},{7,6},{8,9},{9,8},{10,11... | collective-permute-start | bytes 3145736 | tf_op jit(solution)/shard_map/ppermute | solution.py:16
  230.3 4.3 %fusion.8 = f32[1024,1024]{1,0:T(8,128)} fusion(f32[1024,1024]{1,0:T(8,128)S(1)} %copy-done.2, bf16[1024,1024]{1,0:T(8,128)(2,1)S(1)} %bitcast.171, bf16[256,1024]{1,0:T(8,128)(2,1)S(1)} %copy-done.7, bf16[256,1024]{1,0:T(8,128)(2,1)S(1)} %copy-done.6, bf16[256,1024]{1,0:T(8,128)(2,1)S(1)} %get-tuple-element.17, bf16[256,1024]{1,0:T(8,128)(2,1)S(1)} %get-tuple-element.18), kind=kOutput, calls=%fused_computation.13 | convolution fusion | flops 2156920832 | bytes 12582912 | tf_op jit(solution)/shard_map/dot_general | solution.py:39
  (145 shorter events, 69.6 us)
Async XLA Ops:
  4.9 43.8 %collective-permute-start.1 = (bf16[256,1024]{1,0:T(8,128)(2,1)}, bf16[256,1024]{1,0:T(8,128)(2,1)}, u32[]{:S(2)}, u32[]{:S(2)}) collective-permute-start(bf16[256,1024]{1,0:T(8,128)(2,1)} %param.8), channel_id=1, source_target_pairs={{8,40},{16,48},{24,56},{40,72},{48,80},{56,88},{72,104},{80,112},{... | collective-permute-start | bytes 1572872 | tf_op jit(solution)/shard_map/ppermute | solution.py:20
  6.4 15.0 %collective-permute-start.12 = (f32[128,256]{1,0:T(8,128)S(1)}, f32[128,256]{1,0:T(8,128)S(1)}, u32[]{:S(2)}, u32[]{:S(2)}) collective-permute-start(f32[128,256]{1,0:T(8,128)S(1)} %bitcast_add_fusion.4), channel_id=1, source_target_pairs={{0,2},{1,3},{2,0},{3,1},{4,6},{5,7},{6,4},{7,5},{8,10},{9,11},{10,... | collective-permute-start | bytes 393224 | tf_op jit(solution)/shard_map/ppermute | solution.py:16
  6.5 41.0 %collective-permute-start.13 = (f32[128,256]{1,0:T(8,128)S(1)}, f32[128,256]{1,0:T(8,128)S(1)}, u32[]{:S(2)}, u32[]{:S(2)}) collective-permute-start(f32[128,256]{1,0:T(8,128)S(1)} %bitcast_add_fusion.4), channel_id=1, source_target_pairs={{0,4},{1,5},{2,6},{3,7},{4,0},{5,1},{6,2},{7,3},{8,12},{9,13},{10,... | collective-permute-start | bytes 393224 | tf_op jit(solution)/shard_map/ppermute | solution.py:16
  9.4 38.1 %collective-permute-start.14 = (f32[128,256]{1,0:T(8,128)S(1)}, f32[128,256]{1,0:T(8,128)S(1)}, u32[]{:S(2)}, u32[]{:S(2)}) collective-permute-start(f32[128,256]{1,0:T(8,128)S(1)} %bitcast_add_fusion.4), channel_id=1, source_target_pairs={{0,6},{1,7},{2,4},{3,5},{4,2},{5,3},{6,0},{7,1},{8,14},{9,15},{10,... | collective-permute-start | bytes 393224 | tf_op jit(solution)/shard_map/ppermute | solution.py:16
  10.0 73.0 %collective-permute-start = (bf16[256,1024]{1,0:T(8,128)(2,1)}, bf16[256,1024]{1,0:T(8,128)(2,1)S(1)}, u32[]{:S(2)}, u32[]{:S(2)}) collective-permute-start(bf16[256,1024]{1,0:T(8,128)(2,1)} %param.8), channel_id=1, source_target_pairs={{0,8},{8,16},{16,24},{32,40},{40,48},{48,56},{64,72},{72,80},{80,8... | collective-permute-start | bytes 1572872 | tf_op jit(solution)/shard_map/ppermute | solution.py:20
  21.4 57.0 %collective-permute-start.3 = (bf16[256,1024]{1,0:T(8,128)(2,1)S(1)}, bf16[256,1024]{1,0:T(8,128)(2,1)}, u32[]{:S(2)}, u32[]{:S(2)}) collective-permute-start(bf16[256,1024]{1,0:T(8,128)(2,1)S(1)} %copy-done), channel_id=1, source_target_pairs={{0,16},{8,24},{32,48},{40,56},{64,80},{72,88},{96,112},{104,120},{... | collective-permute-start | bytes 1572872 | tf_op jit(solution)/shard_map/ppermute | solution.py:20
  47.6 13.3 %collective-permute-start.15 = (f32[128,256]{1,0:T(8,128)S(1)}, f32[128,256]{1,0:T(8,128)S(1)}, u32[]{:S(2)}, u32[]{:S(2)}) collective-permute-start(f32[128,256]{1,0:T(8,128)S(1)} %add_add_fusion), channel_id=1, source_target_pairs={{0,1},{1,0},{2,3},{3,2},{4,5},{5,4},{6,7},{7,6},{8,9},{9,8},{10,11... | collective-permute-start | bytes 393224 | tf_op jit(solution)/shard_map/ppermute | solution.py:16
  48.7 31.2 %collective-permute-start.4 = (bf16[256,1024]{1,0:T(8,128)(2,1)}, bf16[256,1024]{1,0:T(8,128)(2,1)}, u32[]{:S(2)}, u32[]{:S(2)}) collective-permute-start(bf16[256,1024]{1,0:T(8,128)(2,1)} %collective-permute-done.1), channel_id=1, source_target_pairs={{16,0},{24,8},{48,32},{56,40},{80,64},{88,72},{112,96},{120,104},{... | collective-permute-start | bytes 1572872 | tf_op jit(solution)/shard_map/ppermute | solution.py:20
  51.7 34.1 %collective-permute-start.2 = (bf16[256,1024]{1,0:T(8,128)(2,1)}, bf16[256,1024]{1,0:T(8,128)(2,1)}, u32[]{:S(2)}, u32[]{:S(2)}) collective-permute-start(bf16[256,1024]{1,0:T(8,128)(2,1)} %collective-permute-done.1), channel_id=1, source_target_pairs={{24,0},{56,32},{88,64},{120,96},{152,128},{184,160},{216,192},{248... | collective-permute-start | bytes 1572872 | tf_op jit(solution)/shard_map/ppermute | solution.py:20
  60.9 28.9 %collective-permute-start.5 = (bf16[256,1024]{1,0:T(8,128)(2,1)S(1)}, bf16[256,1024]{1,0:T(8,128)(2,1)}, u32[]{:S(2)}, u32[]{:S(2)}) collective-permute-start(bf16[256,1024]{1,0:T(8,128)(2,1)S(1)} %copy-done), channel_id=1, source_target_pairs={{0,24},{32,56},{64,88},{96,120},{128,152},{160,184},{192,216},{224... | collective-permute-start | bytes 1572872 | tf_op jit(solution)/shard_map/ppermute | solution.py:20
  78.5 13.9 %collective-permute-start.17 = (bf16[256,1024]{1,0:T(8,128)(2,1)}, bf16[256,1024]{1,0:T(8,128)(2,1)}, u32[]{:S(2)}, u32[]{:S(2)}) collective-permute-start(bf16[256,1024]{1,0:T(8,128)(2,1)} %weigh.1), channel_id=1, source_target_pairs={{8,40},{16,48},{24,56},{40,72},{48,80},{56,88},{72,104},{80,112},{... | collective-permute-start | bytes 1572872 | tf_op jit(solution)/shard_map/ppermute | solution.py:20
  79.9 15.0 %collective-permute-start.6 = (bf16[256,1024]{1,0:T(8,128)(2,1)}, bf16[256,1024]{1,0:T(8,128)(2,1)S(1)}, u32[]{:S(2)}, u32[]{:S(2)}) collective-permute-start(bf16[256,1024]{1,0:T(8,128)(2,1)} %collective-permute-done.1), channel_id=1, source_target_pairs={{8,0},{16,8},{24,16},{40,32},{48,40},{56,48},{72,64},{80,72},{88,8... | collective-permute-start | bytes 1572872 | tf_op jit(solution)/shard_map/ppermute | solution.py:20
  83.0 28.3 %collective-permute-start.21 = (bf16[256,1024]{1,0:T(8,128)(2,1)}, bf16[256,1024]{1,0:T(8,128)(2,1)}, u32[]{:S(2)}, u32[]{:S(2)}) collective-permute-start(bf16[256,1024]{1,0:T(8,128)(2,1)} %weigh.1), channel_id=1, source_target_pairs={{0,24},{32,56},{64,88},{96,120},{128,152},{160,184},{192,216},{224... | collective-permute-start | bytes 1572872 | tf_op jit(solution)/shard_map/ppermute | solution.py:20
  85.9 34.2 %collective-permute-start.19 = (bf16[256,1024]{1,0:T(8,128)(2,1)}, bf16[256,1024]{1,0:T(8,128)(2,1)}, u32[]{:S(2)}, u32[]{:S(2)}) collective-permute-start(bf16[256,1024]{1,0:T(8,128)(2,1)} %weigh.1), channel_id=1, source_target_pairs={{0,16},{8,24},{32,48},{40,56},{64,80},{72,88},{96,112},{104,120},{... | collective-permute-start | bytes 1572872 | tf_op jit(solution)/shard_map/ppermute | solution.py:20
  89.8 31.4 %collective-permute-start.16 = (bf16[256,1024]{1,0:T(8,128)(2,1)}, bf16[256,1024]{1,0:T(8,128)(2,1)}, u32[]{:S(2)}, u32[]{:S(2)}) collective-permute-start(bf16[256,1024]{1,0:T(8,128)(2,1)} %weigh.1), channel_id=1, source_target_pairs={{0,8},{8,16},{16,24},{32,40},{40,48},{48,56},{64,72},{72,80},{80,8... | collective-permute-start | bytes 1572872 | tf_op jit(solution)/shard_map/ppermute | solution.py:20
  92.4 23.3 %collective-permute-start.22 = (bf16[256,1024]{1,0:T(8,128)(2,1)}, bf16[256,1024]{1,0:T(8,128)(2,1)}, u32[]{:S(2)}, u32[]{:S(2)}) collective-permute-start(bf16[256,1024]{1,0:T(8,128)(2,1)} %collective-permute-done.17), channel_id=1, source_target_pairs={{8,0},{16,8},{24,16},{40,32},{48,40},{56,48},{72,64},{80,72},{88,8... | collective-permute-start | bytes 1572872 | tf_op jit(solution)/shard_map/ppermute | solution.py:20
  94.9 25.2 %collective-permute-start.20 = (bf16[256,1024]{1,0:T(8,128)(2,1)}, bf16[256,1024]{1,0:T(8,128)(2,1)}, u32[]{:S(2)}, u32[]{:S(2)}) collective-permute-start(bf16[256,1024]{1,0:T(8,128)(2,1)} %collective-permute-done.17), channel_id=1, source_target_pairs={{16,0},{24,8},{48,32},{56,40},{80,64},{88,72},{112,96},{120,104},{... | collective-permute-start | bytes 1572872 | tf_op jit(solution)/shard_map/ppermute | solution.py:20
  111.4 19.3 %collective-permute-start.18 = (bf16[256,1024]{1,0:T(8,128)(2,1)}, bf16[256,1024]{1,0:T(8,128)(2,1)S(1)}, u32[]{:S(2)}, u32[]{:S(2)}) collective-permute-start(bf16[256,1024]{1,0:T(8,128)(2,1)} %collective-permute-done.17), channel_id=1, source_target_pairs={{24,0},{56,32},{88,64},{120,96},{152,128},{184,160},{216,192},{248... | collective-permute-start | bytes 1572872 | tf_op jit(solution)/shard_map/ppermute | solution.py:20
  115.7 53.2 %collective-permute-start.7 = (bf16[4,128,1024]{2,1,0:T(8,128)(2,1)}, bf16[4,128,1024]{2,1,0:T(8,128)(2,1)}, u32[]{:S(2)}, u32[]{:S(2)}) collective-permute-start(bf16[4,128,1024]{2,1,0:T(8,128)(2,1)} %bitcast.140), channel_id=1, source_target_pairs={{0,1},{1,0},{2,3},{3,2},{4,5},{5,4},{6,7},{7,6},{8,9},{9,8},{10,11... | collective-permute-start | bytes 3145736 | tf_op jit(solution)/shard_map/ppermute | solution.py:16
  147.8 13.1 %collective-permute-start.24 = (bf16[192,256]{1,0:T(8,128)(2,1)}, bf16[192,256]{1,0:T(8,128)(2,1)S(1)}, u32[]{:S(2)}, u32[]{:S(2)}) collective-permute-start(bf16[192,256]{1,0:T(8,128)(2,1)} %get-tuple-element.39), channel_id=1, source_target_pairs={{0,2},{1,3},{2,0},{3,1},{4,6},{5,7},{6,4},{7,5},{8,10},{9,11},{10,... | collective-permute-start | bytes 294920 | tf_op jit(solution)/shard_map/ppermute | solution.py:16
  172.9 15.2 %collective-permute-start.8 = (bf16[128,1024]{1,0:T(8,128)(2,1)S(1)}, bf16[128,1024]{1,0:T(8,128)(2,1)S(1)}, u32[]{:S(2)}, u32[]{:S(2)}) collective-permute-start(bf16[128,1024]{1,0:T(8,128)(2,1)S(1)} %get-tuple-element.25), channel_id=1, source_target_pairs={{0,2},{1,3},{2,0},{3,1},{4,6},{5,7},{6,4},{7,5},{8,10},{9,11},{10,... | collective-permute-start | bytes 786440 | tf_op jit(solution)/shard_map/ppermute | solution.py:16
  172.9 27.1 %collective-permute-start.9 = (bf16[128,1024]{1,0:T(8,128)(2,1)S(1)}, bf16[128,1024]{1,0:T(8,128)(2,1)S(1)}, u32[]{:S(2)}, u32[]{:S(2)}) collective-permute-start(bf16[128,1024]{1,0:T(8,128)(2,1)S(1)} %get-tuple-element.27), channel_id=1, source_target_pairs={{0,4},{1,5},{2,6},{3,7},{4,0},{5,1},{6,2},{7,3},{8,12},{9,13},{10,... | collective-permute-start | bytes 786440 | tf_op jit(solution)/shard_map/ppermute | solution.py:16
  175.0 25.9 %collective-permute-start.30 = (bf16[4,192,256]{2,1,0:T(8,128)(2,1)S(1)}, bf16[4,192,256]{2,1,0:T(8,128)(2,1)S(1)}, u32[]{:S(2)}, u32[]{:S(2)}) collective-permute-start(bf16[4,192,256]{2,1,0:T(8,128)(2,1)S(1)} %get-tuple-element.34), channel_id=1, source_target_pairs={{0,1},{1,0},{2,3},{3,2},{4,5},{5,4},{6,7},{7,6},{8,9},{9,8},{10,11... | collective-permute-start | bytes 1179656 | tf_op jit(solution)/shard_map/ppermute | solution.py:16
  205.0 16.3 %collective-permute-start.33 = (bf16[128,1024]{1,0:T(8,128)(2,1)S(1)}, bf16[128,1024]{1,0:T(8,128)(2,1)S(1)}, u32[]{:S(2)}, u32[]{:S(2)}) collective-permute-start(bf16[128,1024]{1,0:T(8,128)(2,1)S(1)} %get-tuple-element.43), channel_id=1, source_target_pairs={{0,6},{1,7},{2,4},{3,5},{4,2},{5,3},{6,0},{7,1},{8,14},{9,15},{10,... | collective-permute-start | bytes 786440 | tf_op jit(solution)/shard_map/ppermute | solution.py:16
  (23 other events, 179.6 us)

commit v2 on v0

v2 whole, which is shorter than its diff:
```python
import jax
import jax.numpy as jnp
from jax import lax
from jax.experimental import pallas as pl
from jax.experimental.pallas import tpu as pltpu
from jax.sharding import PartitionSpec as P

HIGH = lax.Precision.HIGHEST
BF = jnp.bfloat16
F32 = jnp.float32
RING = 4
VMEM = pl.BlockSpec(memory_space=pltpu.VMEM)
SMEM = pl.BlockSpec(memory_space=pltpu.SMEM)
PARAMS = pltpu.CompilerParams(vmem_limit_bytes=48 * 2**20)


def shape(dims, dtype):
    return jax.ShapeDtypeStruct(dims, dtype)


def mem_swap(value, bit):
    count = lax.axis_size("mem")
    return lax.ppermute(value, "mem", [(m, m ^ bit) for m in range(count)])


def band_send(value, pairs):
    return lax.ppermute(value, "band", pairs)


def after(value, *deps):
    return lax.optimization_barrier((value,) + deps)[0]


def send_three(own):
    bands = lax.axis_size("band")
    return band_send(own, [(s, (s + 3) % bands) for s in range(bands)])


def send_ring(own):
    bands = lax.axis_size("band")
    one = band_send(own, [(s, s + 1) for s in range(bands) if s % RING < 3])
    two = band_send(own, [(s, s + 2) for s in range(bands) if s % RING < 2])
    return one, two


def wrap_batches(one, two, three):
    bands = lax.axis_size("band")
    y = lax.axis_index("band") % RING
    two_wrap = band_send(three, [(s, s - 1) for s in range(bands) if s % RING in (1, 2)])
    one_wrap = band_send(three, [(s, s - 2) for s in range(bands) if s % RING == 2])
    return jnp.where(y < 1, one_wrap, one), jnp.where(y < 2, two_wrap, two)


def dot_t(a, b):
    return lax.dot_general(a, b, (((1,), (1,)), ((), ())), preferred_element_type=F32)


def sum_gram(part, core, *gate):
    rows = part.shape[0] // 2
    halves = part.reshape(2, rows, part.shape[1])
    keep = lax.dynamic_index_in_dim(halves, core, 0, keepdims=False)
    give = lax.dynamic_index_in_dim(halves, 1 - core, 0, keepdims=False)
    half = keep + mem_swap(give, 1)
    half = half + after(mem_swap(half, 2), *gate)
    half = half + mem_swap(half, 4)
    return half, mem_swap(half, 1)


def split(x):
    top = x.astype(BF)
    return top, (x - top.astype(F32)).astype(BF)


def dot_split(a, b):
    (a_top, a_low), (b_top, b_low) = a, b
    small = jnp.dot(a_top, b_low, preferred_element_type=F32)
    small = small + jnp.dot(a_low, b_top, preferred_element_type=F32)
    return small + jnp.dot(a_top, b_top, preferred_element_type=F32)


def dot_high(a, b):
    return jnp.dot(a, b, precision=HIGH, preferred_element_type=F32)


def weigh_kernel(scale, ids_ref, half_ref, other_ref, innov_ref, out_ref, x_ref, a_ref):
    rows, n = half_ref.shape
    core = ids_ref[0]
    i = lax.broadcasted_iota(jnp.int32, (n, n), 0)
    j = lax.broadcasted_iota(jnp.int32, (n, n), 1)
    eye = jnp.where(i == j, 1.0, 0.0).astype(F32)
    a_ref[pl.ds(core * rows, rows), :] = half_ref[...] * scale
    a_ref[pl.ds((1 - core) * rows, rows), :] = other_ref[...] * scale
    a = a_ref[...] + eye
    a_ref[...] = a
    most = jnp.max(jnp.sum(jnp.abs(a), axis=1, keepdims=True)) * 1.0001
    rho = (most - 1.0) / (most + 1.0)
    square = rho * rho
    grow = 2.0 / (2.0 - square)
    start = 2.0 / (1.0 + most)
    x_ref[...] = (2.0 * eye - a * start) * (start * grow)
    rho = square / (2.0 - square)

    def improve(product, rho):
        square = rho * rho
        grow = 2.0 / (2.0 - square)
        x = x_ref[...]
        r = eye - product(a_ref[...], x)
        x_ref[...] = (x + product(x, r)) * grow
        return square / (2.0 - square)

    @pl.when(most < 200.0)
    def _():
        a_parts = split(a_ref[...])

        def improve_fast(rho):
            square = rho * rho
            grow = 2.0 / (2.0 - square)
            x = x_ref[...]
            r = eye - dot_split(a_parts, split(x))
            step = jnp.dot(x.astype(BF), r.astype(BF), preferred_element_type=F32)
            x_ref[...] = (x + step) * grow
            return square / (2.0 - square)

        lax.while_loop(lambda rho: rho > 5e-3, improve_fast, rho)

    @pl.when(most >= 200.0)
    def _():
        lax.while_loop(lambda rho: rho > 5e-3, lambda rho: improve(dot_high, rho), rho)

    x = x_ref[...]
    r = eye - dot_high(a_ref[...], x)
    x = x + jnp.dot(x.astype(BF), r.astype(BF), preferred_element_type=F32)
    out_ref[...] = dot_split(split(x), split(innov_ref[...])).astype(BF)


def weigh(ids, half, other, innov, scale):
    n, width = innov.shape
    return pl.pallas_call(
        lambda *refs: weigh_kernel(scale, *refs),
        out_shape=shape((n, width), BF),
        in_specs=[SMEM, VMEM, VMEM, VMEM],
        out_specs=VMEM,
        scratch_shapes=[pltpu.VMEM((n, n), F32)] * 2,
        compiler_params=PARAMS,
        name="weigh",
    )(ids, half, other, innov)


def cross_kernel(ids_ref, x_ref, y0_ref, y1_ref, y2_ref, y3_ref, give_ref, keep_ref):
    rows = give_ref.shape[1]
    core = ids_ref[0]
    x = x_ref[pl.ds((1 - core) * rows, rows), :].astype(BF)
    for a, y_ref in enumerate((y0_ref, y1_ref, y2_ref, y3_ref)):
        give_ref[a] = dot_t(x, y_ref[...]).astype(BF)
    x = x_ref[pl.ds(core * rows, rows), :].astype(BF)
    for a, y_ref in enumerate((y0_ref, y1_ref, y2_ref, y3_ref)):
        keep_ref[a] = dot_t(x, y_ref[...])


def cross_halves(ids, state, y):
    rows = state.shape[0] // 2
    num_obs = y[0].shape[0]
    return pl.pallas_call(
        cross_kernel,
        out_shape=[shape((4, rows, num_obs), BF), shape((4, rows, num_obs), F32)],
        in_specs=[SMEM] + [VMEM] * 5,
        out_specs=[VMEM, VMEM],
        compiler_params=PARAMS,
        name="cross",
    )(ids, state, *y)


def halve_kernel(bit, ids_ref, keep_ref, recv_ref, give_ref, out_ref):
    rows = give_ref.shape[1]
    own = pl.ds(ids_ref[bit] * rows, rows)
    far = pl.ds((1 - ids_ref[bit]) * rows, rows)
    give_ref[...] = (keep_ref[:, far, :] + recv_ref[:, far, :].astype(F32)).astype(BF)
    out_ref[...] = keep_ref[:, own, :] + recv_ref[:, own, :].astype(F32)


def halve(bit, ids, keep, recv):
    a, rows, cols = keep.shape
    dims = (a, rows // 2, cols)
    return pl.pallas_call(
        lambda *refs: halve_kernel(bit, *refs),
        out_shape=[shape(dims, BF), shape(dims, F32)],
        in_specs=[SMEM, VMEM, VMEM],
        out_specs=[VMEM, VMEM],
        compiler_params=PARAMS,
        name="halve",
    )(ids, keep, recv)


def link_kernel(pairs, ids_ref, order_ref, *refs):
    w_refs, y_refs, (give_ref, keep_ref, all_ref) = refs[:4], refs[4:8], refs[8:]
    n = all_ref.shape[2]
    for t in range(4):
        for s in range(4):
            if s != t:
                all_ref[4 * t + s] = dot_t(w_refs[t][...], y_refs[s][...])
    core = ids_ref[0]
    half = len(pairs) // 2

    def pick(p):
        first = second = 0
        for k, (t, s) in enumerate(pairs):
            first = jnp.where(p == k, order_ref[0, t], first)
            second = jnp.where(p == k, order_ref[0, s], second)
        return all_ref[4 * first + second]

    for k in range(half):
        give_ref[0, pl.ds(k * n, n), :] = pick((1 - core) * half + k).astype(BF)
        keep_ref[0, pl.ds(k * n, n), :] = pick(core * half + k)


def link_halves(ids, order, w, y, pairs):
    n = y[0].shape[0]
    dims = (1, len(pairs) // 2 * n, n)
    return pl.pallas_call(
        lambda *refs: link_kernel(pairs, *refs),
        out_shape=[shape(dims, BF), shape(dims, F32)],
        in_specs=[SMEM, SMEM] + [VMEM] * 8,
        out_specs=[VMEM, VMEM],
        scratch_shapes=[pltpu.VMEM((16, n, n), F32)],
        compiler_params=PARAMS,
        name="link",
    )(ids, order, *w, *y)


def solve_kernel(pairs, ids_ref, order_ref, keep_ref, recv_ref, link_ref, far_ref, local_ref, out_ref, all_ref):
    piece = link_ref.shape[2]
    n = local_ref.shape[2]
    mine = ids_ref[3]
    for k in range(4):
        all_ref[pl.ds((mine ^ k) * piece, piece), :] = link_ref[k, 0]
        all_ref[pl.ds((mine ^ (k + 4)) * piece, piece), :] = far_ref[k, 0]
    coefs = []
    for s in range(4):
        a = order_ref[0, s]
        value = keep_ref[a] + recv_ref[a].astype(F32)
        for t in range(s):
            block = all_ref[pl.ds(pairs.index((t, s)) * n, n), :]
            value = value + jnp.dot(coefs[t], block, preferred_element_type=F32)
        coefs.append((value * local_ref[a]).astype(BF))
        out_ref[a] = coefs[s]


def solve(ids, order, keep, recv, link, far, local, pairs):
    n = keep.shape[2]
    return pl.pallas_call(
        lambda *refs: solve_kernel(pairs, *refs),
        out_shape=shape(keep.shape, BF),
        in_specs=[SMEM, SMEM] + [VMEM] * 5,
        out_specs=VMEM,
        scratch_shapes=[pltpu.VMEM((len(pairs) * n, n), BF)],
        compiler_params=PARAMS,
        name="solve",
    )(ids, order, keep, recv, link, far, local)


def most_kernel(ids_ref, x_ref, *refs):
    near_refs, far_ref, w_refs, out_ref = refs[:3], refs[3], refs[4:8], refs[8]
    rows = far_ref.shape[2]
    mine = ids_ref[3]
    for part in range(2):
        total = 0.0
        for a, w_ref in enumerate(w_refs):
            blocks = [near_refs[k][a] if part == 0 else far_ref[k, a] for k in range(3)]
            left = jnp.concatenate(blocks, axis=0)
            total = total + jnp.dot(left, w_ref[...], preferred_element_type=F32)
        for k in range(3):
            spot = pl.ds((mine ^ (k + 4 * part)) * rows, rows)
            out_ref[spot, :] = x_ref[spot, :] + total[k * rows : (k + 1) * rows, :]


def update_most(ids, state, near, far, w):
    cells, width = state.shape
    n = w[0].shape[0]
    step = 256
    tall = pl.BlockSpec((cells, step), lambda i: (0, i))
    whole = pl.BlockSpec(near[0].shape, lambda i: (0, 0, 0))
    whole_far = pl.BlockSpec(far.shape, lambda i: (0, 0, 0, 0))
    return pl.pallas_call(
        most_kernel,
        out_shape=shape((cells, width), F32),
        grid=(width // step,),
        in_specs=[SMEM, tall] + [whole] * 3 + [whole_far]
        + [pl.BlockSpec((n, step), lambda i: (0, i))] * 4,
        out_specs=tall,
        compiler_params=PARAMS,
        name="update_most",
    )(ids, state, *near, far, *w)


def rest_kernel(ids_ref, x_ref, near_ref, far_ref, w0_ref, w1_ref, w2_ref, w3_ref, _, out_ref):
    first = pl.program_id(0) == 0
    total = x_ref[...]
    for a, w_ref in enumerate((w0_ref, w1_ref, w2_ref, w3_ref)):
        left = jnp.where(first, near_ref[a], far_ref[a])
        total = total + jnp.dot(left, w_ref[...], preferred_element_type=F32)
    out_ref[...] = total


def update_rest(ids, state, near, far, w, most):
    cells, width = state.shape
    n = w[0].shape[0]
    rows = near.shape[1]
    block = pl.BlockSpec((rows, width), lambda i, ids: (ids[3] ^ (3 + 4 * i), 0))
    coef = pl.BlockSpec(near.shape, lambda i, ids: (0, 0, 0))
    wide = pl.BlockSpec((n, width), lambda i, ids: (0, 0))
    return pl.pallas_call(
        rest_kernel,
        out_shape=shape((cells, width), F32),
        grid_spec=pltpu.PrefetchScalarGridSpec(
            num_scalar_prefetch=1,
            grid=(2,),
            in_specs=[block, coef, coef] + [wide] * 4 + [pl.BlockSpec(memory_space=pl.ANY)],
            out_specs=block,
        ),
        input_output_aliases={8: 0},
        compiler_params=PARAMS,
        name="update_rest",
    )(ids, state, near, far, *w, most)


def spread_up(block):
    pair = jnp.stack([block, mem_swap(block, 4)])
    near = jnp.concatenate([pair, mem_swap(pair, 2)])
    return near, mem_swap(near, 1)


def on_device(state, obs_anom, innov, pattern, distance, taper, order):
    members = lax.axis_size("mem") * state.shape[1]
    scale = 1.0 / (members - 1)
    num_obs = obs_anom.shape[0]
    arrivals = order.shape[1]
    mem = lax.axis_index("mem")
    core, low, high = mem % 2, mem // 2 % 2, mem // 4
    mine = core * 4 + low * 2 + high
    ids = jnp.stack([core, low, high, mine]).astype(jnp.int32)
    pairs = [(t, s) for t in range(arrivals) for s in range(t + 1, arrivals)]

    y_one, y_two = send_ring(obs_anom)
    y_three = send_three(obs_anom)
    half, other = sum_gram(dot_t(obs_anom, obs_anom), core, y_one, y_two, y_three)
    weights = weigh(ids, half, other, innov, scale)
    y = [obs_anom, *wrap_batches(y_one, y_two, y_three), y_three]
    w_three = send_three(weights)
    w_one, w_two = send_ring(after(weights, y[1], y[2]))
    give, keep = cross_halves(ids, state, y)
    w_three = after(w_three, w_one, w_two)
    w = [weights, *wrap_batches(w_one, w_two, w_three), w_three]
    give, keep = halve(1, ids, keep, after(mem_swap(after(give, w_three), 1)))
    give, keep = halve(2, ids, keep, mem_swap(give, 2))
    cross_recv = mem_swap(give, 4)

    link_give, link_keep = link_halves(ids, order, w, y, pairs)
    link_give, link_keep = halve(1, ids, link_keep, mem_swap(after(link_give, give), 1))
    link_recv = after(mem_swap(link_give, 2), cross_recv)
    link_give, link_keep = halve(2, ids, link_keep, link_recv)
    link = (link_keep + mem_swap(link_give, 4).astype(F32)).astype(BF)
    link_near, link_far = spread_up(link)

    onehot = (distance[0][..., None] == jnp.arange(taper.shape[0], dtype=jnp.int32)).astype(F32)
    local = pattern[0].astype(F32) * jnp.sum(onehot * taper, axis=-1)
    local = lax.dynamic_index_in_dim(local, mine, 1, keepdims=False) * scale
    local = jnp.repeat(local, num_obs // local.shape[1], axis=1)[:, None, :]
    coefs = solve(ids, order, keep, cross_recv, link_near, link_far, local, pairs)
    high_c = mem_swap(coefs, 4)
    low_c = mem_swap(coefs, 2)
    both_c = mem_swap(high_c, 2)
    far_most = mem_swap(jnp.stack([coefs, high_c, low_c]), 1)
    most = update_most(ids, state, [coefs, high_c, low_c], far_most, w)
    far_rest = mem_swap(after(both_c, most), 1)
    return update_rest(ids, state, both_c, far_rest, w, most)


def solution(mesh):
    return jax.shard_map(
        on_device,
        mesh=mesh,
        in_specs=(
            P("band", "mem"),
            P("band", "mem"),
            P("band", "mem"),
            P("band", None, None, None),
            P("band", None, None, None),
            P(),
            P("band", None),
        ),
        out_specs=P("band", "mem"),
        check_vma=False,
    )
```

time: 649 us -> 182 us (0.28); the launches traced: 640 us -> 181 us
  waiting for transfers between devices: 500 us -> 91.8 us
  starting transfers between devices: 1.84 us -> 56.4 us
  other arithmetic: 58 us -> 4.31 us
  matrix products: 43.7 us -> 1.56 us
  Pallas kernels: 0 us -> 23.6 us
  between operations: 22.8 us -> 0.35 us
  local copies, waits for them, and re-layouts: 13.5 us -> 3.08 us
    psum x5 -> x0, waiting for transfers between devices: 353 us -> none  [the longest x4 280 us: on_device(): cross = lax.psum(cross_part, 'mem')]
    another operation x12 -> x3, other arithmetic: 55.9 us -> 0.18 us  [the longest x1 0.09 us: on_device(): far_most = mem_swap(jnp.stack([coefs, high_c, low_c]), 1)]
    ppermute x3 -> x28, waiting for transfers between devices: 147 us -> 91.8 us  [the longest x18 55.7 us: mem_swap(): return lax.ppermute(value, 'mem', [(m, m ^ bit) for m in range(count)])]
    ppermute x3 -> x28, starting transfers between devices: 1.29 us -> 56.4 us  [the longest x10 30.4 us: band_send(): return lax.ppermute(value, 'band', pairs)]
    dot_general x9 -> x1, matrix products: 39.6 us -> 1.56 us  [dot_t(): lax.dot_general(a, b, (((1,), (1,)), ((), ())), preferred_element_type=F32)]
    pallas_call x0 -> x10, Pallas kernels: none -> 23.6 us  [the longest x1 5.83 us: update_most(): pl.pallas_call(most_kernel, out_shape=shape((cells, width), F32), grid=(w...]
  transfers between devices with their start and end apart: 8 -> 28, of which waited for: 8 -> 17; matrix products, arithmetic and copies ran while one was open for 0% -> 3% of each run, Pallas kernels for 0% -> 10%
where the time goes in v2:
time: 182 us; the launch traced here: 181 us
  waiting for transfers between devices  91.8 us (50%)
  starting transfers between devices  56.4 us (31%)
  Pallas kernels  23.6 us (13%)
  other arithmetic  4.31 us (2%)
  local copies, waits for them, and re-layouts  3.08 us (2%)
    ppermute x18, waiting for transfers between devices, mem_swap(): return lax.ppermute(value, 'mem', [(m, m ^ bit) for m in range(count)])  55.7 us
    ppermute x10, waiting for transfers between devices, band_send(): return lax.ppermute(value, 'band', pairs)  36.1 us
    ppermute x10, starting transfers between devices, band_send(): return lax.ppermute(value, 'band', pairs)  30.4 us
    ppermute x18, starting transfers between devices, mem_swap(): return lax.ppermute(value, 'mem', [(m, m ^ bit) for m in range(count)])  26 us
    pallas_call x1, Pallas kernels, update_most(): pl.pallas_call(most_kernel, out_shape=shape((cells, width), F32), grid=(w...  5.83 us
    pallas_call x1, Pallas kernels, cross_halves(): pl.pallas_call(cross_kernel, out_shape=[shape((4, rows, num_obs), BF), sh...  4.56 us
    pallas_call x1, Pallas kernels, weigh(): pl.pallas_call(lambda *refs: weigh_kernel(scale, *refs), out_shape=shape(...  3.83 us
  transfers between devices with their start and end apart: 28, of which 17 were waited for; matrix products, arithmetic and copies ran while one was open for 3% of the time, Pallas kernels for 10%

profile of v2, /device:TPU:1, one launch (start us, length us, event | category | flops | bytes accessed | tf_op | source)
XLA Modules:
  0.0 181.1 jit_solution(5976071202099643259)
XLA Ops:
  0.0 3.6 %collective-permute-start = (bf16[256,1024]{1,0:T(8,128)(2,1)}, bf16[256,1024]{1,0:T(8,128)(2,1)S(1)}, u32[]{:S(2)}, u32[]{:S(2)}) collective-permute-start(bf16[256,1024]{1,0:T(8,128)(2,1)} %refs_6_.1), channel_id=1, source_target_pairs={{0,24},{8,32},{16,40},{24,48},{32,56},{40,64},{48,72},{56,80},{64,... | collective-permute-start | bytes 1572872 | tf_op jit(solution)/shard_map/ppermute | solution.py:27
  3.6 8.9 %collective-permute-start.4 = (bf16[256,1024]{1,0:T(8,128)(2,1)}, bf16[256,1024]{1,0:T(8,128)(2,1)S(1)}, u32[]{:S(2)}, u32[]{:S(2)}) collective-permute-start(bf16[256,1024]{1,0:T(8,128)(2,1)} %refs_6_.1), channel_id=1, source_target_pairs={{0,16},{8,24},{32,48},{40,56},{64,80},{72,88},{96,112},{104,120},{... | collective-permute-start | bytes 1572872 | tf_op jit(solution)/shard_map/ppermute | solution.py:27
  12.5 2.6 %collective-permute-start.2 = (bf16[256,1024]{1,0:T(8,128)(2,1)}, bf16[256,1024]{1,0:T(8,128)(2,1)S(1)}, u32[]{:S(2)}, u32[]{:S(2)}) collective-permute-start(bf16[256,1024]{1,0:T(8,128)(2,1)} %refs_6_.1), channel_id=1, source_target_pairs={{0,8},{8,16},{16,24},{32,40},{40,48},{48,56},{64,72},{72,80},{80,8... | collective-permute-start | bytes 1572872 | tf_op jit(solution)/shard_map/ppermute | solution.py:27
  18.3 6.4 %collective-permute-done.y3_ref.refs_9_ = bf16[256,1024]{1,0:T(8,128)(2,1)S(1)} collective-permute-done((bf16[256,1024]{1,0:T(8,128)(2,1)}, bf16[256,1024]{1,0:T(8,128)(2,1)S(1)}, u32[]{:S(2)}, u32[]{:S(2)}) %collective-permute-start) | collective-permute-done | bytes 524320 | tf_op jit(solution)/shard_map/ppermute | solution.py:27
  26.1 10.2 %collective-permute-start.6 = (f32[128,256]{1,0:T(8,128)S(1)}, f32[128,256]{1,0:T(8,128)S(1)}, u32[]{:S(2)}, u32[]{:S(2)}) collective-permute-start(f32[128,256]{1,0:T(8,128)S(1)} %bitcast_add_fusion), channel_id=1, source_target_pairs={{0,2},{1,3},{2,0},{3,1},{4,6},{5,7},{6,4},{7,5},{8,10},{9,11},{10,... | collective-permute-start | bytes 393224 | tf_op jit(solution)/shard_map/ppermute | solution.py:23
  36.3 2.8 %collective-permute-done.6 = f32[128,256]{1,0:T(8,128)S(1)} collective-permute-done((f32[128,256]{1,0:T(8,128)S(1)}, f32[128,256]{1,0:T(8,128)S(1)}, u32[]{:S(2)}, u32[]{:S(2)}) %collective-permute-start.6) | collective-permute-done | bytes 131104 | tf_op jit(solution)/shard_map/ppermute | solution.py:23
  41.8 4.2 %collective-permute-done.7 = f32[128,256]{1,0:T(8,128)S(1)} collective-permute-done((f32[128,256]{1,0:T(8,128)S(1)}, f32[128,256]{1,0:T(8,128)S(1)}, u32[]{:S(2)}, u32[]{:S(2)}) %collective-permute-start.7) | collective-permute-done | bytes 131104 | tf_op jit(solution)/shard_map/ppermute | solution.py:23
  46.0 2.9 %collective-permute-start.8 = (f32[128,256]{1,0:T(8,128)S(1)}, f32[128,256]{1,0:T(8,128)S(1)}, u32[]{:S(2)}, u32[]{:S(2)}) collective-permute-start(f32[128,256]{1,0:T(8,128)S(1)} %add.52.refs_1_), channel_id=1, source_target_pairs={{0,1},{1,0},{2,3},{3,2},{4,5},{5,4},{6,7},{7,6},{8,9},{9,8},{10,11... | collective-permute-start | bytes 393224 | tf_op jit(solution)/shard_map/ppermute | solution.py:23
  51.1 3.8 %weigh.1.refs_2_.refs_4_.w0_ref = bf16[256,1024]{1,0:T(8,128)(2,1)S(1)} custom-call(s32[4]{0:T(128)S(1)} %pad_add_fusion.ids_ref.refs_0_, f32[128,256]{1,0:T(8,128)S(1)} %add.52.refs_1_, f32[128,256]{1,0:T(8,128)S(1)} %collective-permute-done.8.refs_2_, f32[256,1024]{1,0:T(8,128)S(1)} %copy-done.1), custom_call_target="tpu_custom_call" | custom-call | tf_op jit(solution)/shard_map/weigh/pallas_call | solution.py:138
  57.2 6.7 %collective-permute-start.11 = (bf16[256,1024]{1,0:T(8,128)(2,1)S(1)}, bf16[256,1024]{1,0:T(8,128)(2,1)S(1)}, u32[]{:S(2)}, u32[]{:S(2)}) collective-permute-start(bf16[256,1024]{1,0:T(8,128)(2,1)S(1)} %weigh.1.refs_2_.refs_4_.w0_ref), channel_id=1, source_target_pairs={{0,16},{8,24},{32,48},{40,56},{64,80},{72,88},{96,112},{104,120},{... | collective-permute-start | bytes 1572872 | tf_op jit(solution)/shard_map/ppermute | solution.py:27
  63.9 3.4 %collective-permute-start.10 = (bf16[256,1024]{1,0:T(8,128)(2,1)S(1)}, bf16[256,1024]{1,0:T(8,128)(2,1)S(1)}, u32[]{:S(2)}, u32[]{:S(2)}) collective-permute-start(bf16[256,1024]{1,0:T(8,128)(2,1)S(1)} %weigh.1.refs_2_.refs_4_.w0_ref), channel_id=1, source_target_pairs={{0,8},{8,16},{16,24},{32,40},{40,48},{48,56},{64,72},{72,80},{80,8... | collective-permute-start | bytes 1572872 | tf_op jit(solution)/shard_map/ppermute | solution.py:27
  67.4 4.6 %cross.1 = (bf16[4,512,256]{2,1,0:T(8,128)(2,1)S(1)}, f32[4,512,256]{2,1,0:T(8,128)S(1)}) custom-call(s32[4]{0:T(128)S(1)} %pad_add_fusion.ids_ref.refs_0_, f32[1024,1024]{1,0:T(8,128)} %x_ref.5, bf16[256,1024]{1,0:T(8,128)(2,1)S(1)} %copy-done, bf16[256,1024]{1,0:T(8,128)(2,1)S(1)} %broadcast_select_fusion.3.y1_ref.refs_7_, ...), custom_call_target="tpu_custom_call" | custom-call | tf_op jit(solution)/shard_map/cross/pallas_call | solution.py:163
  71.9 14.4 %collective-permute-done.9.refs_5_.refs_7_.w3_ref = bf16[256,1024]{1,0:T(8,128)(2,1)S(1)} collective-permute-done((bf16[256,1024]{1,0:T(8,128)(2,1)S(1)}, bf16[256,1024]{1,0:T(8,128)(2,1)S(1)}, u32[]{:S(2)}, u32[]{:S(2)}) %collective-permute-start.9) | collective-permute-done | bytes 524320 | tf_op jit(solution)/shard_map/ppermute | solution.py:27
  91.3 12.4 %collective-permute-done.16 = bf16[256,1024]{1,0:T(8,128)(2,1)S(1)} collective-permute-done((bf16[256,1024]{1,0:T(8,128)(2,1)S(1)}, bf16[256,1024]{1,0:T(8,128)(2,1)S(1)}, u32[]{:S(2)}, u32[]{:S(2)}) %collective-permute-start.16) | collective-permute-done | bytes 524320 | tf_op jit(solution)/shard_map/ppermute | solution.py:27
  103.7 2.8 %collective-permute-done.15 = bf16[256,1024]{1,0:T(8,128)(2,1)S(1)} collective-permute-done((bf16[256,1024]{1,0:T(8,128)(2,1)S(1)}, bf16[256,1024]{1,0:T(8,128)(2,1)S(1)}, u32[]{:S(2)}, u32[]{:S(2)}) %collective-permute-start.15) | collective-permute-done | bytes 524320 | tf_op jit(solution)/shard_map/ppermute | solution.py:27
  106.7 2.5 %link.1 = (bf16[1,768,256]{2,1,0:T(8,128)(2,1)S(1)}, f32[1,768,256]{2,1,0:T(8,128)S(1)}) custom-call(s32[4]{0:T(128)S(1)} %pad_add_fusion.ids_ref.refs_0_, s32[1,4]{1,0:T(1,128)S(1)} %copy-done.4, bf16[256,1024]{1,0:T(8,128)(2,1)S(1)} %weigh.1.refs_2_.refs_4_.w0_ref, bf16[256,1024]{1,0:T(8,128)(2,1)S(1)} %broadcast_select_fusion.2.refs_3_.refs_5_.w1_ref, ...), custom_call_target="tpu_custom_call" | custom-call | tf_op jit(solution)/shard_map/link/pallas_call | solution.py:219
  113.6 11.7 %collective-permute-done.14.refs_3_ = bf16[4,128,256]{2,1,0:T(8,128)(2,1)S(1)} collective-permute-done((bf16[4,128,256]{2,1,0:T(8,128)(2,1)S(1)}, bf16[4,128,256]{2,1,0:T(8,128)(2,1)S(1)}, u32[]{:S(2)}, u32[]{:S(2)}) %collective-permute-start.14) | collective-permute-done | bytes 262176 | tf_op jit(solution)/shard_map/ppermute | solution.py:23
  126.7 7.1 %collective-permute-done.19 = bf16[1,192,256]{2,1,0:T(8,128)(2,1)S(1)} collective-permute-done((bf16[1,192,256]{2,1,0:T(8,128)(2,1)S(1)}, bf16[1,192,256]{2,1,0:T(8,128)(2,1)S(1)}, u32[]{:S(2)}, u32[]{:S(2)}) %collective-permute-start.19) | collective-permute-done | bytes 98336 | tf_op jit(solution)/shard_map/ppermute | solution.py:23
  133.9 6.9 %collective-permute-done.20 = bf16[1,192,256]{2,1,0:T(8,128)(2,1)S(1)} collective-permute-done((bf16[1,192,256]{2,1,0:T(8,128)(2,1)S(1)}, bf16[1,192,256]{2,1,0:T(8,128)(2,1)S(1)}, u32[]{:S(2)}, u32[]{:S(2)}) %collective-permute-start.20) | collective-permute-done | bytes 98336 | tf_op jit(solution)/shard_map/ppermute | solution.py:23
  141.0 6.0 %collective-permute-done.21 = bf16[2,1,192,256]{3,2,1,0:T(8,128)(2,1)S(1)} collective-permute-done((bf16[2,1,192,256]{3,2,1,0:T(8,128)(2,1)S(1)}, bf16[2,1,192,256]{3,2,1,0:T(8,128)(2,1)S(1)}, u32[]{:S(2)}, u32[]{:S(2)}) %collective-permute-start.21) | collective-permute-done | bytes 196640 | tf_op jit(solution)/shard_map/ppermute | solution.py:23
  152.4 2.0 %collective-permute-start.23 = (bf16[4,128,256]{2,1,0:T(8,128)(2,1)S(1)}, bf16[4,128,256]{2,1,0:T(8,128)(2,1)S(1)}, u32[]{:S(2)}, u32[]{:S(2)}) collective-permute-start(bf16[4,128,256]{2,1,0:T(8,128)(2,1)S(1)} %solve.1.refs_0_), channel_id=1, source_target_pairs={{0,4},{1,5},{2,6},{3,7},{4,0},{5,1},{6,2},{7,3},{8,12},{9,13},{10,... | collective-permute-start | bytes 786440 | tf_op jit(solution)/shard_map/ppermute | solution.py:23
  154.3 10.8 %collective-permute-done.25.refs_2_ = bf16[4,128,256]{2,1,0:T(8,128)(2,1)S(1)} collective-permute-done((bf16[4,128,256]{2,1,0:T(8,128)(2,1)S(1)}, bf16[4,128,256]{2,1,0:T(8,128)(2,1)S(1)}, u32[]{:S(2)}, u32[]{:S(2)}) %collective-permute-start.25) | collective-permute-done | bytes 262176 | tf_op jit(solution)/shard_map/ppermute | solution.py:23
  169.8 5.8 %update_most.1._ = f32[1024,1024]{1,0:T(8,128)} custom-call(s32[4]{0:T(128)S(1)} %pad_add_fusion.ids_ref.refs_0_, f32[1024,1024]{1,0:T(8,128)} %x_ref.5, bf16[4,128,256]{2,1,0:T(8,128)(2,1)S(1)} %solve.1.refs_0_, bf16[4,128,256]{2,1,0:T(8,128)(2,1)S(1)} %collective-permute-done.23.refs_1_, bf16[4,128,256]{2,1,0:T(8,128)(2,1)S(1)} %collective-permute-done.25.refs_2_, ...), custom_call_target="tpu_custom_call" | custom-call | tf_op jit(solution)/shard_map/update_most/pallas_call | solution.py:283
  177.8 3.3 %update_rest.1 = f32[1024,1024]{1,0:T(8,128)} custom-call(s32[4]{0:T(128)S(1)} %pad_add_fusion.ids_ref.refs_0_, f32[1024,1024]{1,0:T(8,128)} %x_ref.5, bf16[4,128,256]{2,1,0:T(8,128)(2,1)S(1)} %collective-permute-done.24.near_ref, bf16[4,128,256]{2,1,0:T(8,128)(2,1)S(1)} %collective-permute-done.27.far_ref, ...), custom_call_target="tpu_custom_call", output_to_operand_aliasing={{}: (8, {})} | custom-call | tf_op jit(solution)/shard_map/update_rest/pallas_call | solution.py:311
  (73 shorter events, 35.0 us)
Async XLA Ops:
  0.0 24.8 %collective-permute-start = (bf16[256,1024]{1,0:T(8,128)(2,1)}, bf16[256,1024]{1,0:T(8,128)(2,1)S(1)}, u32[]{:S(2)}, u32[]{:S(2)}) collective-permute-start(bf16[256,1024]{1,0:T(8,128)(2,1)} %refs_6_.1), channel_id=1, source_target_pairs={{0,24},{8,32},{16,40},{24,48},{32,56},{40,64},{48,72},{56,80},{64,... | collective-permute-start | bytes 1572872 | tf_op jit(solution)/shard_map/ppermute | solution.py:27
  3.6 35.5 %collective-permute-start.4 = (bf16[256,1024]{1,0:T(8,128)(2,1)}, bf16[256,1024]{1,0:T(8,128)(2,1)S(1)}, u32[]{:S(2)}, u32[]{:S(2)}) collective-permute-start(bf16[256,1024]{1,0:T(8,128)(2,1)} %refs_6_.1), channel_id=1, source_target_pairs={{0,16},{8,24},{32,48},{40,56},{64,80},{72,88},{96,112},{104,120},{... | collective-permute-start | bytes 1572872 | tf_op jit(solution)/shard_map/ppermute | solution.py:27
  12.5 26.6 %collective-permute-start.2 = (bf16[256,1024]{1,0:T(8,128)(2,1)}, bf16[256,1024]{1,0:T(8,128)(2,1)S(1)}, u32[]{:S(2)}, u32[]{:S(2)}) collective-permute-start(bf16[256,1024]{1,0:T(8,128)(2,1)} %refs_6_.1), channel_id=1, source_target_pairs={{0,8},{8,16},{16,24},{32,40},{40,48},{48,56},{64,72},{72,80},{80,8... | collective-permute-start | bytes 1572872 | tf_op jit(solution)/shard_map/ppermute | solution.py:27
  16.7 9.3 %collective-permute-start.5 = (f32[128,256]{1,0:T(8,128)S(1)}, f32[128,256]{1,0:T(8,128)S(1)}, u32[]{:S(2)}, u32[]{:S(2)}) collective-permute-start(f32[128,256]{1,0:T(8,128)S(1)} %dynamic-slice_bitcast_fusion), channel_id=1, source_target_pairs={{0,1},{1,0},{2,3},{3,2},{4,5},{5,4},{6,7},{7,6},{8,9},{9,8},{10,11... | collective-permute-start | bytes 393224 | tf_op jit(solution)/shard_map/ppermute | solution.py:23
  24.8 30.2 %collective-permute-start.3 = (bf16[256,1024]{1,0:T(8,128)(2,1)S(1)}, bf16[256,1024]{1,0:T(8,128)(2,1)}, u32[]{:S(2)}, u32[]{:S(2)}) collective-permute-start(bf16[256,1024]{1,0:T(8,128)(2,1)S(1)} %collective-permute-done.y3_ref.refs_9_), channel_id=1, source_target_pairs={{8,0},{16,8},{40,32},{48,40},{72,64},{80,72},{104,96},{112,104},{1... | collective-permute-start | bytes 1572872 | tf_op jit(solution)/shard_map/ppermute | solution.py:27
  26.1 12.9 %collective-permute-start.6 = (f32[128,256]{1,0:T(8,128)S(1)}, f32[128,256]{1,0:T(8,128)S(1)}, u32[]{:S(2)}, u32[]{:S(2)}) collective-permute-start(f32[128,256]{1,0:T(8,128)S(1)} %bitcast_add_fusion), channel_id=1, source_target_pairs={{0,2},{1,3},{2,0},{3,1},{4,6},{5,7},{6,4},{7,5},{8,10},{9,11},{10,... | collective-permute-start | bytes 393224 | tf_op jit(solution)/shard_map/ppermute | solution.py:23
  39.0 6.9 %collective-permute-start.7 = (f32[128,256]{1,0:T(8,128)S(1)}, f32[128,256]{1,0:T(8,128)S(1)}, u32[]{:S(2)}, u32[]{:S(2)}) collective-permute-start(f32[128,256]{1,0:T(8,128)S(1)} %add.51), channel_id=1, source_target_pairs={{0,4},{1,5},{2,6},{3,7},{4,0},{5,1},{6,2},{7,3},{8,12},{9,13},{10,... | collective-permute-start | bytes 393224 | tf_op jit(solution)/shard_map/ppermute | solution.py:23
  40.5 15.7 %collective-permute-start.1 = (bf16[256,1024]{1,0:T(8,128)(2,1)S(1)}, bf16[256,1024]{1,0:T(8,128)(2,1)}, u32[]{:S(2)}, u32[]{:S(2)}) collective-permute-start(bf16[256,1024]{1,0:T(8,128)(2,1)S(1)} %collective-permute-done.y3_ref.refs_9_), channel_id=1, source_target_pairs={{16,0},{48,32},{80,64},{112,96},{144,128},{176,160},{208,192},{240... | collective-permute-start | bytes 1572872 | tf_op jit(solution)/shard_map/ppermute | solution.py:27
  46.0 3.9 %collective-permute-start.8 = (f32[128,256]{1,0:T(8,128)S(1)}, f32[128,256]{1,0:T(8,128)S(1)}, u32[]{:S(2)}, u32[]{:S(2)}) collective-permute-start(f32[128,256]{1,0:T(8,128)S(1)} %add.52.refs_1_), channel_id=1, source_target_pairs={{0,1},{1,0},{2,3},{3,2},{4,5},{5,4},{6,7},{7,6},{8,9},{9,8},{10,11... | collective-permute-start | bytes 393224 | tf_op jit(solution)/shard_map/ppermute | solution.py:23
  54.9 31.4 %collective-permute-start.9 = (bf16[256,1024]{1,0:T(8,128)(2,1)S(1)}, bf16[256,1024]{1,0:T(8,128)(2,1)S(1)}, u32[]{:S(2)}, u32[]{:S(2)}) collective-permute-start(bf16[256,1024]{1,0:T(8,128)(2,1)S(1)} %weigh.1.refs_2_.refs_4_.w0_ref), channel_id=1, source_target_pairs={{0,24},{8,32},{16,40},{24,48},{32,56},{40,64},{48,72},{56,80},{64,... | collective-permute-start | bytes 1572872 | tf_op jit(solution)/shard_map/ppermute | solution.py:27
  57.2 29.1 %collective-permute-start.11 = (bf16[256,1024]{1,0:T(8,128)(2,1)S(1)}, bf16[256,1024]{1,0:T(8,128)(2,1)S(1)}, u32[]{:S(2)}, u32[]{:S(2)}) collective-permute-start(bf16[256,1024]{1,0:T(8,128)(2,1)S(1)} %weigh.1.refs_2_.refs_4_.w0_ref), channel_id=1, source_target_pairs={{0,16},{8,24},{32,48},{40,56},{64,80},{72,88},{96,112},{104,120},{... | collective-permute-start | bytes 1572872 | tf_op jit(solution)/shard_map/ppermute | solution.py:27
  63.9 22.4 %collective-permute-start.10 = (bf16[256,1024]{1,0:T(8,128)(2,1)S(1)}, bf16[256,1024]{1,0:T(8,128)(2,1)S(1)}, u32[]{:S(2)}, u32[]{:S(2)}) collective-permute-start(bf16[256,1024]{1,0:T(8,128)(2,1)S(1)} %weigh.1.refs_2_.refs_4_.w0_ref), channel_id=1, source_target_pairs={{0,8},{8,16},{16,24},{32,40},{40,48},{48,56},{64,72},{72,80},{80,8... | collective-permute-start | bytes 1572872 | tf_op jit(solution)/shard_map/ppermute | solution.py:27
  86.3 3.9 %collective-permute-start.12 = (bf16[4,512,256]{2,1,0:T(8,128)(2,1)S(1)}, bf16[4,512,256]{2,1,0:T(8,128)(2,1)S(1)}, u32[]{:S(2)}, u32[]{:S(2)}) collective-permute-start(bf16[4,512,256]{2,1,0:T(8,128)(2,1)S(1)} %get-tuple-element.29), channel_id=1, source_target_pairs={{0,1},{1,0},{2,3},{3,2},{4,5},{5,4},{6,7},{7,6},{8,9},{9,8},{10,11... | collective-permute-start | bytes 3145736 | tf_op jit(solution)/shard_map/ppermute | solution.py:23
  87.7 16.0 %collective-permute-start.16 = (bf16[256,1024]{1,0:T(8,128)(2,1)S(1)}, bf16[256,1024]{1,0:T(8,128)(2,1)S(1)}, u32[]{:S(2)}, u32[]{:S(2)}) collective-permute-start(bf16[256,1024]{1,0:T(8,128)(2,1)S(1)} %collective-permute-done.9.refs_5_.refs_7_.w3_ref), channel_id=1, source_target_pairs={{8,0},{16,8},{40,32},{48,40},{72,64},{80,72},{104,96},{112,104},{1... | collective-permute-start | bytes 1572872 | tf_op jit(solution)/shard_map/ppermute | solution.py:27
  89.0 17.6 %collective-permute-start.15 = (bf16[256,1024]{1,0:T(8,128)(2,1)S(1)}, bf16[256,1024]{1,0:T(8,128)(2,1)S(1)}, u32[]{:S(2)}, u32[]{:S(2)}) collective-permute-start(bf16[256,1024]{1,0:T(8,128)(2,1)S(1)} %collective-permute-done.9.refs_5_.refs_7_.w3_ref), channel_id=1, source_target_pairs={{16,0},{48,32},{80,64},{112,96},{144,128},{176,160},{208,192},{240... | collective-permute-start | bytes 1572872 | tf_op jit(solution)/shard_map/ppermute | solution.py:27
  91.0 18.2 %collective-permute-start.13 = (bf16[4,256,256]{2,1,0:T(8,128)(2,1)S(1)}, bf16[4,256,256]{2,1,0:T(8,128)(2,1)S(1)}, u32[]{:S(2)}, u32[]{:S(2)}) collective-permute-start(bf16[4,256,256]{2,1,0:T(8,128)(2,1)S(1)} %get-tuple-element.31), channel_id=1, source_target_pairs={{0,2},{1,3},{2,0},{3,1},{4,6},{5,7},{6,4},{7,5},{8,10},{9,11},{10,... | collective-permute-start | bytes 1572872 | tf_op jit(solution)/shard_map/ppermute | solution.py:23
  110.7 14.7 %collective-permute-start.14 = (bf16[4,128,256]{2,1,0:T(8,128)(2,1)S(1)}, bf16[4,128,256]{2,1,0:T(8,128)(2,1)S(1)}, u32[]{:S(2)}, u32[]{:S(2)}) collective-permute-start(bf16[4,128,256]{2,1,0:T(8,128)(2,1)S(1)} %get-tuple-element.33), channel_id=1, source_target_pairs={{0,4},{1,5},{2,6},{3,7},{4,0},{5,1},{6,2},{7,3},{8,12},{9,13},{10,... | collective-permute-start | bytes 786440 | tf_op jit(solution)/shard_map/ppermute | solution.py:23
  112.7 13.4 %collective-permute-start.18 = (bf16[1,384,256]{2,1,0:T(8,128)(2,1)S(1)}, bf16[1,384,256]{2,1,0:T(8,128)(2,1)S(1)}, u32[]{:S(2)}, u32[]{:S(2)}) collective-permute-start(bf16[1,384,256]{2,1,0:T(8,128)(2,1)S(1)} %get-tuple-element.38), channel_id=1, source_target_pairs={{0,2},{1,3},{2,0},{3,1},{4,6},{5,7},{6,4},{7,5},{8,10},{9,11},{10,... | collective-permute-start | bytes 589832 | tf_op jit(solution)/shard_map/ppermute | solution.py:23
  126.6 7.2 %collective-permute-start.19 = (bf16[1,192,256]{2,1,0:T(8,128)(2,1)S(1)}, bf16[1,192,256]{2,1,0:T(8,128)(2,1)S(1)}, u32[]{:S(2)}, u32[]{:S(2)}) collective-permute-start(bf16[1,192,256]{2,1,0:T(8,128)(2,1)S(1)} %get-tuple-element.41), channel_id=1, source_target_pairs={{0,4},{1,5},{2,6},{3,7},{4,0},{5,1},{6,2},{7,3},{8,12},{9,13},{10,... | collective-permute-start | bytes 294920 | tf_op jit(solution)/shard_map/ppermute | solution.py:23
  133.8 7.0 %collective-permute-start.20 = (bf16[1,192,256]{2,1,0:T(8,128)(2,1)S(1)}, bf16[1,192,256]{2,1,0:T(8,128)(2,1)S(1)}, u32[]{:S(2)}, u32[]{:S(2)}) collective-permute-start(bf16[1,192,256]{2,1,0:T(8,128)(2,1)S(1)} %add_convert_fusion), channel_id=1, source_target_pairs={{0,4},{1,5},{2,6},{3,7},{4,0},{5,1},{6,2},{7,3},{8,12},{9,13},{10,... | collective-permute-start | bytes 294920 | tf_op jit(solution)/shard_map/ppermute | solution.py:23
  140.9 6.1 %collective-permute-start.21 = (bf16[2,1,192,256]{3,2,1,0:T(8,128)(2,1)S(1)}, bf16[2,1,192,256]{3,2,1,0:T(8,128)(2,1)S(1)}, u32[]{:S(2)}, u32[]{:S(2)}) collective-permute-start(bf16[2,1,192,256]{3,2,1,0:T(8,128)(2,1)S(1)} %pad_maximum_fusion.2), channel_id=1, source_target_pairs={{0,2},{1,3},{2,0},{3,1},{4,6},{5,7},{6,4},{7,5},{8,10},{9,11},{10,... | collective-permute-start | bytes 589832 | tf_op jit(solution)/shard_map/ppermute | solution.py:23
  152.3 12.9 %collective-permute-start.25 = (bf16[4,128,256]{2,1,0:T(8,128)(2,1)S(1)}, bf16[4,128,256]{2,1,0:T(8,128)(2,1)S(1)}, u32[]{:S(2)}, u32[]{:S(2)}) collective-permute-start(bf16[4,128,256]{2,1,0:T(8,128)(2,1)S(1)} %solve.1.refs_0_), channel_id=1, source_target_pairs={{0,2},{1,3},{2,0},{3,1},{4,6},{5,7},{6,4},{7,5},{8,10},{9,11},{10,... | collective-permute-start | bytes 786440 | tf_op jit(solution)/shard_map/ppermute | solution.py:23
  152.4 14.3 %collective-permute-start.23 = (bf16[4,128,256]{2,1,0:T(8,128)(2,1)S(1)}, bf16[4,128,256]{2,1,0:T(8,128)(2,1)S(1)}, u32[]{:S(2)}, u32[]{:S(2)}) collective-permute-start(bf16[4,128,256]{2,1,0:T(8,128)(2,1)S(1)} %solve.1.refs_0_), channel_id=1, source_target_pairs={{0,4},{1,5},{2,6},{3,7},{4,0},{5,1},{6,2},{7,3},{8,12},{9,13},{10,... | collective-permute-start | bytes 786440 | tf_op jit(solution)/shard_map/ppermute | solution.py:23
  167.9 7.9 %collective-permute-start.24 = (bf16[4,128,256]{2,1,0:T(8,128)(2,1)S(1)}, bf16[4,128,256]{2,1,0:T(8,128)(2,1)S(1)}, u32[]{:S(2)}, u32[]{:S(2)}) collective-permute-start(bf16[4,128,256]{2,1,0:T(8,128)(2,1)S(1)} %collective-permute-done.23.refs_1_), channel_id=1, source_target_pairs={{0,2},{1,3},{2,0},{3,1},{4,6},{5,7},{6,4},{7,5},{8,10},{9,11},{10,... | collective-permute-start | bytes 786440 | tf_op jit(solution)/shard_map/ppermute | solution.py:23
  (10 other events, 157.3 us)

commit v3 on v2

--- a/solution.py
+++ b/solution.py
@@ -36,11 +36,14 @@
     return band_send(own, [(s, (s + 3) % bands) for s in range(bands)])
 
 
-def send_ring(own):
+def send_one(own):
     bands = lax.axis_size("band")
-    one = band_send(own, [(s, s + 1) for s in range(bands) if s % RING < 3])
-    two = band_send(own, [(s, s + 2) for s in range(bands) if s % RING < 2])
-    return one, two
+    return band_send(own, [(s, s + 1) for s in range(bands) if s % RING < 3])
+
+
+def send_two(one):
+    bands = lax.axis_size("band")
+    return band_send(one, [(s, s + 1) for s in range(bands) if s % RING in (1, 2)])
 
 
 def wrap_batches(one, two, three):
@@ -55,13 +58,13 @@
     return lax.dot_general(a, b, (((1,), (1,)), ((), ())), preferred_element_type=F32)
 
 
-def sum_gram(part, core, *gate):
+def sum_gram(part, core):
     rows = part.shape[0] // 2
     halves = part.reshape(2, rows, part.shape[1])
     keep = lax.dynamic_index_in_dim(halves, core, 0, keepdims=False)
     give = lax.dynamic_index_in_dim(halves, 1 - core, 0, keepdims=False)
     half = keep + mem_swap(give, 1)
-    half = half + after(mem_swap(half, 2), *gate)
+    half = half + mem_swap(half, 2)
     half = half + mem_swap(half, 4)
     return half, mem_swap(half, 1)
 
@@ -340,17 +343,19 @@
     ids = jnp.stack([core, low, high, mine]).astype(jnp.int32)
     pairs = [(t, s) for t in range(arrivals) for s in range(t + 1, arrivals)]
 
-    y_one, y_two = send_ring(obs_anom)
-    y_three = send_three(obs_anom)
-    half, other = sum_gram(dot_t(obs_anom, obs_anom), core, y_one, y_two, y_three)
+    y_one = send_one(obs_anom)
+    y_two = send_two(y_one)
+    half, other = sum_gram(dot_t(obs_anom, obs_anom), core)
+    y_three = send_three(after(obs_anom, half))
     weights = weigh(ids, half, other, innov, scale)
-    y = [obs_anom, *wrap_batches(y_one, y_two, y_three), y_three]
     w_three = send_three(weights)
-    w_one, w_two = send_ring(after(weights, y[1], y[2]))
+    w_one = send_one(after(weights, y_one))
+    w_two = send_two(after(w_one, y_two))
+    y = [obs_anom, *wrap_batches(y_one, y_two, after(y_three, weights)), y_three]
     give, keep = cross_halves(ids, state, y)
     w_three = after(w_three, w_one, w_two)
     w = [weights, *wrap_batches(w_one, w_two, w_three), w_three]
-    give, keep = halve(1, ids, keep, after(mem_swap(after(give, w_three), 1)))
+    give, keep = halve(1, ids, keep, mem_swap(after(give, w_three), 1))
     give, keep = halve(2, ids, keep, mem_swap(give, 2))
     cross_recv = mem_swap(give, 4)
 

time: 182 us -> 177 us (0.973)
  waiting for transfers between devices: 91.8 us -> 87.5 us
    ppermute x18, waiting for transfers between devices: 55.7 us -> 38.4 us  [mem_swap(): return lax.ppermute(value, 'mem', [(m, m ^ bit) for m in range(count)])]
    ppermute x10, waiting for transfers between devices: 36.1 us -> 49.1 us  [band_send(): return lax.ppermute(value, 'band', pairs)]
    ppermute x18, starting transfers between devices: 26 us -> 38.7 us  [mem_swap(): return lax.ppermute(value, 'mem', [(m, m ^ bit) for m in range(count)])]
    ppermute x10, starting transfers between devices: 30.4 us -> 18.8 us  [band_send(): return lax.ppermute(value, 'band', pairs)]
  transfers between devices with their start and end apart: 28 -> 28, of which waited for: 17 -> 18; matrix products, arithmetic and copies ran while one was open for 3% -> 2% of each run, Pallas kernels for 10% -> 10%
where the time goes in v3:
time: 177 us
  waiting for transfers between devices  87.5 us (49%)
  starting transfers between devices  57.5 us (32%)
  Pallas kernels  23.8 us (13%)
  local copies, waits for them, and re-layouts  3.09 us (2%)
  other arithmetic  2.96 us (2%)
    ppermute x10, waiting for transfers between devices, band_send(): return lax.ppermute(value, 'band', pairs)  49.1 us
    ppermute x18, starting transfers between devices, mem_swap(): return lax.ppermute(value, 'mem', [(m, m ^ bit) for m in range(count)])  38.7 us
    ppermute x18, waiting for transfers between devices, mem_swap(): return lax.ppermute(value, 'mem', [(m, m ^ bit) for m in range(count)])  38.4 us
    ppermute x10, starting transfers between devices, band_send(): return lax.ppermute(value, 'band', pairs)  18.8 us
    pallas_call x1, Pallas kernels, update_most(): pl.pallas_call(most_kernel, out_shape=shape((cells, width), F32), grid=(w...  5.86 us
    pallas_call x1, Pallas kernels, cross_halves(): pl.pallas_call(cross_kernel, out_shape=[shape((4, rows, num_obs), BF), sh...  4.57 us
    pallas_call x1, Pallas kernels, weigh(): pl.pallas_call(lambda *refs: weigh_kernel(scale, *refs), out_shape=shape(...  3.83 us
  transfers between devices with their start and end apart: 28, of which 18 were waited for; matrix products, arithmetic and copies ran while one was open for 2% of the time, Pallas kernels for 10%

profile of v3, /device:TPU:1, one launch (start us, length us, event | category | flops | bytes accessed | tf_op | source)
XLA Modules:
  0.0 176.7 jit_solution(915079203226394987)
XLA Ops:
  1.6 3.3 %collective-permute-start = (f32[128,256]{1,0:T(8,128)S(1)}, f32[128,256]{1,0:T(8,128)S(1)}, u32[]{:S(2)}, u32[]{:S(2)}) collective-permute-start(f32[128,256]{1,0:T(8,128)S(1)} %dynamic-slice_bitcast_fusion), channel_id=1, source_target_pairs={{0,1},{1,0},{2,3},{3,2},{4,5},{5,4},{6,7},{7,6},{8,9},{9,8},{10,11... | collective-permute-start | bytes 393224 | tf_op jit(solution)/shard_map/ppermute | solution.py:23
  6.1 4.7 %collective-permute-done.1 = f32[128,256]{1,0:T(8,128)S(1)} collective-permute-done((f32[128,256]{1,0:T(8,128)S(1)}, f32[128,256]{1,0:T(8,128)S(1)}, u32[]{:S(2)}, u32[]{:S(2)}) %collective-permute-start.1) | collective-permute-done | bytes 131104 | tf_op jit(solution)/shard_map/ppermute | solution.py:23
  12.5 4.0 %collective-permute-start.6 = (bf16[256,1024]{1,0:T(8,128)(2,1)}, bf16[256,1024]{1,0:T(8,128)(2,1)}, u32[]{:S(2)}, u32[]{:S(2)}) collective-permute-start(bf16[256,1024]{1,0:T(8,128)(2,1)} %refs_6_.1), channel_id=1, source_target_pairs={{0,8},{8,16},{16,24},{32,40},{40,48},{48,56},{64,72},{72,80},{80,8... | collective-permute-start | bytes 1572872 | tf_op jit(solution)/shard_map/ppermute | solution.py:27
  16.5 3.2 %collective-permute-done.2 = f32[128,256]{1,0:T(8,128)S(1)} collective-permute-done((f32[128,256]{1,0:T(8,128)S(1)}, f32[128,256]{1,0:T(8,128)S(1)}, u32[]{:S(2)}, u32[]{:S(2)}) %collective-permute-start.2) | collective-permute-done | bytes 131104 | tf_op jit(solution)/shard_map/ppermute | solution.py:23
  25.1 3.8 %weigh.1.refs_2_.refs_4_.w0_ref = bf16[256,1024]{1,0:T(8,128)(2,1)S(1)} custom-call(s32[4]{0:T(128)S(1)} %pad_add_fusion.refs_0_.ids_ref, f32[128,256]{1,0:T(8,128)S(1)} %add.52.refs_1_, f32[128,256]{1,0:T(8,128)S(1)} %collective-permute-done.4.refs_2_, f32[256,1024]{1,0:T(8,128)S(1)} %copy-done.1), custom_call_target="tpu_custom_call" | custom-call | tf_op jit(solution)/shard_map/weigh/pallas_call | solution.py:141
  28.9 6.8 %collective-permute-start.10 = (bf16[256,1024]{1,0:T(8,128)(2,1)S(1)}, bf16[256,1024]{1,0:T(8,128)(2,1)S(1)}, u32[]{:S(2)}, u32[]{:S(2)}) collective-permute-start(bf16[256,1024]{1,0:T(8,128)(2,1)S(1)} %weigh.1.refs_2_.refs_4_.w0_ref), channel_id=1, source_target_pairs={{0,8},{8,16},{16,24},{32,40},{40,48},{48,56},{64,72},{72,80},{80,8... | collective-permute-start | bytes 1572872 | tf_op jit(solution)/shard_map/ppermute | solution.py:27
  36.4 14.4 %collective-permute-done.3.y3_ref.refs_9_ = bf16[256,1024]{1,0:T(8,128)(2,1)S(1)} collective-permute-done((bf16[256,1024]{1,0:T(8,128)(2,1)}, bf16[256,1024]{1,0:T(8,128)(2,1)S(1)}, u32[]{:S(2)}, u32[]{:S(2)}) %collective-permute-start.3) | collective-permute-done | bytes 524320 | tf_op jit(solution)/shard_map/ppermute | solution.py:27
  54.3 18.0 %collective-permute-done.5 = bf16[256,1024]{1,0:T(8,128)(2,1)} collective-permute-done((bf16[256,1024]{1,0:T(8,128)(2,1)S(1)}, bf16[256,1024]{1,0:T(8,128)(2,1)}, u32[]{:S(2)}, u32[]{:S(2)}) %collective-permute-start.5) | collective-permute-done | bytes 524320 | tf_op jit(solution)/shard_map/ppermute | solution.py:27
  74.6 4.6 %cross.1 = (bf16[4,512,256]{2,1,0:T(8,128)(2,1)S(1)}, f32[4,512,256]{2,1,0:T(8,128)S(1)}) custom-call(s32[4]{0:T(128)S(1)} %pad_add_fusion.refs_0_.ids_ref, f32[1024,1024]{1,0:T(8,128)} %x_ref.5, bf16[256,1024]{1,0:T(8,128)(2,1)S(1)} %copy-done, bf16[256,1024]{1,0:T(8,128)(2,1)S(1)} %broadcast_select_fusion.3.y1_ref.refs_7_, ...), custom_call_target="tpu_custom_call" | custom-call | tf_op jit(solution)/shard_map/cross/pallas_call | solution.py:166
  85.0 12.4 %collective-permute-done.16 = bf16[256,1024]{1,0:T(8,128)(2,1)S(1)} collective-permute-done((bf16[256,1024]{1,0:T(8,128)(2,1)S(1)}, bf16[256,1024]{1,0:T(8,128)(2,1)S(1)}, u32[]{:S(2)}, u32[]{:S(2)}) %collective-permute-start.16) | collective-permute-done | bytes 524320 | tf_op jit(solution)/shard_map/ppermute | solution.py:27
  97.4 3.1 %collective-permute-done.15 = bf16[256,1024]{1,0:T(8,128)(2,1)S(1)} collective-permute-done((bf16[256,1024]{1,0:T(8,128)(2,1)S(1)}, bf16[256,1024]{1,0:T(8,128)(2,1)S(1)}, u32[]{:S(2)}, u32[]{:S(2)}) %collective-permute-start.15) | collective-permute-done | bytes 524320 | tf_op jit(solution)/shard_map/ppermute | solution.py:27
  100.6 2.5 %link.1 = (bf16[1,768,256]{2,1,0:T(8,128)(2,1)S(1)}, f32[1,768,256]{2,1,0:T(8,128)S(1)}) custom-call(s32[4]{0:T(128)S(1)} %pad_add_fusion.refs_0_.ids_ref, s32[1,4]{1,0:T(1,128)S(1)} %copy-done.4, bf16[256,1024]{1,0:T(8,128)(2,1)S(1)} %weigh.1.refs_2_.refs_4_.w0_ref, bf16[256,1024]{1,0:T(8,128)(2,1)S(1)} %broadcast_select_fusion.2.refs_3_.refs_5_.w1_ref, ...), custom_call_target="tpu_custom_call" | custom-call | tf_op jit(solution)/shard_map/link/pallas_call | solution.py:222
  107.0 6.0 %collective-permute-start.18 = (bf16[1,384,256]{2,1,0:T(8,128)(2,1)S(1)}, bf16[1,384,256]{2,1,0:T(8,128)(2,1)S(1)}, u32[]{:S(2)}, u32[]{:S(2)}) collective-permute-start(bf16[1,384,256]{2,1,0:T(8,128)(2,1)S(1)} %get-tuple-element.42), channel_id=1, source_target_pairs={{0,2},{1,3},{2,0},{3,1},{4,6},{5,7},{6,4},{7,5},{8,10},{9,11},{10,... | collective-permute-start | bytes 589832 | tf_op jit(solution)/shard_map/ppermute | solution.py:23
  113.0 6.0 %collective-permute-done.14.refs_3_ = bf16[4,128,256]{2,1,0:T(8,128)(2,1)S(1)} collective-permute-done((bf16[4,128,256]{2,1,0:T(8,128)(2,1)S(1)}, bf16[4,128,256]{2,1,0:T(8,128)(2,1)S(1)}, u32[]{:S(2)}, u32[]{:S(2)}) %collective-permute-start.14) | collective-permute-done | bytes 262176 | tf_op jit(solution)/shard_map/ppermute | solution.py:23
  120.3 4.7 %collective-permute-start.19 = (bf16[1,192,256]{2,1,0:T(8,128)(2,1)S(1)}, bf16[1,192,256]{2,1,0:T(8,128)(2,1)S(1)}, u32[]{:S(2)}, u32[]{:S(2)}) collective-permute-start(bf16[1,192,256]{2,1,0:T(8,128)(2,1)S(1)} %get-tuple-element.45), channel_id=1, source_target_pairs={{0,4},{1,5},{2,6},{3,7},{4,0},{5,1},{6,2},{7,3},{8,12},{9,13},{10,... | collective-permute-start | bytes 294920 | tf_op jit(solution)/shard_map/ppermute | solution.py:23
  125.0 2.7 %collective-permute-done.19 = bf16[1,192,256]{2,1,0:T(8,128)(2,1)S(1)} collective-permute-done((bf16[1,192,256]{2,1,0:T(8,128)(2,1)S(1)}, bf16[1,192,256]{2,1,0:T(8,128)(2,1)S(1)}, u32[]{:S(2)}, u32[]{:S(2)}) %collective-permute-start.19) | collective-permute-done | bytes 98336 | tf_op jit(solution)/shard_map/ppermute | solution.py:23
  129.9 2.3 %collective-permute-done.20 = bf16[1,192,256]{2,1,0:T(8,128)(2,1)S(1)} collective-permute-done((bf16[1,192,256]{2,1,0:T(8,128)(2,1)S(1)}, bf16[1,192,256]{2,1,0:T(8,128)(2,1)S(1)}, u32[]{:S(2)}, u32[]{:S(2)}) %collective-permute-start.20) | collective-permute-done | bytes 98336 | tf_op jit(solution)/shard_map/ppermute | solution.py:23
  132.3 4.6 %collective-permute-start.21 = (bf16[2,1,192,256]{3,2,1,0:T(8,128)(2,1)S(1)}, bf16[2,1,192,256]{3,2,1,0:T(8,128)(2,1)S(1)}, u32[]{:S(2)}, u32[]{:S(2)}) collective-permute-start(bf16[2,1,192,256]{3,2,1,0:T(8,128)(2,1)S(1)} %pad_maximum_fusion.2), channel_id=1, source_target_pairs={{0,2},{1,3},{2,0},{3,1},{4,6},{5,7},{6,4},{7,5},{8,10},{9,11},{10,... | collective-permute-start | bytes 589832 | tf_op jit(solution)/shard_map/ppermute | solution.py:23
  136.9 3.1 %collective-permute-done.21 = bf16[2,1,192,256]{3,2,1,0:T(8,128)(2,1)S(1)} collective-permute-done((bf16[2,1,192,256]{3,2,1,0:T(8,128)(2,1)S(1)}, bf16[2,1,192,256]{3,2,1,0:T(8,128)(2,1)S(1)}, u32[]{:S(2)}, u32[]{:S(2)}) %collective-permute-start.21) | collective-permute-done | bytes 196640 | tf_op jit(solution)/shard_map/ppermute | solution.py:23
  140.0 4.5 %collective-permute-start.22 = (bf16[4,1,192,256]{3,2,1,0:T(8,128)(2,1)S(1)}, bf16[4,1,192,256]{3,2,1,0:T(8,128)(2,1)S(1)}, u32[]{:S(2)}, u32[]{:S(2)}) collective-permute-start(bf16[4,1,192,256]{3,2,1,0:T(8,128)(2,1)S(1)} %pad_maximum_fusion.1.refs_4_), channel_id=1, source_target_pairs={{0,1},{1,0},{2,3},{3,2},{4,5},{5,4},{6,7},{7,6},{8,9},{9,8},{10,11... | collective-permute-start | bytes 1179656 | tf_op jit(solution)/shard_map/ppermute | solution.py:23
  149.8 10.5 %collective-permute-done.25.refs_2_ = bf16[4,128,256]{2,1,0:T(8,128)(2,1)S(1)} collective-permute-done((bf16[4,128,256]{2,1,0:T(8,128)(2,1)S(1)}, bf16[4,128,256]{2,1,0:T(8,128)(2,1)S(1)}, u32[]{:S(2)}, u32[]{:S(2)}) %collective-permute-start.25) | collective-permute-done | bytes 262176 | tf_op jit(solution)/shard_map/ppermute | solution.py:23
  160.3 3.1 %collective-permute-start.26 = (bf16[3,4,128,256]{3,2,1,0:T(8,128)(2,1)S(1)}, bf16[3,4,128,256]{3,2,1,0:T(8,128)(2,1)S(1)}, u32[]{:S(2)}, u32[]{:S(2)}) collective-permute-start(bf16[3,4,128,256]{3,2,1,0:T(8,128)(2,1)S(1)} %pad_maximum_fusion), channel_id=1, source_target_pairs={{0,1},{1,0},{2,3},{3,2},{4,5},{5,4},{6,7},{7,6},{8,9},{9,8},{10,11... | collective-permute-start | bytes 2359304 | tf_op jit(solution)/shard_map/ppermute | solution.py:23
  165.4 5.9 %update_most.1._ = f32[1024,1024]{1,0:T(8,128)} custom-call(s32[4]{0:T(128)S(1)} %pad_add_fusion.refs_0_.ids_ref, f32[1024,1024]{1,0:T(8,128)} %x_ref.5, bf16[4,128,256]{2,1,0:T(8,128)(2,1)S(1)} %solve.1.refs_0_, bf16[4,128,256]{2,1,0:T(8,128)(2,1)S(1)} %collective-permute-done.23.refs_1_, bf16[4,128,256]{2,1,0:T(8,128)(2,1)S(1)} %collective-permute-done.25.refs_2_, ...), custom_call_target="tpu_custom_call" | custom-call | tf_op jit(solution)/shard_map/update_most/pallas_call | solution.py:286
  173.4 3.4 %update_rest.1 = f32[1024,1024]{1,0:T(8,128)} custom-call(s32[4]{0:T(128)S(1)} %pad_add_fusion.refs_0_.ids_ref, f32[1024,1024]{1,0:T(8,128)} %x_ref.5, bf16[4,128,256]{2,1,0:T(8,128)(2,1)S(1)} %collective-permute-done.24.near_ref, bf16[4,128,256]{2,1,0:T(8,128)(2,1)S(1)} %collective-permute-done.27.far_ref, ...), custom_call_target="tpu_custom_call", output_to_operand_aliasing={{}: (8, {})} | custom-call | tf_op jit(solution)/shard_map/update_rest/pallas_call | solution.py:314
  (81 shorter events, 38.8 us)
Async XLA Ops:
  1.6 4.3 %collective-permute-start = (f32[128,256]{1,0:T(8,128)S(1)}, f32[128,256]{1,0:T(8,128)S(1)}, u32[]{:S(2)}, u32[]{:S(2)}) collective-permute-start(f32[128,256]{1,0:T(8,128)S(1)} %dynamic-slice_bitcast_fusion), channel_id=1, source_target_pairs={{0,1},{1,0},{2,3},{3,2},{4,5},{5,4},{6,7},{7,6},{8,9},{9,8},{10,11... | collective-permute-start | bytes 393224 | tf_op jit(solution)/shard_map/ppermute | solution.py:23
  6.0 4.8 %collective-permute-start.1 = (f32[128,256]{1,0:T(8,128)S(1)}, f32[128,256]{1,0:T(8,128)S(1)}, u32[]{:S(2)}, u32[]{:S(2)}) collective-permute-start(f32[128,256]{1,0:T(8,128)S(1)} %bitcast_add_fusion), channel_id=1, source_target_pairs={{0,2},{1,3},{2,0},{3,1},{4,6},{5,7},{6,4},{7,5},{8,10},{9,11},{10,... | collective-permute-start | bytes 393224 | tf_op jit(solution)/shard_map/ppermute | solution.py:23
  10.8 8.9 %collective-permute-start.2 = (f32[128,256]{1,0:T(8,128)S(1)}, f32[128,256]{1,0:T(8,128)S(1)}, u32[]{:S(2)}, u32[]{:S(2)}) collective-permute-start(f32[128,256]{1,0:T(8,128)S(1)} %add.51), channel_id=1, source_target_pairs={{0,4},{1,5},{2,6},{3,7},{4,0},{5,1},{6,2},{7,3},{8,12},{9,13},{10,... | collective-permute-start | bytes 393224 | tf_op jit(solution)/shard_map/ppermute | solution.py:23
  12.5 16.4 %collective-permute-start.6 = (bf16[256,1024]{1,0:T(8,128)(2,1)}, bf16[256,1024]{1,0:T(8,128)(2,1)}, u32[]{:S(2)}, u32[]{:S(2)}) collective-permute-start(bf16[256,1024]{1,0:T(8,128)(2,1)} %refs_6_.1), channel_id=1, source_target_pairs={{0,8},{8,16},{16,24},{32,40},{40,48},{48,56},{64,72},{72,80},{80,8... | collective-permute-start | bytes 1572872 | tf_op jit(solution)/shard_map/ppermute | solution.py:27
  19.7 31.2 %collective-permute-start.3 = (bf16[256,1024]{1,0:T(8,128)(2,1)}, bf16[256,1024]{1,0:T(8,128)(2,1)S(1)}, u32[]{:S(2)}, u32[]{:S(2)}) collective-permute-start(bf16[256,1024]{1,0:T(8,128)(2,1)} %refs_6_.1), channel_id=1, source_target_pairs={{0,24},{8,32},{16,40},{24,48},{32,56},{40,64},{48,72},{56,80},{64,... | collective-permute-start | bytes 1572872 | tf_op jit(solution)/shard_map/ppermute | solution.py:27
  28.9 24.6 %collective-permute-start.10 = (bf16[256,1024]{1,0:T(8,128)(2,1)S(1)}, bf16[256,1024]{1,0:T(8,128)(2,1)S(1)}, u32[]{:S(2)}, u32[]{:S(2)}) collective-permute-start(bf16[256,1024]{1,0:T(8,128)(2,1)S(1)} %weigh.1.refs_2_.refs_4_.w0_ref), channel_id=1, source_target_pairs={{0,8},{8,16},{16,24},{32,40},{40,48},{48,56},{64,72},{72,80},{80,8... | collective-permute-start | bytes 1572872 | tf_op jit(solution)/shard_map/ppermute | solution.py:27
  35.7 17.9 %collective-permute-start.8 = (bf16[256,1024]{1,0:T(8,128)(2,1)}, bf16[256,1024]{1,0:T(8,128)(2,1)S(1)}, u32[]{:S(2)}, u32[]{:S(2)}) collective-permute-start(bf16[256,1024]{1,0:T(8,128)(2,1)} %collective-permute-done.6), channel_id=1, source_target_pairs={{8,16},{16,24},{40,48},{48,56},{72,80},{80,88},{104,112},{112,120}... | collective-permute-start | bytes 1572872 | tf_op jit(solution)/shard_map/ppermute | solution.py:27
  50.9 21.5 %collective-permute-start.5 = (bf16[256,1024]{1,0:T(8,128)(2,1)S(1)}, bf16[256,1024]{1,0:T(8,128)(2,1)}, u32[]{:S(2)}, u32[]{:S(2)}) collective-permute-start(bf16[256,1024]{1,0:T(8,128)(2,1)S(1)} %collective-permute-done.3.y3_ref.refs_9_), channel_id=1, source_target_pairs={{16,0},{48,32},{80,64},{112,96},{144,128},{176,160},{208,192},{240... | collective-permute-start | bytes 1572872 | tf_op jit(solution)/shard_map/ppermute | solution.py:27
  52.2 21.3 %collective-permute-start.7 = (bf16[256,1024]{1,0:T(8,128)(2,1)S(1)}, bf16[256,1024]{1,0:T(8,128)(2,1)}, u32[]{:S(2)}, u32[]{:S(2)}) collective-permute-start(bf16[256,1024]{1,0:T(8,128)(2,1)S(1)} %collective-permute-done.3.y3_ref.refs_9_), channel_id=1, source_target_pairs={{8,0},{16,8},{40,32},{48,40},{72,64},{80,72},{104,96},{112,104},{1... | collective-permute-start | bytes 1572872 | tf_op jit(solution)/shard_map/ppermute | solution.py:27
  53.5 26.8 %collective-permute-start.9 = (bf16[256,1024]{1,0:T(8,128)(2,1)S(1)}, bf16[256,1024]{1,0:T(8,128)(2,1)S(1)}, u32[]{:S(2)}, u32[]{:S(2)}) collective-permute-start(bf16[256,1024]{1,0:T(8,128)(2,1)S(1)} %weigh.1.refs_2_.refs_4_.w0_ref), channel_id=1, source_target_pairs={{0,24},{8,32},{16,40},{24,48},{32,56},{40,64},{48,72},{56,80},{64,... | collective-permute-start | bytes 1572872 | tf_op jit(solution)/shard_map/ppermute | solution.py:27
  53.6 26.7 %collective-permute-start.11 = (bf16[256,1024]{1,0:T(8,128)(2,1)S(1)}, bf16[256,1024]{1,0:T(8,128)(2,1)S(1)}, u32[]{:S(2)}, u32[]{:S(2)}) collective-permute-start(bf16[256,1024]{1,0:T(8,128)(2,1)S(1)} %collective-permute-done.10), channel_id=1, source_target_pairs={{8,16},{16,24},{40,48},{48,56},{72,80},{80,88},{104,112},{112,120}... | collective-permute-start | bytes 1572872 | tf_op jit(solution)/shard_map/ppermute | solution.py:27
  81.3 16.1 %collective-permute-start.16 = (bf16[256,1024]{1,0:T(8,128)(2,1)S(1)}, bf16[256,1024]{1,0:T(8,128)(2,1)S(1)}, u32[]{:S(2)}, u32[]{:S(2)}) collective-permute-start(bf16[256,1024]{1,0:T(8,128)(2,1)S(1)} %collective-permute-done.9.refs_5_.refs_7_.w3_ref), channel_id=1, source_target_pairs={{8,0},{16,8},{40,32},{48,40},{72,64},{80,72},{104,96},{112,104},{1... | collective-permute-start | bytes 1572872 | tf_op jit(solution)/shard_map/ppermute | solution.py:27
  82.6 17.9 %collective-permute-start.15 = (bf16[256,1024]{1,0:T(8,128)(2,1)S(1)}, bf16[256,1024]{1,0:T(8,128)(2,1)S(1)}, u32[]{:S(2)}, u32[]{:S(2)}) collective-permute-start(bf16[256,1024]{1,0:T(8,128)(2,1)S(1)} %collective-permute-done.9.refs_5_.refs_7_.w3_ref), channel_id=1, source_target_pairs={{16,0},{48,32},{80,64},{112,96},{144,128},{176,160},{208,192},{240... | collective-permute-start | bytes 1572872 | tf_op jit(solution)/shard_map/ppermute | solution.py:27
  84.7 18.4 %collective-permute-start.13 = (bf16[4,256,256]{2,1,0:T(8,128)(2,1)S(1)}, bf16[4,256,256]{2,1,0:T(8,128)(2,1)S(1)}, u32[]{:S(2)}, u32[]{:S(2)}) collective-permute-start(bf16[4,256,256]{2,1,0:T(8,128)(2,1)S(1)} %get-tuple-element.35), channel_id=1, source_target_pairs={{0,2},{1,3},{2,0},{3,1},{4,6},{5,7},{6,4},{7,5},{8,10},{9,11},{10,... | collective-permute-start | bytes 1572872 | tf_op jit(solution)/shard_map/ppermute | solution.py:23
  104.7 14.3 %collective-permute-start.14 = (bf16[4,128,256]{2,1,0:T(8,128)(2,1)S(1)}, bf16[4,128,256]{2,1,0:T(8,128)(2,1)S(1)}, u32[]{:S(2)}, u32[]{:S(2)}) collective-permute-start(bf16[4,128,256]{2,1,0:T(8,128)(2,1)S(1)} %get-tuple-element.37), channel_id=1, source_target_pairs={{0,4},{1,5},{2,6},{3,7},{4,0},{5,1},{6,2},{7,3},{8,12},{9,13},{10,... | collective-permute-start | bytes 786440 | tf_op jit(solution)/shard_map/ppermute | solution.py:23
  107.0 12.7 %collective-permute-start.18 = (bf16[1,384,256]{2,1,0:T(8,128)(2,1)S(1)}, bf16[1,384,256]{2,1,0:T(8,128)(2,1)S(1)}, u32[]{:S(2)}, u32[]{:S(2)}) collective-permute-start(bf16[1,384,256]{2,1,0:T(8,128)(2,1)S(1)} %get-tuple-element.42), channel_id=1, source_target_pairs={{0,2},{1,3},{2,0},{3,1},{4,6},{5,7},{6,4},{7,5},{8,10},{9,11},{10,... | collective-permute-start | bytes 589832 | tf_op jit(solution)/shard_map/ppermute | solution.py:23
  120.3 7.5 %collective-permute-start.19 = (bf16[1,192,256]{2,1,0:T(8,128)(2,1)S(1)}, bf16[1,192,256]{2,1,0:T(8,128)(2,1)S(1)}, u32[]{:S(2)}, u32[]{:S(2)}) collective-permute-start(bf16[1,192,256]{2,1,0:T(8,128)(2,1)S(1)} %get-tuple-element.45), channel_id=1, source_target_pairs={{0,4},{1,5},{2,6},{3,7},{4,0},{5,1},{6,2},{7,3},{8,12},{9,13},{10,... | collective-permute-start | bytes 294920 | tf_op jit(solution)/shard_map/ppermute | solution.py:23
  127.8 4.5 %collective-permute-start.20 = (bf16[1,192,256]{2,1,0:T(8,128)(2,1)S(1)}, bf16[1,192,256]{2,1,0:T(8,128)(2,1)S(1)}, u32[]{:S(2)}, u32[]{:S(2)}) collective-permute-start(bf16[1,192,256]{2,1,0:T(8,128)(2,1)S(1)} %add_convert_fusion), channel_id=1, source_target_pairs={{0,4},{1,5},{2,6},{3,7},{4,0},{5,1},{6,2},{7,3},{8,12},{9,13},{10,... | collective-permute-start | bytes 294920 | tf_op jit(solution)/shard_map/ppermute | solution.py:23
  132.3 7.7 %collective-permute-start.21 = (bf16[2,1,192,256]{3,2,1,0:T(8,128)(2,1)S(1)}, bf16[2,1,192,256]{3,2,1,0:T(8,128)(2,1)S(1)}, u32[]{:S(2)}, u32[]{:S(2)}) collective-permute-start(bf16[2,1,192,256]{3,2,1,0:T(8,128)(2,1)S(1)} %pad_maximum_fusion.2), channel_id=1, source_target_pairs={{0,2},{1,3},{2,0},{3,1},{4,6},{5,7},{6,4},{7,5},{8,10},{9,11},{10,... | collective-permute-start | bytes 589832 | tf_op jit(solution)/shard_map/ppermute | solution.py:23
  140.0 5.8 %collective-permute-start.22 = (bf16[4,1,192,256]{3,2,1,0:T(8,128)(2,1)S(1)}, bf16[4,1,192,256]{3,2,1,0:T(8,128)(2,1)S(1)}, u32[]{:S(2)}, u32[]{:S(2)}) collective-permute-start(bf16[4,1,192,256]{3,2,1,0:T(8,128)(2,1)S(1)} %pad_maximum_fusion.1.refs_4_), channel_id=1, source_target_pairs={{0,1},{1,0},{2,3},{3,2},{4,5},{5,4},{6,7},{7,6},{8,9},{9,8},{10,11... | collective-permute-start | bytes 1179656 | tf_op jit(solution)/shard_map/ppermute | solution.py:23
  147.8 12.4 %collective-permute-start.25 = (bf16[4,128,256]{2,1,0:T(8,128)(2,1)S(1)}, bf16[4,128,256]{2,1,0:T(8,128)(2,1)S(1)}, u32[]{:S(2)}, u32[]{:S(2)}) collective-permute-start(bf16[4,128,256]{2,1,0:T(8,128)(2,1)S(1)} %solve.1.refs_0_), channel_id=1, source_target_pairs={{0,2},{1,3},{2,0},{3,1},{4,6},{5,7},{6,4},{7,5},{8,10},{9,11},{10,... | collective-permute-start | bytes 786440 | tf_op jit(solution)/shard_map/ppermute | solution.py:23
  147.9 12.3 %collective-permute-start.23 = (bf16[4,128,256]{2,1,0:T(8,128)(2,1)S(1)}, bf16[4,128,256]{2,1,0:T(8,128)(2,1)S(1)}, u32[]{:S(2)}, u32[]{:S(2)}) collective-permute-start(bf16[4,128,256]{2,1,0:T(8,128)(2,1)S(1)} %solve.1.refs_0_), channel_id=1, source_target_pairs={{0,4},{1,5},{2,6},{3,7},{4,0},{5,1},{6,2},{7,3},{8,12},{9,13},{10,... | collective-permute-start | bytes 786440 | tf_op jit(solution)/shard_map/ppermute | solution.py:23
  160.3 5.0 %collective-permute-start.26 = (bf16[3,4,128,256]{3,2,1,0:T(8,128)(2,1)S(1)}, bf16[3,4,128,256]{3,2,1,0:T(8,128)(2,1)S(1)}, u32[]{:S(2)}, u32[]{:S(2)}) collective-permute-start(bf16[3,4,128,256]{3,2,1,0:T(8,128)(2,1)S(1)} %pad_maximum_fusion), channel_id=1, source_target_pairs={{0,1},{1,0},{2,3},{3,2},{4,5},{5,4},{6,7},{7,6},{8,9},{9,8},{10,11... | collective-permute-start | bytes 2359304 | tf_op jit(solution)/shard_map/ppermute | solution.py:23
  163.5 7.9 %collective-permute-start.24 = (bf16[4,128,256]{2,1,0:T(8,128)(2,1)S(1)}, bf16[4,128,256]{2,1,0:T(8,128)(2,1)S(1)}, u32[]{:S(2)}, u32[]{:S(2)}) collective-permute-start(bf16[4,128,256]{2,1,0:T(8,128)(2,1)S(1)} %collective-permute-done.23.refs_1_), channel_id=1, source_target_pairs={{0,2},{1,3},{2,0},{3,1},{4,6},{5,7},{6,4},{7,5},{8,10},{9,11},{10,... | collective-permute-start | bytes 786440 | tf_op jit(solution)/shard_map/ppermute | solution.py:23
  (14 other events, 282.5 us)

commit v4 on v3

--- a/solution.py
+++ b/solution.py
@@ -46,12 +46,16 @@
     return band_send(one, [(s, s + 1) for s in range(bands) if s % RING in (1, 2)])
 
 
-def wrap_batches(one, two, three):
+def send_wraps(three):
     bands = lax.axis_size("band")
+    two = band_send(three, [(s, s - 1) for s in range(bands) if s % RING in (1, 2)])
+    one = band_send(three, [(s, s - 2) for s in range(bands) if s % RING == 2])
+    return one, two
+
+
+def pick_batches(one, two, one_wrap, two_wrap):
     y = lax.axis_index("band") % RING
-    two_wrap = band_send(three, [(s, s - 1) for s in range(bands) if s % RING in (1, 2)])
-    one_wrap = band_send(three, [(s, s - 2) for s in range(bands) if s % RING == 2])
-    return jnp.where(y < 1, one_wrap, one), jnp.where(y < 2, two_wrap, two)
+    return [jnp.where(y < 1, one_wrap, one), jnp.where(y < 2, two_wrap, two)]
 
 
 def dot_t(a, b):
@@ -351,16 +355,19 @@
     w_three = send_three(weights)
     w_one = send_one(after(weights, y_one))
     w_two = send_two(after(w_one, y_two))
-    y = [obs_anom, *wrap_batches(y_one, y_two, after(y_three, weights)), y_three]
+    y_wraps = send_wraps(after(y_three, weights))
+    y = [obs_anom, *pick_batches(y_one, y_two, *y_wraps), y_three]
     give, keep = cross_halves(ids, state, y)
     w_three = after(w_three, w_one, w_two)
-    w = [weights, *wrap_batches(w_one, w_two, w_three), w_three]
+    one_wrap, two_wrap = send_wraps(w_three)
     give, keep = halve(1, ids, keep, mem_swap(after(give, w_three), 1))
+    w_wraps = after(one_wrap, give), after(two_wrap, give)
+    w = [weights, *pick_batches(w_one, w_two, *w_wraps), w_three]
     give, keep = halve(2, ids, keep, mem_swap(give, 2))
     cross_recv = mem_swap(give, 4)
 
     link_give, link_keep = link_halves(ids, order, w, y, pairs)
-    link_give, link_keep = halve(1, ids, link_keep, mem_swap(after(link_give, give), 1))
+    link_give, link_keep = halve(1, ids, link_keep, after(mem_swap(link_give, 1), give))
     link_recv = after(mem_swap(link_give, 2), cross_recv)
     link_give, link_keep = halve(2, ids, link_keep, link_recv)
     link = (link_keep + mem_swap(link_give, 4).astype(F32)).astype(BF)

time: 177 us -> 176 us (level)
  starting transfers between devices: 57.5 us -> 54.5 us
  waiting for transfers between devices: 87.5 us -> 90.5 us
    ppermute x18, starting transfers between devices: 38.7 us -> 35.5 us  [mem_swap(): return lax.ppermute(value, 'mem', [(m, m ^ bit) for m in range(count)])]
    ppermute x18, waiting for transfers between devices: 38.4 us -> 40.2 us  [mem_swap(): return lax.ppermute(value, 'mem', [(m, m ^ bit) for m in range(count)])]
  transfers between devices with their start and end apart: 28 -> 28, of which waited for: 18 -> 20; matrix products, arithmetic and copies ran while one was open for 2% -> 1% of each run, Pallas kernels for 10% -> 11%
where the time goes in v4:
time: 176 us
  waiting for transfers between devices  90.5 us (51%)
  starting transfers between devices  54.5 us (31%)
  Pallas kernels  23.7 us (13%)
  local copies, waits for them, and re-layouts  3.08 us (2%)
  other arithmetic  1.94 us (1%)
    ppermute x10, waiting for transfers between devices, band_send(): return lax.ppermute(value, 'band', pairs)  50.3 us
    ppermute x18, waiting for transfers between devices, mem_swap(): return lax.ppermute(value, 'mem', [(m, m ^ bit) for m in range(count)])  40.2 us
    ppermute x18, starting transfers between devices, mem_swap(): return lax.ppermute(value, 'mem', [(m, m ^ bit) for m in range(count)])  35.5 us
    ppermute x10, starting transfers between devices, band_send(): return lax.ppermute(value, 'band', pairs)  19.1 us
    pallas_call x1, Pallas kernels, update_most(): pl.pallas_call(most_kernel, out_shape=shape((cells, width), F32), grid=(w...  5.86 us
    pallas_call x1, Pallas kernels, cross_halves(): pl.pallas_call(cross_kernel, out_shape=[shape((4, rows, num_obs), BF), sh...  4.57 us
    pallas_call x1, Pallas kernels, weigh(): pl.pallas_call(lambda *refs: weigh_kernel(scale, *refs), out_shape=shape(...  3.83 us
  transfers between devices with their start and end apart: 28, of which 20 were waited for; matrix products, arithmetic and copies ran while one was open for 1% of the time, Pallas kernels for 11%

profile of v4, /device:TPU:1, one launch (start us, length us, event | category | flops | bytes accessed | tf_op | source)
XLA Modules:
  0.0 175.7 jit_solution(494491005375169361)
XLA Ops:
  1.6 3.3 %collective-permute-start = (f32[128,256]{1,0:T(8,128)S(1)}, f32[128,256]{1,0:T(8,128)S(1)}, u32[]{:S(2)}, u32[]{:S(2)}) collective-permute-start(f32[128,256]{1,0:T(8,128)S(1)} %dynamic-slice_bitcast_fusion), channel_id=1, source_target_pairs={{0,1},{1,0},{2,3},{3,2},{4,5},{5,4},{6,7},{7,6},{8,9},{9,8},{10,11... | collective-permute-start | bytes 393224 | tf_op jit(solution)/shard_map/ppermute | solution.py:23
  6.1 4.7 %collective-permute-done.1 = f32[128,256]{1,0:T(8,128)S(1)} collective-permute-done((f32[128,256]{1,0:T(8,128)S(1)}, f32[128,256]{1,0:T(8,128)S(1)}, u32[]{:S(2)}, u32[]{:S(2)}) %collective-permute-start.1) | collective-permute-done | bytes 131104 | tf_op jit(solution)/shard_map/ppermute | solution.py:23
  12.5 4.0 %collective-permute-start.6 = (bf16[256,1024]{1,0:T(8,128)(2,1)}, bf16[256,1024]{1,0:T(8,128)(2,1)}, u32[]{:S(2)}, u32[]{:S(2)}) collective-permute-start(bf16[256,1024]{1,0:T(8,128)(2,1)} %refs_6_.1), channel_id=1, source_target_pairs={{0,8},{8,16},{16,24},{32,40},{40,48},{48,56},{64,72},{72,80},{80,8... | collective-permute-start | bytes 1572872 | tf_op jit(solution)/shard_map/ppermute | solution.py:27
  16.5 3.2 %collective-permute-done.2 = f32[128,256]{1,0:T(8,128)S(1)} collective-permute-done((f32[128,256]{1,0:T(8,128)S(1)}, f32[128,256]{1,0:T(8,128)S(1)}, u32[]{:S(2)}, u32[]{:S(2)}) %collective-permute-start.2) | collective-permute-done | bytes 131104 | tf_op jit(solution)/shard_map/ppermute | solution.py:23
  25.1 3.8 %weigh.1.refs_2_.refs_4_.w0_ref = bf16[256,1024]{1,0:T(8,128)(2,1)S(1)} custom-call(s32[4]{0:T(128)S(1)} %pad_add_fusion.refs_0_.ids_ref, f32[128,256]{1,0:T(8,128)S(1)} %add.52.refs_1_, f32[128,256]{1,0:T(8,128)S(1)} %collective-permute-done.4.refs_2_, f32[256,1024]{1,0:T(8,128)S(1)} %copy-done.1), custom_call_target="tpu_custom_call" | custom-call | tf_op jit(solution)/shard_map/weigh/pallas_call | solution.py:145
  28.9 7.1 %collective-permute-start.10 = (bf16[256,1024]{1,0:T(8,128)(2,1)S(1)}, bf16[256,1024]{1,0:T(8,128)(2,1)}, u32[]{:S(2)}, u32[]{:S(2)}) collective-permute-start(bf16[256,1024]{1,0:T(8,128)(2,1)S(1)} %weigh.1.refs_2_.refs_4_.w0_ref), channel_id=1, source_target_pairs={{0,8},{8,16},{16,24},{32,40},{40,48},{48,56},{64,72},{72,80},{80,8... | collective-permute-start | bytes 1572872 | tf_op jit(solution)/shard_map/ppermute | solution.py:27
  36.7 14.2 %collective-permute-done.3.y3_ref.refs_9_ = bf16[256,1024]{1,0:T(8,128)(2,1)S(1)} collective-permute-done((bf16[256,1024]{1,0:T(8,128)(2,1)}, bf16[256,1024]{1,0:T(8,128)(2,1)S(1)}, u32[]{:S(2)}, u32[]{:S(2)}) %collective-permute-start.3) | collective-permute-done | bytes 524320 | tf_op jit(solution)/shard_map/ppermute | solution.py:27
  54.3 18.1 %collective-permute-done.5 = bf16[256,1024]{1,0:T(8,128)(2,1)} collective-permute-done((bf16[256,1024]{1,0:T(8,128)(2,1)S(1)}, bf16[256,1024]{1,0:T(8,128)(2,1)}, u32[]{:S(2)}, u32[]{:S(2)}) %collective-permute-start.5) | collective-permute-done | bytes 524320 | tf_op jit(solution)/shard_map/ppermute | solution.py:27
  73.6 4.6 %cross.1 = (bf16[4,512,256]{2,1,0:T(8,128)(2,1)S(1)}, f32[4,512,256]{2,1,0:T(8,128)S(1)}) custom-call(s32[4]{0:T(128)S(1)} %pad_add_fusion.refs_0_.ids_ref, f32[1024,1024]{1,0:T(8,128)} %x_ref.5, bf16[256,1024]{1,0:T(8,128)(2,1)S(1)} %copy-done, bf16[256,1024]{1,0:T(8,128)(2,1)S(1)} %broadcast_select_fusion.3.y1_ref.refs_7_, ...), custom_call_target="tpu_custom_call" | custom-call | tf_op jit(solution)/shard_map/cross/pallas_call | solution.py:170
  84.5 13.0 %collective-permute-done.16 = bf16[256,1024]{1,0:T(8,128)(2,1)S(1)} collective-permute-done((bf16[256,1024]{1,0:T(8,128)(2,1)S(1)}, bf16[256,1024]{1,0:T(8,128)(2,1)S(1)}, u32[]{:S(2)}, u32[]{:S(2)}) %collective-permute-start.16) | collective-permute-done | bytes 524320 | tf_op jit(solution)/shard_map/ppermute | solution.py:27
  97.5 2.9 %collective-permute-done.15 = bf16[256,1024]{1,0:T(8,128)(2,1)S(1)} collective-permute-done((bf16[256,1024]{1,0:T(8,128)(2,1)S(1)}, bf16[256,1024]{1,0:T(8,128)(2,1)S(1)}, u32[]{:S(2)}, u32[]{:S(2)}) %collective-permute-start.15) | collective-permute-done | bytes 524320 | tf_op jit(solution)/shard_map/ppermute | solution.py:27
  100.6 2.5 %link.1 = (bf16[1,768,256]{2,1,0:T(8,128)(2,1)S(1)}, f32[1,768,256]{2,1,0:T(8,128)S(1)}) custom-call(s32[4]{0:T(128)S(1)} %pad_add_fusion.refs_0_.ids_ref, s32[1,4]{1,0:T(1,128)S(1)} %copy-done.4, bf16[256,1024]{1,0:T(8,128)(2,1)S(1)} %weigh.1.refs_2_.refs_4_.w0_ref, bf16[256,1024]{1,0:T(8,128)(2,1)S(1)} %get-tuple-element.52.refs_3_.refs_5_.w1_ref, ...), custom_call_target="tpu_custom_call" | custom-call | tf_op jit(solution)/shard_map/link/pallas_call | solution.py:226
  105.9 6.0 %collective-permute-start.18 = (bf16[1,384,256]{2,1,0:T(8,128)(2,1)S(1)}, bf16[1,384,256]{2,1,0:T(8,128)(2,1)S(1)}, u32[]{:S(2)}, u32[]{:S(2)}) collective-permute-start(bf16[1,384,256]{2,1,0:T(8,128)(2,1)S(1)} %get-tuple-element.46), channel_id=1, source_target_pairs={{0,2},{1,3},{2,0},{3,1},{4,6},{5,7},{6,4},{7,5},{8,10},{9,11},{10,... | collective-permute-start | bytes 589832 | tf_op jit(solution)/shard_map/ppermute | solution.py:23
  111.9 5.1 %collective-permute-done.18.refs_2_ = bf16[1,384,256]{2,1,0:T(8,128)(2,1)S(1)} collective-permute-done((bf16[1,384,256]{2,1,0:T(8,128)(2,1)S(1)}, bf16[1,384,256]{2,1,0:T(8,128)(2,1)S(1)}, u32[]{:S(2)}, u32[]{:S(2)}) %collective-permute-start.18) | collective-permute-done | bytes 196640 | tf_op jit(solution)/shard_map/ppermute | solution.py:23
  120.4 3.6 %collective-permute-start.19 = (bf16[1,192,256]{2,1,0:T(8,128)(2,1)S(1)}, bf16[1,192,256]{2,1,0:T(8,128)(2,1)S(1)}, u32[]{:S(2)}, u32[]{:S(2)}) collective-permute-start(bf16[1,192,256]{2,1,0:T(8,128)(2,1)S(1)} %get-tuple-element.49), channel_id=1, source_target_pairs={{0,4},{1,5},{2,6},{3,7},{4,0},{5,1},{6,2},{7,3},{8,12},{9,13},{10,... | collective-permute-start | bytes 294920 | tf_op jit(solution)/shard_map/ppermute | solution.py:23
  124.0 2.7 %collective-permute-done.19 = bf16[1,192,256]{2,1,0:T(8,128)(2,1)S(1)} collective-permute-done((bf16[1,192,256]{2,1,0:T(8,128)(2,1)S(1)}, bf16[1,192,256]{2,1,0:T(8,128)(2,1)S(1)}, u32[]{:S(2)}, u32[]{:S(2)}) %collective-permute-start.19) | collective-permute-done | bytes 98336 | tf_op jit(solution)/shard_map/ppermute | solution.py:23
  128.9 2.3 %collective-permute-done.20 = bf16[1,192,256]{2,1,0:T(8,128)(2,1)S(1)} collective-permute-done((bf16[1,192,256]{2,1,0:T(8,128)(2,1)S(1)}, bf16[1,192,256]{2,1,0:T(8,128)(2,1)S(1)}, u32[]{:S(2)}, u32[]{:S(2)}) %collective-permute-start.20) | collective-permute-done | bytes 98336 | tf_op jit(solution)/shard_map/ppermute | solution.py:23
  131.3 4.6 %collective-permute-start.21 = (bf16[2,1,192,256]{3,2,1,0:T(8,128)(2,1)S(1)}, bf16[2,1,192,256]{3,2,1,0:T(8,128)(2,1)S(1)}, u32[]{:S(2)}, u32[]{:S(2)}) collective-permute-start(bf16[2,1,192,256]{3,2,1,0:T(8,128)(2,1)S(1)} %pad_maximum_fusion.2), channel_id=1, source_target_pairs={{0,2},{1,3},{2,0},{3,1},{4,6},{5,7},{6,4},{7,5},{8,10},{9,11},{10,... | collective-permute-start | bytes 589832 | tf_op jit(solution)/shard_map/ppermute | solution.py:23
  135.9 3.1 %collective-permute-done.21 = bf16[2,1,192,256]{3,2,1,0:T(8,128)(2,1)S(1)} collective-permute-done((bf16[2,1,192,256]{3,2,1,0:T(8,128)(2,1)S(1)}, bf16[2,1,192,256]{3,2,1,0:T(8,128)(2,1)S(1)}, u32[]{:S(2)}, u32[]{:S(2)}) %collective-permute-start.21) | collective-permute-done | bytes 196640 | tf_op jit(solution)/shard_map/ppermute | solution.py:23
  139.0 4.5 %collective-permute-start.22 = (bf16[4,1,192,256]{3,2,1,0:T(8,128)(2,1)S(1)}, bf16[4,1,192,256]{3,2,1,0:T(8,128)(2,1)S(1)}, u32[]{:S(2)}, u32[]{:S(2)}) collective-permute-start(bf16[4,1,192,256]{3,2,1,0:T(8,128)(2,1)S(1)} %pad_maximum_fusion.1.refs_4_), channel_id=1, source_target_pairs={{0,1},{1,0},{2,3},{3,2},{4,5},{5,4},{6,7},{7,6},{8,9},{9,8},{10,11... | collective-permute-start | bytes 1179656 | tf_op jit(solution)/shard_map/ppermute | solution.py:23
  148.8 10.4 %collective-permute-done.25.refs_2_ = bf16[4,128,256]{2,1,0:T(8,128)(2,1)S(1)} collective-permute-done((bf16[4,128,256]{2,1,0:T(8,128)(2,1)S(1)}, bf16[4,128,256]{2,1,0:T(8,128)(2,1)S(1)}, u32[]{:S(2)}, u32[]{:S(2)}) %collective-permute-start.25) | collective-permute-done | bytes 262176 | tf_op jit(solution)/shard_map/ppermute | solution.py:23
  159.4 3.1 %collective-permute-start.26 = (bf16[3,4,128,256]{3,2,1,0:T(8,128)(2,1)S(1)}, bf16[3,4,128,256]{3,2,1,0:T(8,128)(2,1)S(1)}, u32[]{:S(2)}, u32[]{:S(2)}) collective-permute-start(bf16[3,4,128,256]{3,2,1,0:T(8,128)(2,1)S(1)} %pad_maximum_fusion), channel_id=1, source_target_pairs={{0,1},{1,0},{2,3},{3,2},{4,5},{5,4},{6,7},{7,6},{8,9},{9,8},{10,11... | collective-permute-start | bytes 2359304 | tf_op jit(solution)/shard_map/ppermute | solution.py:23
  164.4 5.9 %update_most.1._ = f32[1024,1024]{1,0:T(8,128)} custom-call(s32[4]{0:T(128)S(1)} %pad_add_fusion.refs_0_.ids_ref, f32[1024,1024]{1,0:T(8,128)} %x_ref.5, bf16[4,128,256]{2,1,0:T(8,128)(2,1)S(1)} %solve.1.refs_0_, bf16[4,128,256]{2,1,0:T(8,128)(2,1)S(1)} %collective-permute-done.23.refs_1_, bf16[4,128,256]{2,1,0:T(8,128)(2,1)S(1)} %collective-permute-done.25.refs_2_, ...), custom_call_target="tpu_custom_call" | custom-call | tf_op jit(solution)/shard_map/update_most/pallas_call | solution.py:290
  172.4 3.4 %update_rest.1 = f32[1024,1024]{1,0:T(8,128)} custom-call(s32[4]{0:T(128)S(1)} %pad_add_fusion.refs_0_.ids_ref, f32[1024,1024]{1,0:T(8,128)} %x_ref.5, bf16[4,128,256]{2,1,0:T(8,128)(2,1)S(1)} %collective-permute-done.24.near_ref, bf16[4,128,256]{2,1,0:T(8,128)(2,1)S(1)} %collective-permute-done.27.far_ref, ...), custom_call_target="tpu_custom_call", output_to_operand_aliasing={{}: (8, {})} | custom-call | tf_op jit(solution)/shard_map/update_rest/pallas_call | solution.py:318
  (76 shorter events, 39.4 us)
Async XLA Ops:
  1.6 4.3 %collective-permute-start = (f32[128,256]{1,0:T(8,128)S(1)}, f32[128,256]{1,0:T(8,128)S(1)}, u32[]{:S(2)}, u32[]{:S(2)}) collective-permute-start(f32[128,256]{1,0:T(8,128)S(1)} %dynamic-slice_bitcast_fusion), channel_id=1, source_target_pairs={{0,1},{1,0},{2,3},{3,2},{4,5},{5,4},{6,7},{7,6},{8,9},{9,8},{10,11... | collective-permute-start | bytes 393224 | tf_op jit(solution)/shard_map/ppermute | solution.py:23
  6.0 4.8 %collective-permute-start.1 = (f32[128,256]{1,0:T(8,128)S(1)}, f32[128,256]{1,0:T(8,128)S(1)}, u32[]{:S(2)}, u32[]{:S(2)}) collective-permute-start(f32[128,256]{1,0:T(8,128)S(1)} %bitcast_add_fusion), channel_id=1, source_target_pairs={{0,2},{1,3},{2,0},{3,1},{4,6},{5,7},{6,4},{7,5},{8,10},{9,11},{10,... | collective-permute-start | bytes 393224 | tf_op jit(solution)/shard_map/ppermute | solution.py:23
  10.8 8.9 %collective-permute-start.2 = (f32[128,256]{1,0:T(8,128)S(1)}, f32[128,256]{1,0:T(8,128)S(1)}, u32[]{:S(2)}, u32[]{:S(2)}) collective-permute-start(f32[128,256]{1,0:T(8,128)S(1)} %add.51), channel_id=1, source_target_pairs={{0,4},{1,5},{2,6},{3,7},{4,0},{5,1},{6,2},{7,3},{8,12},{9,13},{10,... | collective-permute-start | bytes 393224 | tf_op jit(solution)/shard_map/ppermute | solution.py:23
  12.5 16.4 %collective-permute-start.6 = (bf16[256,1024]{1,0:T(8,128)(2,1)}, bf16[256,1024]{1,0:T(8,128)(2,1)}, u32[]{:S(2)}, u32[]{:S(2)}) collective-permute-start(bf16[256,1024]{1,0:T(8,128)(2,1)} %refs_6_.1), channel_id=1, source_target_pairs={{0,8},{8,16},{16,24},{32,40},{40,48},{48,56},{64,72},{72,80},{80,8... | collective-permute-start | bytes 1572872 | tf_op jit(solution)/shard_map/ppermute | solution.py:27
  19.7 31.2 %collective-permute-start.3 = (bf16[256,1024]{1,0:T(8,128)(2,1)}, bf16[256,1024]{1,0:T(8,128)(2,1)S(1)}, u32[]{:S(2)}, u32[]{:S(2)}) collective-permute-start(bf16[256,1024]{1,0:T(8,128)(2,1)} %refs_6_.1), channel_id=1, source_target_pairs={{0,24},{8,32},{16,40},{24,48},{32,56},{40,64},{48,72},{56,80},{64,... | collective-permute-start | bytes 1572872 | tf_op jit(solution)/shard_map/ppermute | solution.py:27
  28.9 24.6 %collective-permute-start.10 = (bf16[256,1024]{1,0:T(8,128)(2,1)S(1)}, bf16[256,1024]{1,0:T(8,128)(2,1)}, u32[]{:S(2)}, u32[]{:S(2)}) collective-permute-start(bf16[256,1024]{1,0:T(8,128)(2,1)S(1)} %weigh.1.refs_2_.refs_4_.w0_ref), channel_id=1, source_target_pairs={{0,8},{8,16},{16,24},{32,40},{40,48},{48,56},{64,72},{72,80},{80,8... | collective-permute-start | bytes 1572872 | tf_op jit(solution)/shard_map/ppermute | solution.py:27
  36.0 17.6 %collective-permute-start.8 = (bf16[256,1024]{1,0:T(8,128)(2,1)}, bf16[256,1024]{1,0:T(8,128)(2,1)S(1)}, u32[]{:S(2)}, u32[]{:S(2)}) collective-permute-start(bf16[256,1024]{1,0:T(8,128)(2,1)} %collective-permute-done.6), channel_id=1, source_target_pairs={{8,16},{16,24},{40,48},{48,56},{72,80},{80,88},{104,112},{112,120}... | collective-permute-start | bytes 1572872 | tf_op jit(solution)/shard_map/ppermute | solution.py:27
  50.9 21.5 %collective-permute-start.5 = (bf16[256,1024]{1,0:T(8,128)(2,1)S(1)}, bf16[256,1024]{1,0:T(8,128)(2,1)}, u32[]{:S(2)}, u32[]{:S(2)}) collective-permute-start(bf16[256,1024]{1,0:T(8,128)(2,1)S(1)} %collective-permute-done.3.y3_ref.refs_9_), channel_id=1, source_target_pairs={{16,0},{48,32},{80,64},{112,96},{144,128},{176,160},{208,192},{240... | collective-permute-start | bytes 1572872 | tf_op jit(solution)/shard_map/ppermute | solution.py:27
  52.2 21.3 %collective-permute-start.7 = (bf16[256,1024]{1,0:T(8,128)(2,1)S(1)}, bf16[256,1024]{1,0:T(8,128)(2,1)S(1)}, u32[]{:S(2)}, u32[]{:S(2)}) collective-permute-start(bf16[256,1024]{1,0:T(8,128)(2,1)S(1)} %collective-permute-done.3.y3_ref.refs_9_), channel_id=1, source_target_pairs={{8,0},{16,8},{40,32},{48,40},{72,64},{80,72},{104,96},{112,104},{1... | collective-permute-start | bytes 1572872 | tf_op jit(solution)/shard_map/ppermute | solution.py:27
  53.5 26.8 %collective-permute-start.9 = (bf16[256,1024]{1,0:T(8,128)(2,1)S(1)}, bf16[256,1024]{1,0:T(8,128)(2,1)S(1)}, u32[]{:S(2)}, u32[]{:S(2)}) collective-permute-start(bf16[256,1024]{1,0:T(8,128)(2,1)S(1)} %weigh.1.refs_2_.refs_4_.w0_ref), channel_id=1, source_target_pairs={{0,24},{8,32},{16,40},{24,48},{32,56},{40,64},{48,72},{56,80},{64,... | collective-permute-start | bytes 1572872 | tf_op jit(solution)/shard_map/ppermute | solution.py:27
  53.6 26.7 %collective-permute-start.11 = (bf16[256,1024]{1,0:T(8,128)(2,1)}, bf16[256,1024]{1,0:T(8,128)(2,1)S(1)}, u32[]{:S(2)}, u32[]{:S(2)}) collective-permute-start(bf16[256,1024]{1,0:T(8,128)(2,1)} %collective-permute-done.10), channel_id=1, source_target_pairs={{8,16},{16,24},{40,48},{48,56},{72,80},{80,88},{104,112},{112,120}... | collective-permute-start | bytes 1572872 | tf_op jit(solution)/shard_map/ppermute | solution.py:27
  80.8 16.7 %collective-permute-start.16 = (bf16[256,1024]{1,0:T(8,128)(2,1)S(1)}, bf16[256,1024]{1,0:T(8,128)(2,1)S(1)}, u32[]{:S(2)}, u32[]{:S(2)}) collective-permute-start(bf16[256,1024]{1,0:T(8,128)(2,1)S(1)} %collective-permute-done.9.refs_5_.refs_7_.w3_ref), channel_id=1, source_target_pairs={{8,0},{16,8},{40,32},{48,40},{72,64},{80,72},{104,96},{112,104},{1... | collective-permute-start | bytes 1572872 | tf_op jit(solution)/shard_map/ppermute | solution.py:27
  82.1 18.3 %collective-permute-start.15 = (bf16[256,1024]{1,0:T(8,128)(2,1)S(1)}, bf16[256,1024]{1,0:T(8,128)(2,1)S(1)}, u32[]{:S(2)}, u32[]{:S(2)}) collective-permute-start(bf16[256,1024]{1,0:T(8,128)(2,1)S(1)} %collective-permute-done.9.refs_5_.refs_7_.w3_ref), channel_id=1, source_target_pairs={{16,0},{48,32},{80,64},{112,96},{144,128},{176,160},{208,192},{240... | collective-permute-start | bytes 1572872 | tf_op jit(solution)/shard_map/ppermute | solution.py:27
  84.2 19.7 %collective-permute-start.13 = (bf16[4,256,256]{2,1,0:T(8,128)(2,1)S(1)}, bf16[4,256,256]{2,1,0:T(8,128)(2,1)S(1)}, u32[]{:S(2)}, u32[]{:S(2)}) collective-permute-start(bf16[4,256,256]{2,1,0:T(8,128)(2,1)S(1)} %get-tuple-element.37), channel_id=1, source_target_pairs={{0,2},{1,3},{2,0},{3,1},{4,6},{5,7},{6,4},{7,5},{8,10},{9,11},{10,... | collective-permute-start | bytes 1572872 | tf_op jit(solution)/shard_map/ppermute | solution.py:23
  104.6 14.5 %collective-permute-start.14 = (bf16[4,128,256]{2,1,0:T(8,128)(2,1)S(1)}, bf16[4,128,256]{2,1,0:T(8,128)(2,1)S(1)}, u32[]{:S(2)}, u32[]{:S(2)}) collective-permute-start(bf16[4,128,256]{2,1,0:T(8,128)(2,1)S(1)} %get-tuple-element.39), channel_id=1, source_target_pairs={{0,4},{1,5},{2,6},{3,7},{4,0},{5,1},{6,2},{7,3},{8,12},{9,13},{10,... | collective-permute-start | bytes 786440 | tf_op jit(solution)/shard_map/ppermute | solution.py:23
  105.9 11.1 %collective-permute-start.18 = (bf16[1,384,256]{2,1,0:T(8,128)(2,1)S(1)}, bf16[1,384,256]{2,1,0:T(8,128)(2,1)S(1)}, u32[]{:S(2)}, u32[]{:S(2)}) collective-permute-start(bf16[1,384,256]{2,1,0:T(8,128)(2,1)S(1)} %get-tuple-element.46), channel_id=1, source_target_pairs={{0,2},{1,3},{2,0},{3,1},{4,6},{5,7},{6,4},{7,5},{8,10},{9,11},{10,... | collective-permute-start | bytes 589832 | tf_op jit(solution)/shard_map/ppermute | solution.py:23
  120.4 6.4 %collective-permute-start.19 = (bf16[1,192,256]{2,1,0:T(8,128)(2,1)S(1)}, bf16[1,192,256]{2,1,0:T(8,128)(2,1)S(1)}, u32[]{:S(2)}, u32[]{:S(2)}) collective-permute-start(bf16[1,192,256]{2,1,0:T(8,128)(2,1)S(1)} %get-tuple-element.49), channel_id=1, source_target_pairs={{0,4},{1,5},{2,6},{3,7},{4,0},{5,1},{6,2},{7,3},{8,12},{9,13},{10,... | collective-permute-start | bytes 294920 | tf_op jit(solution)/shard_map/ppermute | solution.py:23
  126.8 4.5 %collective-permute-start.20 = (bf16[1,192,256]{2,1,0:T(8,128)(2,1)S(1)}, bf16[1,192,256]{2,1,0:T(8,128)(2,1)S(1)}, u32[]{:S(2)}, u32[]{:S(2)}) collective-permute-start(bf16[1,192,256]{2,1,0:T(8,128)(2,1)S(1)} %add_convert_fusion), channel_id=1, source_target_pairs={{0,4},{1,5},{2,6},{3,7},{4,0},{5,1},{6,2},{7,3},{8,12},{9,13},{10,... | collective-permute-start | bytes 294920 | tf_op jit(solution)/shard_map/ppermute | solution.py:23
  131.3 7.7 %collective-permute-start.21 = (bf16[2,1,192,256]{3,2,1,0:T(8,128)(2,1)S(1)}, bf16[2,1,192,256]{3,2,1,0:T(8,128)(2,1)S(1)}, u32[]{:S(2)}, u32[]{:S(2)}) collective-permute-start(bf16[2,1,192,256]{3,2,1,0:T(8,128)(2,1)S(1)} %pad_maximum_fusion.2), channel_id=1, source_target_pairs={{0,2},{1,3},{2,0},{3,1},{4,6},{5,7},{6,4},{7,5},{8,10},{9,11},{10,... | collective-permute-start | bytes 589832 | tf_op jit(solution)/shard_map/ppermute | solution.py:23
  139.0 5.8 %collective-permute-start.22 = (bf16[4,1,192,256]{3,2,1,0:T(8,128)(2,1)S(1)}, bf16[4,1,192,256]{3,2,1,0:T(8,128)(2,1)S(1)}, u32[]{:S(2)}, u32[]{:S(2)}) collective-permute-start(bf16[4,1,192,256]{3,2,1,0:T(8,128)(2,1)S(1)} %pad_maximum_fusion.1.refs_4_), channel_id=1, source_target_pairs={{0,1},{1,0},{2,3},{3,2},{4,5},{5,4},{6,7},{7,6},{8,9},{9,8},{10,11... | collective-permute-start | bytes 1179656 | tf_op jit(solution)/shard_map/ppermute | solution.py:23
  146.8 12.4 %collective-permute-start.25 = (bf16[4,128,256]{2,1,0:T(8,128)(2,1)S(1)}, bf16[4,128,256]{2,1,0:T(8,128)(2,1)S(1)}, u32[]{:S(2)}, u32[]{:S(2)}) collective-permute-start(bf16[4,128,256]{2,1,0:T(8,128)(2,1)S(1)} %solve.1.refs_0_), channel_id=1, source_target_pairs={{0,2},{1,3},{2,0},{3,1},{4,6},{5,7},{6,4},{7,5},{8,10},{9,11},{10,... | collective-permute-start | bytes 786440 | tf_op jit(solution)/shard_map/ppermute | solution.py:23
  146.9 12.3 %collective-permute-start.23 = (bf16[4,128,256]{2,1,0:T(8,128)(2,1)S(1)}, bf16[4,128,256]{2,1,0:T(8,128)(2,1)S(1)}, u32[]{:S(2)}, u32[]{:S(2)}) collective-permute-start(bf16[4,128,256]{2,1,0:T(8,128)(2,1)S(1)} %solve.1.refs_0_), channel_id=1, source_target_pairs={{0,4},{1,5},{2,6},{3,7},{4,0},{5,1},{6,2},{7,3},{8,12},{9,13},{10,... | collective-permute-start | bytes 786440 | tf_op jit(solution)/shard_map/ppermute | solution.py:23
  159.4 5.0 %collective-permute-start.26 = (bf16[3,4,128,256]{3,2,1,0:T(8,128)(2,1)S(1)}, bf16[3,4,128,256]{3,2,1,0:T(8,128)(2,1)S(1)}, u32[]{:S(2)}, u32[]{:S(2)}) collective-permute-start(bf16[3,4,128,256]{3,2,1,0:T(8,128)(2,1)S(1)} %pad_maximum_fusion), channel_id=1, source_target_pairs={{0,1},{1,0},{2,3},{3,2},{4,5},{5,4},{6,7},{7,6},{8,9},{9,8},{10,11... | collective-permute-start | bytes 2359304 | tf_op jit(solution)/shard_map/ppermute | solution.py:23
  162.5 7.9 %collective-permute-start.24 = (bf16[4,128,256]{2,1,0:T(8,128)(2,1)S(1)}, bf16[4,128,256]{2,1,0:T(8,128)(2,1)S(1)}, u32[]{:S(2)}, u32[]{:S(2)}) collective-permute-start(bf16[4,128,256]{2,1,0:T(8,128)(2,1)S(1)} %collective-permute-done.23.refs_1_), channel_id=1, source_target_pairs={{0,2},{1,3},{2,0},{3,1},{4,6},{5,7},{6,4},{7,5},{8,10},{9,11},{10,... | collective-permute-start | bytes 786440 | tf_op jit(solution)/shard_map/ppermute | solution.py:23
  (12 other events, 233.0 us)

commit v5 on v4

--- a/solution.py
+++ b/solution.py
@@ -368,9 +368,9 @@
 
     link_give, link_keep = link_halves(ids, order, w, y, pairs)
     link_give, link_keep = halve(1, ids, link_keep, after(mem_swap(link_give, 1), give))
-    link_recv = after(mem_swap(link_give, 2), cross_recv)
-    link_give, link_keep = halve(2, ids, link_keep, link_recv)
-    link = (link_keep + mem_swap(link_give, 4).astype(F32)).astype(BF)
+    link_give, link_keep = halve(2, ids, link_keep, mem_swap(link_give, 2))
+    link_recv = after(mem_swap(link_give, 4), cross_recv)
+    link = (link_keep + link_recv.astype(F32)).astype(BF)
     link_near, link_far = spread_up(link)
 
     onehot = (distance[0][..., None] == jnp.arange(taper.shape[0], dtype=jnp.int32)).astype(F32)

time: 176 us -> 176 us (level)
  waiting for transfers between devices: 90.5 us -> 101 us
  starting transfers between devices: 54.5 us -> 44.9 us
    ppermute x18, waiting for transfers between devices: 40.2 us -> 50.5 us  [mem_swap(): return lax.ppermute(value, 'mem', [(m, m ^ bit) for m in range(count)])]
    ppermute x18, starting transfers between devices: 35.5 us -> 25.8 us  [mem_swap(): return lax.ppermute(value, 'mem', [(m, m ^ bit) for m in range(count)])]
where the time goes in v5:
time: 176 us
  waiting for transfers between devices  101 us (57%)
  starting transfers between devices  44.9 us (26%)
  Pallas kernels  23.7 us (13%)
  local copies, waits for them, and re-layouts  2.38 us (1%)
  other arithmetic  1.93 us (1%)
    ppermute x18, waiting for transfers between devices, mem_swap(): return lax.ppermute(value, 'mem', [(m, m ^ bit) for m in range(count)])  50.5 us
    ppermute x10, waiting for transfers between devices, band_send(): return lax.ppermute(value, 'band', pairs)  50.3 us
    ppermute x18, starting transfers between devices, mem_swap(): return lax.ppermute(value, 'mem', [(m, m ^ bit) for m in range(count)])  25.8 us
    ppermute x10, starting transfers between devices, band_send(): return lax.ppermute(value, 'band', pairs)  19.1 us
    pallas_call x1, Pallas kernels, update_most(): pl.pallas_call(most_kernel, out_shape=shape((cells, width), F32), grid=(w...  5.86 us
    pallas_call x1, Pallas kernels, cross_halves(): pl.pallas_call(cross_kernel, out_shape=[shape((4, rows, num_obs), BF), sh...  4.57 us
    pallas_call x1, Pallas kernels, weigh(): pl.pallas_call(lambda *refs: weigh_kernel(scale, *refs), out_shape=shape(...  3.83 us
  transfers between devices with their start and end apart: 28, of which 20 were waited for; matrix products, arithmetic and copies ran while one was open for 1% of the time, Pallas kernels for 11%

profile of v5, /device:TPU:1, one launch (start us, length us, event | category | flops | bytes accessed | tf_op | source)
XLA Modules:
  0.0 175.7 jit_solution(3610097584648355681)
XLA Ops:
  1.6 3.3 %collective-permute-start = (f32[128,256]{1,0:T(8,128)S(1)}, f32[128,256]{1,0:T(8,128)S(1)}, u32[]{:S(2)}, u32[]{:S(2)}) collective-permute-start(f32[128,256]{1,0:T(8,128)S(1)} %dynamic-slice_bitcast_fusion), channel_id=1, source_target_pairs={{0,1},{1,0},{2,3},{3,2},{4,5},{5,4},{6,7},{7,6},{8,9},{9,8},{10,11... | collective-permute-start | bytes 393224 | tf_op jit(solution)/shard_map/ppermute | solution.py:23
  6.1 4.7 %collective-permute-done.1 = f32[128,256]{1,0:T(8,128)S(1)} collective-permute-done((f32[128,256]{1,0:T(8,128)S(1)}, f32[128,256]{1,0:T(8,128)S(1)}, u32[]{:S(2)}, u32[]{:S(2)}) %collective-permute-start.1) | collective-permute-done | bytes 131104 | tf_op jit(solution)/shard_map/ppermute | solution.py:23
  12.5 4.0 %collective-permute-start.6 = (bf16[256,1024]{1,0:T(8,128)(2,1)}, bf16[256,1024]{1,0:T(8,128)(2,1)}, u32[]{:S(2)}, u32[]{:S(2)}) collective-permute-start(bf16[256,1024]{1,0:T(8,128)(2,1)} %refs_6_.1), channel_id=1, source_target_pairs={{0,8},{8,16},{16,24},{32,40},{40,48},{48,56},{64,72},{72,80},{80,8... | collective-permute-start | bytes 1572872 | tf_op jit(solution)/shard_map/ppermute | solution.py:27
  16.5 3.2 %collective-permute-done.2 = f32[128,256]{1,0:T(8,128)S(1)} collective-permute-done((f32[128,256]{1,0:T(8,128)S(1)}, f32[128,256]{1,0:T(8,128)S(1)}, u32[]{:S(2)}, u32[]{:S(2)}) %collective-permute-start.2) | collective-permute-done | bytes 131104 | tf_op jit(solution)/shard_map/ppermute | solution.py:23
  25.1 3.8 %weigh.1.refs_2_.refs_4_.w0_ref = bf16[256,1024]{1,0:T(8,128)(2,1)S(1)} custom-call(s32[4]{0:T(128)S(1)} %pad_add_fusion.refs_0_.ids_ref, f32[128,256]{1,0:T(8,128)S(1)} %add.52.refs_1_, f32[128,256]{1,0:T(8,128)S(1)} %collective-permute-done.4.refs_2_, f32[256,1024]{1,0:T(8,128)S(1)} %copy-done.1), custom_call_target="tpu_custom_call" | custom-call | tf_op jit(solution)/shard_map/weigh/pallas_call | solution.py:145
  28.9 7.1 %collective-permute-start.10 = (bf16[256,1024]{1,0:T(8,128)(2,1)S(1)}, bf16[256,1024]{1,0:T(8,128)(2,1)}, u32[]{:S(2)}, u32[]{:S(2)}) collective-permute-start(bf16[256,1024]{1,0:T(8,128)(2,1)S(1)} %weigh.1.refs_2_.refs_4_.w0_ref), channel_id=1, source_target_pairs={{0,8},{8,16},{16,24},{32,40},{40,48},{48,56},{64,72},{72,80},{80,8... | collective-permute-start | bytes 1572872 | tf_op jit(solution)/shard_map/ppermute | solution.py:27
  36.7 14.2 %collective-permute-done.3.y3_ref.refs_9_ = bf16[256,1024]{1,0:T(8,128)(2,1)S(1)} collective-permute-done((bf16[256,1024]{1,0:T(8,128)(2,1)}, bf16[256,1024]{1,0:T(8,128)(2,1)S(1)}, u32[]{:S(2)}, u32[]{:S(2)}) %collective-permute-start.3) | collective-permute-done | bytes 524320 | tf_op jit(solution)/shard_map/ppermute | solution.py:27
  54.3 18.1 %collective-permute-done.5 = bf16[256,1024]{1,0:T(8,128)(2,1)} collective-permute-done((bf16[256,1024]{1,0:T(8,128)(2,1)S(1)}, bf16[256,1024]{1,0:T(8,128)(2,1)}, u32[]{:S(2)}, u32[]{:S(2)}) %collective-permute-start.5) | collective-permute-done | bytes 524320 | tf_op jit(solution)/shard_map/ppermute | solution.py:27
  73.6 4.6 %cross.1 = (bf16[4,512,256]{2,1,0:T(8,128)(2,1)S(1)}, f32[4,512,256]{2,1,0:T(8,128)S(1)}) custom-call(s32[4]{0:T(128)S(1)} %pad_add_fusion.refs_0_.ids_ref, f32[1024,1024]{1,0:T(8,128)} %x_ref.5, bf16[256,1024]{1,0:T(8,128)(2,1)S(1)} %copy-done, bf16[256,1024]{1,0:T(8,128)(2,1)S(1)} %broadcast_select_fusion.3.y1_ref.refs_7_, ...), custom_call_target="tpu_custom_call" | custom-call | tf_op jit(solution)/shard_map/cross/pallas_call | solution.py:170
  78.1 2.1 %collective-permute-done.9.refs_5_.refs_7_.w3_ref = bf16[256,1024]{1,0:T(8,128)(2,1)S(1)} collective-permute-done((bf16[256,1024]{1,0:T(8,128)(2,1)S(1)}, bf16[256,1024]{1,0:T(8,128)(2,1)S(1)}, u32[]{:S(2)}, u32[]{:S(2)}) %collective-permute-start.9) | collective-permute-done | bytes 524320 | tf_op jit(solution)/shard_map/ppermute | solution.py:27
  84.5 13.0 %collective-permute-done.16 = bf16[256,1024]{1,0:T(8,128)(2,1)S(1)} collective-permute-done((bf16[256,1024]{1,0:T(8,128)(2,1)S(1)}, bf16[256,1024]{1,0:T(8,128)(2,1)S(1)}, u32[]{:S(2)}, u32[]{:S(2)}) %collective-permute-start.16) | collective-permute-done | bytes 524320 | tf_op jit(solution)/shard_map/ppermute | solution.py:27
  97.5 2.9 %collective-permute-done.15 = bf16[256,1024]{1,0:T(8,128)(2,1)S(1)} collective-permute-done((bf16[256,1024]{1,0:T(8,128)(2,1)S(1)}, bf16[256,1024]{1,0:T(8,128)(2,1)S(1)}, u32[]{:S(2)}, u32[]{:S(2)}) %collective-permute-start.15) | collective-permute-done | bytes 524320 | tf_op jit(solution)/shard_map/ppermute | solution.py:27
  100.6 2.5 %link.1 = (bf16[1,768,256]{2,1,0:T(8,128)(2,1)S(1)}, f32[1,768,256]{2,1,0:T(8,128)S(1)}) custom-call(s32[4]{0:T(128)S(1)} %pad_add_fusion.refs_0_.ids_ref, s32[1,4]{1,0:T(1,128)S(1)} %copy-done.4, bf16[256,1024]{1,0:T(8,128)(2,1)S(1)} %weigh.1.refs_2_.refs_4_.w0_ref, bf16[256,1024]{1,0:T(8,128)(2,1)S(1)} %get-tuple-element.52.refs_3_.refs_5_.w1_ref, ...), custom_call_target="tpu_custom_call" | custom-call | tf_op jit(solution)/shard_map/link/pallas_call | solution.py:226
  106.0 6.5 %collective-permute-start.14 = (bf16[4,128,256]{2,1,0:T(8,128)(2,1)S(1)}, bf16[4,128,256]{2,1,0:T(8,128)(2,1)S(1)}, u32[]{:S(2)}, u32[]{:S(2)}) collective-permute-start(bf16[4,128,256]{2,1,0:T(8,128)(2,1)S(1)} %get-tuple-element.39), channel_id=1, source_target_pairs={{0,4},{1,5},{2,6},{3,7},{4,0},{5,1},{6,2},{7,3},{8,12},{9,13},{10,... | collective-permute-start | bytes 786440 | tf_op jit(solution)/shard_map/ppermute | solution.py:23
  113.1 5.1 %collective-permute-start.19 = (bf16[1,192,256]{2,1,0:T(8,128)(2,1)S(1)}, bf16[1,192,256]{2,1,0:T(8,128)(2,1)S(1)}, u32[]{:S(2)}, u32[]{:S(2)}) collective-permute-start(bf16[1,192,256]{2,1,0:T(8,128)(2,1)S(1)} %get-tuple-element.48), channel_id=1, source_target_pairs={{0,4},{1,5},{2,6},{3,7},{4,0},{5,1},{6,2},{7,3},{8,12},{9,13},{10,... | collective-permute-start | bytes 294920 | tf_op jit(solution)/shard_map/ppermute | solution.py:23
  118.2 8.1 %collective-permute-done.14.refs_3_ = bf16[4,128,256]{2,1,0:T(8,128)(2,1)S(1)} collective-permute-done((bf16[4,128,256]{2,1,0:T(8,128)(2,1)S(1)}, bf16[4,128,256]{2,1,0:T(8,128)(2,1)S(1)}, u32[]{:S(2)}, u32[]{:S(2)}) %collective-permute-start.14) | collective-permute-done | bytes 262176 | tf_op jit(solution)/shard_map/ppermute | solution.py:23
  126.3 2.1 %collective-permute-done.19 = bf16[1,192,256]{2,1,0:T(8,128)(2,1)S(1)} collective-permute-done((bf16[1,192,256]{2,1,0:T(8,128)(2,1)S(1)}, bf16[1,192,256]{2,1,0:T(8,128)(2,1)S(1)}, u32[]{:S(2)}, u32[]{:S(2)}) %collective-permute-start.19) | collective-permute-done | bytes 98336 | tf_op jit(solution)/shard_map/ppermute | solution.py:23
  128.5 7.3 %collective-permute-done.20 = bf16[1,192,256]{2,1,0:T(8,128)(2,1)S(1)} collective-permute-done((bf16[1,192,256]{2,1,0:T(8,128)(2,1)S(1)}, bf16[1,192,256]{2,1,0:T(8,128)(2,1)S(1)}, u32[]{:S(2)}, u32[]{:S(2)}) %collective-permute-start.20) | collective-permute-done | bytes 98336 | tf_op jit(solution)/shard_map/ppermute | solution.py:23
  136.0 5.7 %collective-permute-done.21 = bf16[2,1,192,256]{3,2,1,0:T(8,128)(2,1)S(1)} collective-permute-done((bf16[2,1,192,256]{3,2,1,0:T(8,128)(2,1)S(1)}, bf16[2,1,192,256]{3,2,1,0:T(8,128)(2,1)S(1)}, u32[]{:S(2)}, u32[]{:S(2)}) %collective-permute-start.21) | collective-permute-done | bytes 196640 | tf_op jit(solution)/shard_map/ppermute | solution.py:23
  148.1 10.4 %collective-permute-done.25.refs_2_ = bf16[4,128,256]{2,1,0:T(8,128)(2,1)S(1)} collective-permute-done((bf16[4,128,256]{2,1,0:T(8,128)(2,1)S(1)}, bf16[4,128,256]{2,1,0:T(8,128)(2,1)S(1)}, u32[]{:S(2)}, u32[]{:S(2)}) %collective-permute-start.25) | collective-permute-done | bytes 262176 | tf_op jit(solution)/shard_map/ppermute | solution.py:23
  158.5 2.3 %collective-permute-done.23.refs_1_ = bf16[4,128,256]{2,1,0:T(8,128)(2,1)S(1)} collective-permute-done((bf16[4,128,256]{2,1,0:T(8,128)(2,1)S(1)}, bf16[4,128,256]{2,1,0:T(8,128)(2,1)S(1)}, u32[]{:S(2)}, u32[]{:S(2)}) %collective-permute-start.23) | collective-permute-done | bytes 262176 | tf_op jit(solution)/shard_map/ppermute | solution.py:23
  162.4 1.9 %collective-permute-done.26.refs_3_ = bf16[3,4,128,256]{3,2,1,0:T(8,128)(2,1)S(1)} collective-permute-done((bf16[3,4,128,256]{3,2,1,0:T(8,128)(2,1)S(1)}, bf16[3,4,128,256]{3,2,1,0:T(8,128)(2,1)S(1)}, u32[]{:S(2)}, u32[]{:S(2)}) %collective-permute-start.26) | collective-permute-done | bytes 786464 | tf_op jit(solution)/shard_map/ppermute | solution.py:23
  164.3 5.9 %update_most.1._ = f32[1024,1024]{1,0:T(8,128)} custom-call(s32[4]{0:T(128)S(1)} %pad_add_fusion.refs_0_.ids_ref, f32[1024,1024]{1,0:T(8,128)} %x_ref.5, bf16[4,128,256]{2,1,0:T(8,128)(2,1)S(1)} %solve.1.refs_0_, bf16[4,128,256]{2,1,0:T(8,128)(2,1)S(1)} %collective-permute-done.23.refs_1_, bf16[4,128,256]{2,1,0:T(8,128)(2,1)S(1)} %collective-permute-done.25.refs_2_, ...), custom_call_target="tpu_custom_call" | custom-call | tf_op jit(solution)/shard_map/update_most/pallas_call | solution.py:290
  172.3 3.4 %update_rest.1 = f32[1024,1024]{1,0:T(8,128)} custom-call(s32[4]{0:T(128)S(1)} %pad_add_fusion.refs_0_.ids_ref, f32[1024,1024]{1,0:T(8,128)} %x_ref.5, bf16[4,128,256]{2,1,0:T(8,128)(2,1)S(1)} %collective-permute-done.24.near_ref, bf16[4,128,256]{2,1,0:T(8,128)(2,1)S(1)} %collective-permute-done.27.far_ref, ...), custom_call_target="tpu_custom_call", output_to_operand_aliasing={{}: (8, {})} | custom-call | tf_op jit(solution)/shard_map/update_rest/pallas_call | solution.py:318
  (76 shorter events, 33.1 us)
Async XLA Ops:
  1.6 4.3 %collective-permute-start = (f32[128,256]{1,0:T(8,128)S(1)}, f32[128,256]{1,0:T(8,128)S(1)}, u32[]{:S(2)}, u32[]{:S(2)}) collective-permute-start(f32[128,256]{1,0:T(8,128)S(1)} %dynamic-slice_bitcast_fusion), channel_id=1, source_target_pairs={{0,1},{1,0},{2,3},{3,2},{4,5},{5,4},{6,7},{7,6},{8,9},{9,8},{10,11... | collective-permute-start | bytes 393224 | tf_op jit(solution)/shard_map/ppermute | solution.py:23
  6.0 4.8 %collective-permute-start.1 = (f32[128,256]{1,0:T(8,128)S(1)}, f32[128,256]{1,0:T(8,128)S(1)}, u32[]{:S(2)}, u32[]{:S(2)}) collective-permute-start(f32[128,256]{1,0:T(8,128)S(1)} %bitcast_add_fusion), channel_id=1, source_target_pairs={{0,2},{1,3},{2,0},{3,1},{4,6},{5,7},{6,4},{7,5},{8,10},{9,11},{10,... | collective-permute-start | bytes 393224 | tf_op jit(solution)/shard_map/ppermute | solution.py:23
  10.8 8.9 %collective-permute-start.2 = (f32[128,256]{1,0:T(8,128)S(1)}, f32[128,256]{1,0:T(8,128)S(1)}, u32[]{:S(2)}, u32[]{:S(2)}) collective-permute-start(f32[128,256]{1,0:T(8,128)S(1)} %add.51), channel_id=1, source_target_pairs={{0,4},{1,5},{2,6},{3,7},{4,0},{5,1},{6,2},{7,3},{8,12},{9,13},{10,... | collective-permute-start | bytes 393224 | tf_op jit(solution)/shard_map/ppermute | solution.py:23
  12.5 16.4 %collective-permute-start.6 = (bf16[256,1024]{1,0:T(8,128)(2,1)}, bf16[256,1024]{1,0:T(8,128)(2,1)}, u32[]{:S(2)}, u32[]{:S(2)}) collective-permute-start(bf16[256,1024]{1,0:T(8,128)(2,1)} %refs_6_.1), channel_id=1, source_target_pairs={{0,8},{8,16},{16,24},{32,40},{40,48},{48,56},{64,72},{72,80},{80,8... | collective-permute-start | bytes 1572872 | tf_op jit(solution)/shard_map/ppermute | solution.py:27
  19.7 31.2 %collective-permute-start.3 = (bf16[256,1024]{1,0:T(8,128)(2,1)}, bf16[256,1024]{1,0:T(8,128)(2,1)S(1)}, u32[]{:S(2)}, u32[]{:S(2)}) collective-permute-start(bf16[256,1024]{1,0:T(8,128)(2,1)} %refs_6_.1), channel_id=1, source_target_pairs={{0,24},{8,32},{16,40},{24,48},{32,56},{40,64},{48,72},{56,80},{64,... | collective-permute-start | bytes 1572872 | tf_op jit(solution)/shard_map/ppermute | solution.py:27
  28.9 24.6 %collective-permute-start.10 = (bf16[256,1024]{1,0:T(8,128)(2,1)S(1)}, bf16[256,1024]{1,0:T(8,128)(2,1)}, u32[]{:S(2)}, u32[]{:S(2)}) collective-permute-start(bf16[256,1024]{1,0:T(8,128)(2,1)S(1)} %weigh.1.refs_2_.refs_4_.w0_ref), channel_id=1, source_target_pairs={{0,8},{8,16},{16,24},{32,40},{40,48},{48,56},{64,72},{72,80},{80,8... | collective-permute-start | bytes 1572872 | tf_op jit(solution)/shard_map/ppermute | solution.py:27
  36.0 17.6 %collective-permute-start.8 = (bf16[256,1024]{1,0:T(8,128)(2,1)}, bf16[256,1024]{1,0:T(8,128)(2,1)S(1)}, u32[]{:S(2)}, u32[]{:S(2)}) collective-permute-start(bf16[256,1024]{1,0:T(8,128)(2,1)} %collective-permute-done.6), channel_id=1, source_target_pairs={{8,16},{16,24},{40,48},{48,56},{72,80},{80,88},{104,112},{112,120}... | collective-permute-start | bytes 1572872 | tf_op jit(solution)/shard_map/ppermute | solution.py:27
  50.9 21.5 %collective-permute-start.5 = (bf16[256,1024]{1,0:T(8,128)(2,1)S(1)}, bf16[256,1024]{1,0:T(8,128)(2,1)}, u32[]{:S(2)}, u32[]{:S(2)}) collective-permute-start(bf16[256,1024]{1,0:T(8,128)(2,1)S(1)} %collective-permute-done.3.y3_ref.refs_9_), channel_id=1, source_target_pairs={{16,0},{48,32},{80,64},{112,96},{144,128},{176,160},{208,192},{240... | collective-permute-start | bytes 1572872 | tf_op jit(solution)/shard_map/ppermute | solution.py:27
  52.2 21.3 %collective-permute-start.7 = (bf16[256,1024]{1,0:T(8,128)(2,1)S(1)}, bf16[256,1024]{1,0:T(8,128)(2,1)S(1)}, u32[]{:S(2)}, u32[]{:S(2)}) collective-permute-start(bf16[256,1024]{1,0:T(8,128)(2,1)S(1)} %collective-permute-done.3.y3_ref.refs_9_), channel_id=1, source_target_pairs={{8,0},{16,8},{40,32},{48,40},{72,64},{80,72},{104,96},{112,104},{1... | collective-permute-start | bytes 1572872 | tf_op jit(solution)/shard_map/ppermute | solution.py:27
  53.5 26.8 %collective-permute-start.9 = (bf16[256,1024]{1,0:T(8,128)(2,1)S(1)}, bf16[256,1024]{1,0:T(8,128)(2,1)S(1)}, u32[]{:S(2)}, u32[]{:S(2)}) collective-permute-start(bf16[256,1024]{1,0:T(8,128)(2,1)S(1)} %weigh.1.refs_2_.refs_4_.w0_ref), channel_id=1, source_target_pairs={{0,24},{8,32},{16,40},{24,48},{32,56},{40,64},{48,72},{56,80},{64,... | collective-permute-start | bytes 1572872 | tf_op jit(solution)/shard_map/ppermute | solution.py:27
  53.6 26.7 %collective-permute-start.11 = (bf16[256,1024]{1,0:T(8,128)(2,1)}, bf16[256,1024]{1,0:T(8,128)(2,1)S(1)}, u32[]{:S(2)}, u32[]{:S(2)}) collective-permute-start(bf16[256,1024]{1,0:T(8,128)(2,1)} %collective-permute-done.10), channel_id=1, source_target_pairs={{8,16},{16,24},{40,48},{48,56},{72,80},{80,88},{104,112},{112,120}... | collective-permute-start | bytes 1572872 | tf_op jit(solution)/shard_map/ppermute | solution.py:27
  80.3 3.1 %collective-permute-start.12 = (bf16[4,512,256]{2,1,0:T(8,128)(2,1)S(1)}, bf16[4,512,256]{2,1,0:T(8,128)(2,1)S(1)}, u32[]{:S(2)}, u32[]{:S(2)}) collective-permute-start(bf16[4,512,256]{2,1,0:T(8,128)(2,1)S(1)} %get-tuple-element.35), channel_id=1, source_target_pairs={{0,1},{1,0},{2,3},{3,2},{4,5},{5,4},{6,7},{7,6},{8,9},{9,8},{10,11... | collective-permute-start | bytes 3145736 | tf_op jit(solution)/shard_map/ppermute | solution.py:23
  80.8 16.7 %collective-permute-start.16 = (bf16[256,1024]{1,0:T(8,128)(2,1)S(1)}, bf16[256,1024]{1,0:T(8,128)(2,1)S(1)}, u32[]{:S(2)}, u32[]{:S(2)}) collective-permute-start(bf16[256,1024]{1,0:T(8,128)(2,1)S(1)} %collective-permute-done.9.refs_5_.refs_7_.w3_ref), channel_id=1, source_target_pairs={{8,0},{16,8},{40,32},{48,40},{72,64},{80,72},{104,96},{112,104},{1... | collective-permute-start | bytes 1572872 | tf_op jit(solution)/shard_map/ppermute | solution.py:27
  82.1 18.3 %collective-permute-start.15 = (bf16[256,1024]{1,0:T(8,128)(2,1)S(1)}, bf16[256,1024]{1,0:T(8,128)(2,1)S(1)}, u32[]{:S(2)}, u32[]{:S(2)}) collective-permute-start(bf16[256,1024]{1,0:T(8,128)(2,1)S(1)} %collective-permute-done.9.refs_5_.refs_7_.w3_ref), channel_id=1, source_target_pairs={{16,0},{48,32},{80,64},{112,96},{144,128},{176,160},{208,192},{240... | collective-permute-start | bytes 1572872 | tf_op jit(solution)/shard_map/ppermute | solution.py:27
  84.2 19.7 %collective-permute-start.13 = (bf16[4,256,256]{2,1,0:T(8,128)(2,1)S(1)}, bf16[4,256,256]{2,1,0:T(8,128)(2,1)S(1)}, u32[]{:S(2)}, u32[]{:S(2)}) collective-permute-start(bf16[4,256,256]{2,1,0:T(8,128)(2,1)S(1)} %get-tuple-element.37), channel_id=1, source_target_pairs={{0,2},{1,3},{2,0},{3,1},{4,6},{5,7},{6,4},{7,5},{8,10},{9,11},{10,... | collective-permute-start | bytes 1572872 | tf_op jit(solution)/shard_map/ppermute | solution.py:23
  105.9 6.6 %collective-permute-start.18 = (bf16[1,384,256]{2,1,0:T(8,128)(2,1)S(1)}, bf16[1,384,256]{2,1,0:T(8,128)(2,1)S(1)}, u32[]{:S(2)}, u32[]{:S(2)}) collective-permute-start(bf16[1,384,256]{2,1,0:T(8,128)(2,1)S(1)} %get-tuple-element.46), channel_id=1, source_target_pairs={{0,2},{1,3},{2,0},{3,1},{4,6},{5,7},{6,4},{7,5},{8,10},{9,11},{10,... | collective-permute-start | bytes 589832 | tf_op jit(solution)/shard_map/ppermute | solution.py:23
  106.0 20.3 %collective-permute-start.14 = (bf16[4,128,256]{2,1,0:T(8,128)(2,1)S(1)}, bf16[4,128,256]{2,1,0:T(8,128)(2,1)S(1)}, u32[]{:S(2)}, u32[]{:S(2)}) collective-permute-start(bf16[4,128,256]{2,1,0:T(8,128)(2,1)S(1)} %get-tuple-element.39), channel_id=1, source_target_pairs={{0,4},{1,5},{2,6},{3,7},{4,0},{5,1},{6,2},{7,3},{8,12},{9,13},{10,... | collective-permute-start | bytes 786440 | tf_op jit(solution)/shard_map/ppermute | solution.py:23
  113.1 15.3 %collective-permute-start.19 = (bf16[1,192,256]{2,1,0:T(8,128)(2,1)S(1)}, bf16[1,192,256]{2,1,0:T(8,128)(2,1)S(1)}, u32[]{:S(2)}, u32[]{:S(2)}) collective-permute-start(bf16[1,192,256]{2,1,0:T(8,128)(2,1)S(1)} %get-tuple-element.48), channel_id=1, source_target_pairs={{0,4},{1,5},{2,6},{3,7},{4,0},{5,1},{6,2},{7,3},{8,12},{9,13},{10,... | collective-permute-start | bytes 294920 | tf_op jit(solution)/shard_map/ppermute | solution.py:23
  128.4 7.4 %collective-permute-start.20 = (bf16[1,192,256]{2,1,0:T(8,128)(2,1)S(1)}, bf16[1,192,256]{2,1,0:T(8,128)(2,1)S(1)}, u32[]{:S(2)}, u32[]{:S(2)}) collective-permute-start(bf16[1,192,256]{2,1,0:T(8,128)(2,1)S(1)} %add_convert_fusion), channel_id=1, source_target_pairs={{0,4},{1,5},{2,6},{3,7},{4,0},{5,1},{6,2},{7,3},{8,12},{9,13},{10,... | collective-permute-start | bytes 294920 | tf_op jit(solution)/shard_map/ppermute | solution.py:23
  135.9 5.8 %collective-permute-start.21 = (bf16[2,1,192,256]{3,2,1,0:T(8,128)(2,1)S(1)}, bf16[2,1,192,256]{3,2,1,0:T(8,128)(2,1)S(1)}, u32[]{:S(2)}, u32[]{:S(2)}) collective-permute-start(bf16[2,1,192,256]{3,2,1,0:T(8,128)(2,1)S(1)} %pad_maximum_fusion.2), channel_id=1, source_target_pairs={{0,2},{1,3},{2,0},{3,1},{4,6},{5,7},{6,4},{7,5},{8,10},{9,11},{10,... | collective-permute-start | bytes 589832 | tf_op jit(solution)/shard_map/ppermute | solution.py:23
  146.8 11.8 %collective-permute-start.25 = (bf16[4,128,256]{2,1,0:T(8,128)(2,1)S(1)}, bf16[4,128,256]{2,1,0:T(8,128)(2,1)S(1)}, u32[]{:S(2)}, u32[]{:S(2)}) collective-permute-start(bf16[4,128,256]{2,1,0:T(8,128)(2,1)S(1)} %solve.1.refs_0_), channel_id=1, source_target_pairs={{0,2},{1,3},{2,0},{3,1},{4,6},{5,7},{6,4},{7,5},{8,10},{9,11},{10,... | collective-permute-start | bytes 786440 | tf_op jit(solution)/shard_map/ppermute | solution.py:23
  146.9 14.0 %collective-permute-start.23 = (bf16[4,128,256]{2,1,0:T(8,128)(2,1)S(1)}, bf16[4,128,256]{2,1,0:T(8,128)(2,1)S(1)}, u32[]{:S(2)}, u32[]{:S(2)}) collective-permute-start(bf16[4,128,256]{2,1,0:T(8,128)(2,1)S(1)} %solve.1.refs_0_), channel_id=1, source_target_pairs={{0,4},{1,5},{2,6},{3,7},{4,0},{5,1},{6,2},{7,3},{8,12},{9,13},{10,... | collective-permute-start | bytes 786440 | tf_op jit(solution)/shard_map/ppermute | solution.py:23
  161.0 3.4 %collective-permute-start.26 = (bf16[3,4,128,256]{3,2,1,0:T(8,128)(2,1)S(1)}, bf16[3,4,128,256]{3,2,1,0:T(8,128)(2,1)S(1)}, u32[]{:S(2)}, u32[]{:S(2)}) collective-permute-start(bf16[3,4,128,256]{3,2,1,0:T(8,128)(2,1)S(1)} %pad_maximum_fusion), channel_id=1, source_target_pairs={{0,1},{1,0},{2,3},{3,2},{4,5},{5,4},{6,7},{7,6},{8,9},{9,8},{10,11... | collective-permute-start | bytes 2359304 | tf_op jit(solution)/shard_map/ppermute | solution.py:23
  162.4 7.9 %collective-permute-start.24 = (bf16[4,128,256]{2,1,0:T(8,128)(2,1)S(1)}, bf16[4,128,256]{2,1,0:T(8,128)(2,1)S(1)}, u32[]{:S(2)}, u32[]{:S(2)}) collective-permute-start(bf16[4,128,256]{2,1,0:T(8,128)(2,1)S(1)} %collective-permute-done.23.refs_1_), channel_id=1, source_target_pairs={{0,2},{1,3},{2,0},{3,1},{4,6},{5,7},{6,4},{7,5},{8,10},{9,11},{10,... | collective-permute-start | bytes 786440 | tf_op jit(solution)/shard_map/ppermute | solution.py:23
  (12 other events, 247.4 us)
